TPU v7x, 32 devices: a whole 2x2x4 slice. The times are simulated.
32 devices in a mesh: members: 2 (over y), tiles: 4 (over z), chan: 2 (over x), dirs: 2 (over core).
Axes of the slice: x: 2, y: 2, z: 4, core: 2. Of those that a mesh axis runs over, the one named last changes fastest.
Arguments:
- field: float32 [64, 128, 256], P(('members', 'tiles'), 'chan'), parts along dimension 0, may hold values from -6 to 6
- tangents: float32 [4, 64, 128, 256], P('dirs', ('members', 'tiles'), 'chan'), parts along dimension 1, may hold values from -6 to 6
- weight_one: float32 [9, 128, 128], replicated, may hold values from -0.1875 to 0.1875
- bias_one: float32 [128], replicated, may hold values from -3 to 3
- weight_two: float32 [9, 128, 128], replicated, may hold values from -0.1875 to 0.1875
- bias_two: float32 [128], replicated, may hold values from -3 to 3
- adjacency: int32 [32, 4], replicated, may hold values from 0 to 31
- side_code: int32 [32, 4], replicated, may hold values from 0 to 3
- mirror_flag: int32 [32, 4], replicated, may hold values from 0 to 1
- placement: int32 [32], replicated, may hold values from 0 to 31, each once
Outputs:
- output: float32 [64, 128, 256], P(('members', 'tiles'), 'chan'), parts along dimension 0
- output_tangents: float32 [4, 64, 128, 256], P('dirs', ('members', 'tiles'), 'chan'), parts along dimension 1
There are 2 independent parts, one for each index of `members`. A program takes and returns all parts, laid end to end along the dimension named above; an argument that names none is the same for every part. Nothing has to cross between parts.
Inputs may be any that keep to these rules, and one draw needn't show every extreme that they name: `adjacency`: tile ids; a tile may border itself or the same tile on several sides. `placement`: every tile id once.
All inputs are finite; a program needn't handle non-finite values.
Results may differ from a plain program's by a relative error of at most 0.00011.
Values sent between devices are 32-bit elements; how exact they have to be, the bound alone decides.
No kernel may reach another device: no remote copies, remote signals or barrier semaphores. Data moves between devices by JAX's collectives and lax.ppermute only.
A program may use at most 128 MiB of HBM per device.

v0:
```python
import jax
import jax.numpy as jnp
import numpy as np
from jax import lax
from jax.sharding import PartitionSpec as P

S = 16


def static_tables():
    width = S + 2
    length = width * width + 2
    where_at = np.arange(length)
    row_at = where_at // width
    col_at = where_at % width
    inside = where_at < width * width
    mid_row = (row_at >= 1) & (row_at <= S)
    mid_col = (col_at >= 1) & (col_at <= S)
    side_at = np.full(length, 4)
    along = np.zeros(length, dtype=np.int64)
    side_at = np.where(inside & (row_at == 0) & mid_col, 0, side_at)
    side_at = np.where(inside & (row_at == S + 1) & mid_col, 1, side_at)
    side_at = np.where(inside & (col_at == 0) & mid_row, 2, side_at)
    side_at = np.where(inside & (col_at == S + 1) & mid_row, 3, side_at)
    side_at = np.where(inside & mid_row & mid_col, -1, side_at)
    along = np.where((side_at == 0) | (side_at == 1), col_at - 1, along)
    along = np.where((side_at == 2) | (side_at == 3), row_at - 1, along)
    along = np.where(side_at == -1, (row_at - 1) * S + (col_at - 1), along)
    return (side_at.astype(np.int32), along.astype(np.int32))


def pad_index(flips):
    side_np, along_np = static_tables()
    side_at = jnp.asarray(side_np)
    along = jnp.asarray(along_np)
    side_safe = jnp.clip(side_at, 0, 3)
    flip_at = jnp.take(flips, side_safe, axis=1)
    rim_index = (
        S * S
        + side_safe[None, :] * S
        + jnp.where(flip_at == 1, S - 1 - along[None, :], along[None, :])
    )
    zero_index = S * S + 4 * S
    index = jnp.where(
        side_at[None, :] == -1,
        along[None, :],
        jnp.where(side_at[None, :] == 4, zero_index, rim_index),
    )
    return index.astype(jnp.int32)


def convolve(padded, weight):
    tap_count = weight.shape[0]
    out_count = weight.shape[1]
    width = S + 2
    span = S * width
    flat_weight = weight.reshape(tap_count * out_count, weight.shape[2])
    planes = jnp.einsum("kc,btcl->btkl", flat_weight, padded, precision=lax.Precision.HIGHEST)
    planes = planes.reshape(padded.shape[0], padded.shape[1], tap_count, out_count, padded.shape[3])
    summed = None
    for row_off in range(3):
        for col_off in range(3):
            offset = row_off * width + col_off
            term = planes[:, :, row_off * 3 + col_off, :, offset : offset + span]
            summed = term if summed is None else summed + term
    keep_np = (np.arange(S)[:, None] * width + np.arange(S)[None, :]).reshape(-1).astype(np.int32)
    return jnp.take(summed, jnp.asarray(keep_np), axis=-1)


def pad_fields(fields, near_slot, codes, index):
    stream_count = fields.shape[0]
    tile_count = fields.shape[1]
    chan_count = fields.shape[2]
    grid_view = fields.reshape(stream_count, tile_count, chan_count, S, S)
    edges = jnp.stack(
        [
            grid_view[..., 0, :],
            grid_view[..., S - 1, :],
            grid_view[..., :, 0],
            grid_view[..., :, S - 1],
        ],
        axis=2,
    )
    everyone = lax.all_gather(
        edges.reshape(stream_count, tile_count, 4 * chan_count * S), "tiles", axis=1, tiled=True
    )
    flat_edges = everyone.reshape(stream_count, everyone.shape[1] * 4, chan_count * S)
    lookup = (near_slot * 4 + codes).reshape(-1)
    rims = jnp.take(flat_edges, lookup, axis=1).reshape(stream_count, tile_count, 4, chan_count, S)
    rims = jnp.transpose(rims, (0, 1, 3, 2, 4)).reshape(stream_count, tile_count, chan_count, 4 * S)
    zeros_col = jnp.zeros((stream_count, tile_count, chan_count, 1), jnp.float32)
    source = jnp.concatenate([fields, rims, zeros_col], axis=-1)
    return jnp.take_along_axis(source, index[None, :, None, :], axis=-1)


def layer_sums(padded, weight):
    chan_group = padded.shape[2]
    chan_start = lax.axis_index("chan") * chan_group
    weight_rows = lax.dynamic_slice_in_dim(weight, chan_start, chan_group, 1)
    gathered = lax.all_gather(padded, "chan", axis=2, tiled=True)
    return convolve(gathered, weight_rows)


def local(
    field,
    tangents,
    weight_one,
    bias_one,
    weight_two,
    bias_two,
    adjacency,
    side_code,
    mirror_flag,
    placement,
):
    tile_count = field.shape[0]
    chan_group = field.shape[1]
    total_tiles = placement.shape[0]
    ident = jnp.arange(total_tiles, dtype=jnp.int32)
    slot_of = jnp.sum(jnp.where(placement[None, :] == ident[:, None], ident[None, :], 0), axis=1)
    mine = lax.dynamic_slice_in_dim(placement, lax.axis_index("tiles") * tile_count, tile_count)
    near_slot = jnp.take(slot_of, jnp.take(adjacency, mine, axis=0).reshape(-1), axis=0).reshape(
        tile_count, 4
    )
    codes = jnp.take(side_code, mine, axis=0)
    flips = jnp.take(mirror_flag, mine, axis=0)
    index = pad_index(flips)
    chan_start = lax.axis_index("chan") * chan_group
    streams = jnp.concatenate([field[None], tangents], axis=0)
    weights = (weight_one, weight_two)
    biases = (
        lax.dynamic_slice_in_dim(bias_one, chan_start, chan_group),
        lax.dynamic_slice_in_dim(bias_two, chan_start, chan_group),
    )
    result = None
    for layer in range(2):
        summed = layer_sums(pad_fields(streams, near_slot, codes, index), weights[layer])
        pre = summed[0] + biases[layer][:, None]
        if layer == 0:
            sigma = jax.nn.sigmoid(pre)
            slope = sigma * (1.0 + pre * (1.0 - sigma))
            streams = jnp.concatenate([(pre * sigma)[None], summed[1:] * slope[None]], axis=0)
        else:
            result = (pre, summed[1:])
    return result


def solution(mesh):
    placed = (
        P(("members", "tiles"), "chan", None),
        P("dirs", ("members", "tiles"), "chan", None),
        P(),
        P(),
        P(),
        P(),
        P(),
        P(),
        P(),
        P(),
    )
    return jax.shard_map(
        local,
        mesh=mesh,
        in_specs=placed,
        out_specs=(
            P(("members", "tiles"), "chan", None),
            P("dirs", ("members", "tiles"), "chan", None),
        ),
        check_vma=False,
    )
```

profile of v0, /device:TPU:0, one launch (start us, length us, event | category | flops | bytes accessed | tf_op | source)
XLA Modules:
  0.0 596.3 jit_solution(17269689504091182904)
XLA Ops:
  28.4 30.6 %all-gather.5.cloned.1.call-done = f32[3,32,4096]{2,1,0:T(8,128)} async-done(((f32[3,8,4096]{2,1,0:T(8,128)}), f32[3,32,4096]{2,1,0:T(8,128)}) %all-gather.5.cloned.1.call-update) | async-done | bytes 1572880 | tf_op jit(solution)/shard_map/all_gather | solution.py:84
  71.6 6.8 %maximum_maximum_fusion = f32[3,8,64,321]{2,0,3,1:T(4,128)} fusion(f32[3,8,64,64]{2,0,3,1:T(4,128)S(1)} %copy.267, f32[3,8,64,256]{2,0,3,1:T(4,128)} %copy.266, f32[321]{0:T(512)S(1)} %pad.10.clone), kind=kLoop, calls=%fused_computation.13 | loop fusion | flops 986112 | bytes 3939588 | tf_op jit(solution)/shard_map/concatenate | solution.py:92
  78.4 29.1 %gather_fusion.6 = f32[2608,3,64]{2,1,0:T(4,128)} fusion(f32[3,8,64,321]{2,0,3,1:T(4,128)} %maximum_maximum_fusion, s32[2608]{0:T(1024)S(1)} %reshape.450), kind=kCustom, calls=%fused_computation.2.clone | custom fusion | bytes 4026752 | tf_op jit(solution)/shard_map/jit(take_along_axis)/gather | solution.py:93
  107.5 5.1 copy.269
  114.5 61.5 %all-gather.7.cloned.1.call-done = f32[3,8,128,326]{3,2,1,0:T(8,128)} async-done(((f32[3,8,64,326]{3,2,1,0:T(8,128)}), f32[3,8,128,326]{3,2,1,0:T(8,128)}) %all-gather.7.cloned.1.call-update) | async-done | bytes 4005904 | tf_op jit(solution)/shard_map/all_gather | solution.py:100
  176.0 26.3 %convolution_bitcast_fusion.1 = f32[3,8,576,326]{2,3,1,0:T(8,128)} fusion(f32[3,8,128,326]{3,2,1,0:T(8,128)} %all-gather.7.cloned.1.call-done, f32[576,128,1,1]{1,0,3,2:T(8,128)S(1)} %bitcast.119), kind=kOutput, calls=%fused_computation.12 | convolution fusion | flops 6922174464 | bytes 22327296 | tf_op jit(solution)/shard_map/kc,btcl->btkl/dot_general | solution.py:58
  202.3 22.3 %copy.270 = f32[3,8,576,326]{3,2,1,0:T(8,128)} copy(f32[3,8,576,326]{2,3,1,0:T(8,128)} %convolution_bitcast_fusion.1) | data formatting | bytes 36052992 | tf_op jit(solution)/shard_map/kc,btcl->btkl/transpose | solution.py:58
  224.6 13.3 %fusion.4 = (f32[3,8,1,64,288]{4,3,2,1,0:T(8,128)}, f32[3,8,1,64,288]{4,3,2,1,0:T(8,128)}, f32[3,8,1,64,288]{4,3,2,1,0:T(8,128)}, f32[3,8,1,64,288]{4,3,2,1,0:T(...) fusion(f32[3,8,9,64,326]{4,3,2,1,0:T(8,128)} %bitcast.99), kind=kLoop, calls=%fused_computation.64 | loop fusion | bytes 31850496 | tf_op jit(solution)/shard_map/slice | solution.py:64
  237.9 4.7 copy.313
  256.6 4.7 copy.317
  266.0 4.7 copy.319
  278.7 12.7 %add_bitcast_fusion.1 = f32[3,8,64,288]{2,1,3,0:T(8,128)} fusion(f32[3,8,1,64,288]{3,1,4,0,2:T(8,128)} %copy.321, f32[3,8,1,64,288]{3,1,4,0,2:T(8,128)} %copy.320, f32[3,8,1,64,288]{3,1,4,0,2:T(8,128)} %copy.319, f32[3,8,1,64,288]{3,1,4,0,2:T(8,128)} %copy.318, f32[3,8,1,64,288]{3,1,4,0,2:T(8,128)} %copy.317, f32[3,8,1,64,288]{3,1,4,0,2:T(8,128)} %copy.316, ...), kind=kLoop, calls=%fused_computation.16 | loop fusion | flops 3538944 | bytes 17694720 | tf_op jit(solution)/shard_map/add | solution.py:65
  307.5 37.1 %all-gather.9.cloned.1.call-done = f32[3,32,4096]{2,1,0:T(8,128)} async-done(((f32[3,8,4096]{2,1,0:T(8,128)}), f32[3,32,4096]{2,1,0:T(8,128)}) %all-gather.9.cloned.1.call-update) | async-done | bytes 1572880 | tf_op jit(solution)/shard_map/all_gather | solution.py:84
  365.7 29.3 %gather_fusion.9 = f32[2608,3,64]{2,1,0:T(4,128)} fusion(f32[3,8,64,321]{2,0,3,1:T(4,128)} %copy.290, s32[2608]{0:T(1024)S(1)} %reshape.450), kind=kCustom, calls=%fused_computation.7.clone | custom fusion | bytes 4026752 | tf_op jit(solution)/shard_map/jit(take_along_axis)/gather | solution.py:93
  395.1 4.9 copy.292
  401.8 61.5 %all-gather.11.cloned.1.call-done = f32[3,8,128,326]{3,2,1,0:T(8,128)} async-done(((f32[3,8,64,326]{3,2,1,0:T(8,128)}), f32[3,8,128,326]{3,2,1,0:T(8,128)}) %all-gather.11.cloned.1.call-update) | async-done | bytes 4005904 | tf_op jit(solution)/shard_map/all_gather | solution.py:100
  463.3 26.3 %convolution_bitcast_fusion = f32[3,8,576,326]{2,3,1,0:T(8,128)} fusion(f32[3,8,128,326]{3,2,1,0:T(8,128)} %all-gather.11.cloned.1.call-done, f32[576,128,1,1]{1,0,3,2:T(8,128)S(1)} %bitcast.118), kind=kOutput, calls=%fused_computation.11 | convolution fusion | flops 6922174464 | bytes 22327296 | tf_op jit(solution)/shard_map/kc,btcl->btkl/dot_general | solution.py:58
  489.6 22.3 %copy.293 = f32[3,8,576,326]{3,2,1,0:T(8,128)} copy(f32[3,8,576,326]{2,3,1,0:T(8,128)} %convolution_bitcast_fusion) | data formatting | bytes 36052992 | tf_op jit(solution)/shard_map/kc,btcl->btkl/transpose | solution.py:58
  511.9 13.3 %fusion.3 = (f32[3,8,1,64,288]{4,3,2,1,0:T(8,128)}, f32[3,8,1,64,288]{4,3,2,1,0:T(8,128)}, f32[3,8,1,64,288]{4,3,2,1,0:T(8,128)}, f32[3,8,1,64,288]{4,3,2,1,0:T(...) fusion(f32[3,8,9,64,326]{4,3,2,1,0:T(8,128)} %bitcast.100), kind=kLoop, calls=%fused_computation.63 | loop fusion | bytes 31850496 | tf_op jit(solution)/shard_map/slice | solution.py:64
  525.1 4.7 copy.322
  543.9 4.7 copy.326
  553.3 4.7 copy.328
  558.0 4.9 copy.329
  566.0 12.7 %add_bitcast_fusion = f32[3,8,64,288]{2,1,3,0:T(8,128)} fusion(f32[3,8,1,64,288]{3,1,4,0,2:T(8,128)} %copy.330, f32[3,8,1,64,288]{3,1,4,0,2:T(8,128)} %copy.329, f32[3,8,1,64,288]{3,1,4,0,2:T(8,128)} %copy.328, f32[3,8,1,64,288]{3,1,4,0,2:T(8,128)} %copy.327, f32[3,8,1,64,288]{3,1,4,0,2:T(8,128)} %copy.326, f32[3,8,1,64,288]{3,1,4,0,2:T(8,128)} %copy.325, ...), kind=kLoop, calls=%fused_computation.15 | loop fusion | flops 3538944 | bytes 17694720 | tf_op jit(solution)/shard_map/add | solution.py:65
  (138 shorter events, 133.5 us)
Async XLA Ops:
  7.2 107.3 %copy-start = (f32[9,128,128]{2,1,0:T(8,128)S(1)}, f32[9,128,128]{2,1,0:T(8,128)}, u32[]{:S(2)}) copy-start(f32[9,128,128]{2,1,0:T(8,128)} %param.24) | copy-start | bytes 1769476
  7.2 2.0 copy-start.6
  7.2 51.8 %all-gather.5.cloned.1.call-start = ((), (), s32[]{:S(2)}) async-start(), calls=%async_computation | async-start | bytes 1966080 | tf_op jit(solution)/shard_map/all_gather | solution.py:84
  10.5 1.6 copy-start.2
  12.2 6.9 %copy-start.13 = (s32[32,4]{0,1:T(4,128)S(1)}, s32[32,4]{0,1:T(4,128)}, u32[]{:S(2)}) copy-start(s32[32,4]{0,1:T(4,128)} %param.28) | copy-start | bytes 1540
  12.3 7.0 %copy-start.14 = (s32[32,4]{0,1:T(4,128)S(1)}, s32[32,4]{0,1:T(4,128)}, u32[]{:S(2)}) copy-start(s32[32,4]{0,1:T(4,128)} %param.30) | copy-start | bytes 1540
  12.3 7.0 %copy-start.18 = (s32[32]{0:T(128)S(1)}, s32[32]{0:T(128)}, u32[]{:S(2)}) copy-start(s32[32]{0:T(128)} %param.31) | copy-start | bytes 388
  12.3 8.4 %copy-start.17 = (s32[256]{0:T(256)S(1)}, s32[256]{0:T(256)}, u32[]{:S(2)}) copy-start(s32[256]{0:T(256)} %constant.181) | copy-start | bytes 3076
  14.5 7.1 %copy-start.15 = (s32[32,4]{0,1:T(4,128)S(1)}, s32[32,4]{0,1:T(4,128)}, u32[]{:S(2)}) copy-start(s32[32,4]{0,1:T(4,128)} %param.29) | copy-start | bytes 1540
  14.5 7.9 %copy-start.5 = (f32[2,8,64,256]{3,2,1,0:T(8,128)S(1)}, f32[2,8,64,256]{3,2,1,0:T(8,128)}, u32[]{:S(2)}) copy-start(f32[2,8,64,256]{3,2,1,0:T(8,128)} %param.23) | copy-start | bytes 3145732
  19.1 156.9 %all-gather.7.cloned.1.call-start = ((), (), s32[]{:S(2)}) async-start(), calls=%async_computation.1 | async-start | bytes 7077888 | tf_op jit(solution)/shard_map/all_gather | solution.py:100
  23.6 3.3 copy-start.16
  23.6 4.4 copy-start.8
  23.6 4.4 copy-start.9
  23.6 4.4 copy-start.10
  23.7 4.4 copy-start.11
  23.7 4.4 copy-start.12
  112.7 1.7 copy-start.19
  114.4 230.2 %all-gather.9.cloned.1.call-start = ((), (), s32[]{:S(2)}) async-start(), calls=%async_computation.2 | async-start | bytes 1966080 | tf_op jit(solution)/shard_map/all_gather | solution.py:84
  296.0 2.2 copy-start.4
  307.4 155.9 %all-gather.11.cloned.1.call-start = ((), (), s32[]{:S(2)}) async-start(), calls=%async_computation.3 | async-start | bytes 7077888 | tf_op jit(solution)/shard_map/all_gather | solution.py:100
  400.0 1.7 copy-start.20
  400.0 1.8 copy-start.7
  583.3 6.3 %copy-start.1 = (f32[9,128,128]{2,1,0:T(8,128)S(1)}, f32[9,128,128]{2,1,0:T(8,128)}, u32[]{:S(2)}) copy-start(f32[9,128,128]{2,1,0:T(8,128)} %param.24) | copy-start | bytes 1769476
  (1 other events, 1.3 us)
Sparse Core Ops, SparseCore 0:
  19.2 39.7 all-gather.4
  114.5 61.4 all-gather.6
  307.5 37.0 all-gather.8
  401.8 61.4 all-gather.10
where the time goes:
time: 607 us; the launch traced here: 596 us
  local copies, waits for them, and re-layouts  293 us (48%)
  waiting for transfers between devices  191 us (31%)
  matrix products  52.6 us (9%)
  other arithmetic  45.5 us (7%)
  between operations  14.5 us (2%)
    all_gather x2, waiting for transfers between devices, layer_sums(): gathered = lax.all_gather(padded, 'chan', axis=2, tiled=True)  123 us
    unnamed x68, local copies, waits for them, and re-layouts  89.5 us
    gather x5, local copies, waits for them, and re-layouts, pad_fields(): return jnp.take_along_axis(source, index[None, :, None, :], axis=-1)  68.6 us
    all_gather x2, waiting for transfers between devices, pad_fields(): lax.all_gather(edges.reshape(stream_count, tile_count, 4 * chan_count * S...  67.7 us
    dot_general x2, matrix products, convolve(): jnp.einsum('kc,btcl->btkl', flat_weight, padded, precision=lax.Precision....  52.6 us
    transpose x2, local copies, waits for them, and re-layouts, convolve(): jnp.einsum('kc,btcl->btkl', flat_weight, padded, precision=lax.Precision....  44.5 us
    slice x2, local copies, waits for them, and re-layouts, convolve(): term = planes[:, :, row_off * 3 + col_off, :, offset:offset + span]  26.5 us
    add x2, other arithmetic, convolve(): summed = term if summed is None else summed + term  25.5 us
  transfers between devices with their start and end apart: 4, of which 4 were waited for; matrix products, arithmetic and copies ran while one was open for 2% of the time, Pallas kernels for 0%

commit v1 on v0

--- a/solution.py
+++ b/solution.py
@@ -1,10 +1,672 @@
+import functools
+
 import jax
 import jax.numpy as jnp
 import numpy as np
 from jax import lax
+from jax.experimental import pallas as pl
+from jax.experimental.pallas import tpu as pltpu
 from jax.sharding import PartitionSpec as P
 
 S = 16
+CELLS = S * S
+F32 = jnp.float32
+BF16 = jnp.bfloat16
+VMEM = pltpu.VMEM
+SMEM = pltpu.SMEM
+
+
+LIMIT = pltpu.CompilerParams(vmem_limit_bytes=16 << 20)
+
+
+def vmem_spec():
+    return pl.BlockSpec(memory_space=VMEM)
+
+
+def smem_spec():
+    return pl.BlockSpec(memory_space=SMEM)
+
+
+def cost(flops, moved):
+    return pl.CostEstimate(flops=int(flops), bytes_accessed=int(moved), transcendentals=0)
+
+
+def f32_of(*shape):
+    return jax.ShapeDtypeStruct(shape, F32)
+
+
+def high_low(x):
+    high = x.astype(BF16)
+    return high, (x - high.astype(F32)).astype(BF16)
+
+
+def beside(x):
+    return jnp.concatenate(high_low(x), axis=1)
+
+
+def below(x):
+    return jnp.concatenate(high_low(x), axis=0)
+
+
+def dot_rows(a, b):
+    return lax.dot_general(a, b, (((1,), (1,)), ((), ())), preferred_element_type=F32)
+
+
+def lane_half(shape):
+    return lax.broadcasted_iota(jnp.int32, shape, 1) < shape[1] // 2
+
+
+def swap(x):
+    return pltpu.roll(x, x.shape[1] // 2, 1)
+
+
+def edge_cells(rows):
+    row = lax.broadcasted_iota(jnp.int32, (rows, CELLS), 0)
+    cell = lax.broadcasted_iota(jnp.int32, (rows, CELLS), 1)
+    along = row % S
+    along = jnp.where(row >= 4 * S, S - 1 - along, along)
+    side = (row // S) % 4
+    want = jnp.where(
+        side == 0,
+        along,
+        jnp.where(side == 1, CELLS - S + along, jnp.where(side == 2, along * S, along * S + S - 1)),
+    )
+    return jnp.where(cell == want, 1.0, 0.0).astype(BF16)
+
+
+def flip8(v):
+    row = lax.broadcasted_iota(jnp.int32, v.shape, 0)
+    v = pltpu.roll(v, 4, 0)
+    v = jnp.where((row & 2) != 0, pltpu.roll(v, 2, 0), pltpu.roll(v, 6, 0))
+    return jnp.where((row & 1) != 0, pltpu.roll(v, 1, 0), pltpu.roll(v, 7, 0))
+
+
+def flip16(v):
+    return jnp.concatenate([flip8(v[8:16]), flip8(v[0:8])], axis=0)
+
+
+def shifts(x):
+    rows = x.shape[0]
+    along = lax.broadcasted_iota(jnp.int32, x.shape, 0) % S
+    before = jnp.where(along == 0, 0.0, pltpu.roll(x, 1, 0))
+    after = jnp.where(along == S - 1, 0.0, pltpu.roll(x, rows - 1, 0))
+    return before, x, after
+
+
+def edge_rows(side):
+    return (slice(0, S), slice(CELLS - S, CELLS), pl.ds(0, S, stride=S), pl.ds(S - 1, S, stride=S))[side]
+
+
+def any_spec():
+    return pl.BlockSpec(memory_space=pl.ANY)
+
+
+def started(pairs, sems):
+    copies = [pltpu.make_async_copy(a, b, sems.at[k]) for k, (a, b) in enumerate(pairs)]
+    for c in copies:
+        c.start()
+    return copies
+
+
+def finished(copies):
+    for c in copies:
+        c.wait()
+
+
+def weights_kernel(w1, w2, b1, b2, o1, o2, c1, c2):
+    x = lax.axis_index("chan")
+    chans = w1.shape[1]
+    half = chans // 2
+    for b, c in ((b1, c1), (b2, c2)):
+        c[...] = jnp.where(x == 1, swap(b[...]), b[...])
+    for w, o in ((w1, o1), (w2, o2)):
+        for tap in range(w.shape[0]):
+            own = w[tap, pl.ds(pl.multiple_of(x * half, half), half), :]
+            oth = w[tap, pl.ds(pl.multiple_of((1 - x) * half, half), half), :]
+            v = beside(jnp.concatenate([own, oth], axis=0).T)
+            o[pl.ds(pl.multiple_of(tap * chans + x * half, half), half), :] = v[:half]
+            o[pl.ds(pl.multiple_of(tap * chans + (1 - x) * half, half), half), :] = v[half:]
+
+
+def prepare_weights(w1, b1, w2, b2):
+    taps, chans, _ = w1.shape
+    wide = jax.ShapeDtypeStruct((taps * chans, 2 * chans), BF16)
+    return pl.pallas_call(
+        weights_kernel,
+        out_shape=(wide, wide, f32_of(1, chans), f32_of(1, chans)),
+        in_specs=[vmem_spec()] * 4,
+        out_specs=[vmem_spec()] * 4,
+        compiler_params=LIMIT,
+        cost_estimate=cost(0, 4 << 20),
+    )(w1, w2, b1.reshape(1, chans), b2.reshape(1, chans))
+
+
+def inputs_kernel(t, f, edges, send_t, send_f, where, sems):
+    x = lax.axis_index("chan")
+    d = lax.axis_index("dirs")
+    where[0] = x
+    where[1] = d
+    tiles = f.shape[0]
+    group = tiles // 2
+    copies = started([(f.at[pl.ds(d * group, group)], send_f), (t.at[1 - x], send_t)], sems)
+    pick = edge_cells(4 * S)
+    pairs = [(t, (x, k), (1 - x, k)) for k in range(tiles)] + [(f, (k,), (k + group,)) for k in range(group)]
+    for k, (r, a, b) in enumerate(pairs):
+        e = dot_rows(pick, below(jnp.concatenate([r[a], r[b]], axis=0)))
+        half = e.shape[1] // 2
+        edges[k * 4 * S : (k + 1) * 4 * S, :] = e[:, :half] + e[:, half:]
+    finished(copies)
+
+
+def read_inputs(t, f):
+    tiles, half, cells = f.shape
+    return pl.pallas_call(
+        inputs_kernel,
+        out_shape=(
+            f32_of((tiles + tiles // 2) * 4 * S, 2 * half),
+            f32_of(tiles, half, cells),
+            f32_of(tiles // 2, half, cells),
+            jax.ShapeDtypeStruct((2,), jnp.int32),
+        ),
+        in_specs=[vmem_spec()] * 2,
+        out_specs=[vmem_spec(), any_spec(), any_spec(), smem_spec()],
+        scratch_shapes=[pltpu.SemaphoreType.DMA((2,))],
+        compiler_params=LIMIT,
+        cost_estimate=cost(0, 3 << 20),
+    )(t, f)
+
+
+def table_kernel(packed, place, table, slot_of):
+    def put(p, _):
+        slot_of[place[p]] = p
+        return 0
+
+    total = place.shape[0]
+    lax.fori_loop(0, total, put, 0, unroll=8)
+
+    def look_up(p, _):
+        t = place[p]
+        for s in range(4):
+            v = packed[t, s]
+            table[p * 4 + s] = slot_of[v >> 3] * 8 + (v & 7)
+        return 0
+
+    lax.fori_loop(0, total, look_up, 0, unroll=4)
+
+
+def index_table(packed, place):
+    total = place.shape[0]
+    return pl.pallas_call(
+        table_kernel,
+        out_shape=jax.ShapeDtypeStruct((total * 4,), jnp.int32),
+        in_specs=[smem_spec()] * 2,
+        out_specs=smem_spec(),
+        scratch_shapes=[SMEM((total,), jnp.int32)],
+        compiler_params=LIMIT,
+        cost_estimate=cost(0, 1 << 20),
+    )(packed, place)
+
+
+def planes_of(count, chans):
+    return VMEM((3, 2, count, CELLS + 2 * S, chans), BF16)
+
+
+def clear_rims(planes):
+    @pl.when(pl.program_id(0) == 0)
+    def _():
+        zero = jnp.zeros(planes.shape[:3] + (S, planes.shape[4]), BF16)
+        planes[:, :, :, 0:S, :] = zero
+        planes[:, :, :, S + CELLS :, :] = zero
+
+
+def four_products(r):
+    rows, chans = r.shape[0] // 2, r.shape[1] // 2
+    return (r[:rows, :chans] + r[:rows, chans:]) + (r[rows:, :chans] + r[rows:, chans:])
+
+
+def conv_tiles(x, w, planes, count):
+    for b, v in enumerate(shifts(x)):
+        for part, u in enumerate(high_low(v)):
+            for t in range(count):
+                planes[b, part, t, S : S + CELLS, :] = u[t * CELLS : (t + 1) * CELLS]
+    sums = []
+    for t in range(count):
+        rows = [
+            jnp.concatenate(
+                [planes[b, part, t, a * S : a * S + CELLS, :] for a in range(3) for b in range(3)], axis=1
+            )
+            for part in range(2)
+        ]
+        acc = jnp.dot(jnp.concatenate(rows, axis=0), w[...], preferred_element_type=F32)
+        sums.append(four_products(acc))
+    return sums
+
+
+def conv_in_kernel(count, where, *refs):
+    own, far, (w, main, edges, planes) = refs[0], refs[1:-4], refs[-4:]
+    clear_rims(planes)
+    first = pl.program_id(0) < pl.num_programs(0) // 2
+
+    def far_of(t):
+        return far[0][t] if len(far) == 1 else jnp.where(first, far[0][t], far[1][t])
+
+    x = jnp.concatenate([jnp.concatenate([own[t], far_of(t)], axis=0).T for t in range(count)], axis=0)
+    for t, v in enumerate(conv_tiles(x, w, planes, count)):
+        main[t] = v
+        for side in range(4):
+            edges[(t * 4 + side) * S : (t * 4 + side + 1) * S, :] = main[t, edge_rows(side), :]
+
+
+def conv_in(where, own, far, w, count):
+    tiles, half, cells = own.shape[-3:]
+    chans = 2 * half
+    steps = tiles // count
+    split = steps // 2
+    block = (count, half, cells)
+    if len(far) == 1:
+        at = lambda i, s: i
+        own_spec = pl.BlockSpec((None,) + block, lambda i, s: (s[0], i, 0, 0))
+        far_specs = [pl.BlockSpec(block, lambda i, s: (i, 0, 0))]
+    else:
+        at = lambda i, s: lax.rem(i + s[1] * split, steps)
+        own_spec = pl.BlockSpec(block, lambda i, s: (at(i, s), 0, 0))
+        far_specs = [
+            pl.BlockSpec(block, lambda i, s: (jnp.minimum(i, split - 1), 0, 0)),
+            pl.BlockSpec(block, lambda i, s: (jnp.maximum(i - split, 0), 0, 0)),
+        ]
+    return pl.pallas_call(
+        functools.partial(conv_in_kernel, count),
+        out_shape=(f32_of(tiles, cells, chans), f32_of(tiles * 4 * S, chans)),
+        grid_spec=pltpu.PrefetchScalarGridSpec(
+            num_scalar_prefetch=1,
+            grid=(steps,),
+            in_specs=[own_spec] + far_specs + [pl.BlockSpec(w.shape, lambda i, s: (0, 0))],
+            out_specs=[
+                pl.BlockSpec((count, cells, chans), lambda i, s: (at(i, s), 0, 0)),
+                pl.BlockSpec((count * 4 * S, chans), lambda i, s: (at(i, s), 0)),
+            ],
+            scratch_shapes=[planes_of(count, chans)],
+        ),
+        compiler_params=LIMIT,
+        cost_estimate=cost(2 * tiles * cells * chans * chans * 36, 4 << 20),
+    )(where, own, *far, w)
+
+
+def activation(pre):
+    g = 1.0 / (1.0 + jnp.exp(-pre))
+    return pre * g, g * (1.0 + pre * (1.0 - g))
+
+
+def conv_out_kernel(count, values_too, where, main_v, main_t, c_v, c_t, w, b1, b2, *refs):
+    outs, (planes, sums) = refs[:-2], refs[-2:]
+    clear_rims(planes)
+    chans = main_v.shape[2]
+    for k, (main, c) in enumerate(((main_v, c_v), (main_t, c_t))):
+        for t in range(count):
+            sums[k, t] = main[t]
+            for side in range(4):
+                at = edge_rows(side)
+                rows = slice((t * 4 + side) * S, (t * 4 + side + 1) * S)
+                sums[k, t, at, :] = sums[k, t, at, :] + c[rows, :]
+    values = jnp.logical_and(pl.program_id(0) == pl.num_programs(0) - 1, values_too)
+    add = jnp.where(values, b2[...], 0.0)
+    x = []
+    for t in range(count):
+        hidden, slope = activation(sums[0, t] + b1[...])
+        x.append(jnp.where(values, hidden, sums[1, t] * slope))
+    x = jnp.concatenate(x, axis=0)
+
+    def put(own, oth, v):
+        for t in range(count):
+            own[t] = v[t][: chans // 2]
+            oth[t] = v[t][chans // 2 :]
+
+    v = [(v + add).T for v in conv_tiles(x, w, planes, count)]
+    if not values_too:
+        put(outs[0], outs[1], v)
+        return
+
+    @pl.when(values)
+    def _():
+        put(outs[2], outs[3], v)
+
+    @pl.when(jnp.logical_not(values))
+    def _():
+        put(outs[0], outs[1], v)
+
+
+def conv_out(where, main_v, main_t, c_v, c_t, w, b1, b2, count, first, last, values_too):
+    _, cells, chans = main_v.shape
+    start, steps = first // count, (last - first) // count
+    v_at = lambda i, s: jnp.where(i < steps, start + i, 2 * s[0] + s[1])
+    t_at = lambda i: start + jnp.minimum(i, steps - 1)
+    out = pl.BlockSpec((count, chans // 2, cells), lambda i, s: (jnp.minimum(i, steps - 1), 0, 0))
+    share = pl.BlockSpec((count, chans // 2, cells), lambda i, s: (0, 0, 0))
+    whole = lambda r: pl.BlockSpec(r.shape, lambda i, s: (0, 0))
+    more = 1 if values_too else 0
+    return pl.pallas_call(
+        functools.partial(conv_out_kernel, count, values_too),
+        out_shape=(f32_of(last - first, chans // 2, cells),) * 2 + (f32_of(count, chans // 2, cells),) * (2 * more),
+        grid_spec=pltpu.PrefetchScalarGridSpec(
+            num_scalar_prefetch=1,
+            grid=(steps + more,),
+            in_specs=[
+                pl.BlockSpec((count, cells, chans), lambda i, s: (v_at(i, s), 0, 0)),
+                pl.BlockSpec((count, cells, chans), lambda i, s: (t_at(i), 0, 0)),
+                pl.BlockSpec((count * 4 * S, chans), lambda i, s: (v_at(i, s), 0)),
+                pl.BlockSpec((count * 4 * S, chans), lambda i, s: (t_at(i), 0)),
+                whole(w),
+                whole(b1),
+                whole(b2),
+            ],
+            out_specs=[out, out] + [share, share] * more,
+            scratch_shapes=[planes_of(count, chans), VMEM((2, count, cells, chans), F32)],
+        ),
+        compiler_params=LIMIT,
+        cost_estimate=cost(2 * (last - first) * cells * chans * chans * 36, 6 << 20),
+    )(where, main_v, main_t, c_v, c_t, w, b1, b2)
+
+
+LINE = 4
+
+
+ARRIVALS = 6
+SLOTS = LINE + 2
+
+
+def came_from(z):
+    end = jnp.logical_or(z == 0, z == LINE - 1)
+    mirrored, two_on = LINE - 1 - z, (z + 2) % LINE
+    inside = lambda where, other: jnp.where(end, other, where)
+    at_end = lambda where, other: jnp.where(end, where, other)
+    return [
+        z,
+        z ^ 1,
+        inside(mirrored, LINE),
+        at_end(mirrored, LINE),
+        inside(two_on, LINE + 1),
+        at_end(two_on, LINE + 1),
+    ]
+
+
+def source(v, tiles):
+    slot = v >> 3
+    where = slot // tiles
+    return where, slot - where * tiles, (v >> 1) & 3, (v & 1) == 1
+
+
+def rims_one_kernel(tiles, table, *refs):
+    parts, (keep, send, ring, sems) = refs[:ARRIVALS], refs[ARRIVALS:]
+    z = lax.axis_index("tiles")
+    finished(started([(e, ring.at[w]) for e, w in zip(parts, came_from(z))], sems))
+    base = tiles * 4 * S
+    low = lane_half((S, keep.shape[1]))
+    for m in range(tiles * 4):
+        where, loc, code, mirrored = source(table[z * tiles * 4 + m], tiles)
+        upper = loc // (tiles // 2)
+        t_row = pl.multiple_of((loc * 4 + code) * S, S)
+        v_row = pl.multiple_of(base + ((loc - upper * (tiles // 2)) * 4 + code) * S, S)
+        t = ring[where, pl.ds(t_row, S), :]
+        v = ring[where, pl.ds(v_row, S), :]
+        v = jnp.where(upper == 1, v, swap(v))
+        a = jnp.where(low, t, v)
+        b = jnp.where(low, swap(t), v)
+        keep[m * S : (m + 1) * S, :] = jnp.where(mirrored, flip16(a), a)
+        send[m * S : (m + 1) * S, :] = jnp.where(mirrored, flip16(b), b)
+
+
+def rims_one(table, parts, tiles):
+    rows, chans = parts[0].shape
+    out = f32_of(tiles * 4 * S, chans)
+    return pl.pallas_call(
+        functools.partial(rims_one_kernel, tiles),
+        out_shape=(out, out),
+        in_specs=[smem_spec()] + [any_spec()] * len(parts),
+        out_specs=[vmem_spec()] * 2,
+        scratch_shapes=[VMEM((SLOTS, rows, chans), F32), pltpu.SemaphoreType.DMA((len(parts),))],
+        compiler_params=LIMIT,
+        cost_estimate=cost(0, 3 << 20),
+    )(table, *parts)
+
+
+SIDE_TAPS = ((0, 1, 2), (6, 7, 8), (0, 3, 6), (2, 5, 8))
+
+
+def rim_sums(rims, w, side):
+    chans = rims.shape[1]
+    parts = [high_low(v) for v in shifts(rims)]
+    lhs = jnp.concatenate([jnp.concatenate([p[k] for p in parts], axis=1) for k in range(2)], axis=0)
+    taps = jnp.concatenate([w[tap * chans : (tap + 1) * chans, :] for tap in SIDE_TAPS[side]], axis=0)
+    return four_products(jnp.dot(lhs, taps, preferred_element_type=F32))
+
+
+def with_corners(c):
+    rows = c[0].shape[0]
+    along = lax.broadcasted_iota(jnp.int32, c[0].shape, 0) % S
+    first, last = along == 0, along == S - 1
+    down = lambda v: pltpu.roll(v, S - 1, 0)
+    up = lambda v: pltpu.roll(v, rows - S + 1, 0)
+    pick = lambda a, b: jnp.where(first, a, jnp.where(last, b, 0.0))
+    return (
+        c[0] + pick(c[2], down(c[3])),
+        c[1] + pick(up(c[2]), c[3]),
+        c[2] + pick(c[0], down(c[1])),
+        c[3] + pick(up(c[0]), c[1]),
+    )
+
+
+def seam_kernel(share, table, edges_v, edges_t, keep, far, w, bias, c_v, c_t, home, near, inner, mirror, outer, got, plain, mirrored, sem):
+    arrival = started([(far, got)], sem)
+    z = lax.axis_index("tiles")
+    q = lax.axis_index("chan") * 2 + lax.axis_index("dirs")
+    rows = edges_v.shape[0]
+    tiles = rows // (4 * S)
+    run = tiles * S
+
+    def side_of(v, side):
+        return jnp.concatenate([v[(t * 4 + side) * S : (t * 4 + side + 1) * S, :] for t in range(tiles)], axis=0)
+
+    finished(arrival)
+    low = lane_half((run, keep.shape[1]))
+    sums = []
+    for side in range(4):
+        k, g = side_of(keep, side), side_of(got, side)
+        c = rim_sums(jnp.concatenate([jnp.where(low, swap(k), g), jnp.where(low, k, swap(g))], axis=0), w, side)
+        sums.append((c[:run], c[run:]))
+    for out, k in ((c_v, 0), (c_t, 1)):
+        for side in range(4):
+            for t in range(tiles):
+                out[(t * 4 + side) * S : (t * 4 + side + 1) * S, :] = sums[side][k][t * S : (t + 1) * S]
+    sums_v = with_corners([c[0] for c in sums])
+    sums_t = with_corners([c[1] for c in sums])
+    for side in range(4):
+        hidden, slope = activation(side_of(edges_v, side) + sums_v[side] + bias[...])
+        tangent = (side_of(edges_t, side) + sums_t[side]) * slope
+        for t in range(tiles):
+            at = t * 4 + side
+            e = tangent[t * S : (t + 1) * S]
+            for msg in (home, near, inner, mirror, outer):
+                msg[at * S : (at + 1) * S, :] = e
+            v = hidden[t * S : (t + 1) * S]
+            plain[at] = v
+            mirrored[at] = flip16(v)
+    across_two = (z + 2) % LINE
+    for zz, places in (
+        (z, ((home, rows),)),
+        (z ^ 1, ((near, rows),)),
+        (LINE - 1 - z, ((inner, rows), (mirror, rows))),
+        (across_two, ((outer, rows), (inner, rows + share * 4 * S))),
+    ):
+        for m in range(share * 4):
+            where, loc, code, flip = source(table[(zz * tiles + q * share) * 4 + m], tiles)
+            at = loc * 4 + code
+            v = jnp.where(flip, mirrored[at], plain[at])
+            v = jnp.where(where == z, v, 0.0)
+            for msg, base in places:
+                msg[base + m * S : base + (m + 1) * S, :] = v
+
+
+def seam(table, edges_v, edges_t, keep, far, w, bias, share):
+    rows, chans = edges_v.shape
+    tail = share * 4 * S
+    single, double = f32_of(rows + tail, chans), f32_of(rows + 2 * tail, chans)
+    outs = pl.pallas_call(
+        functools.partial(seam_kernel, share),
+        out_shape=(f32_of(rows, chans),) * 2 + (single, single, double, single, single),
+        in_specs=[smem_spec()] + [vmem_spec()] * 3 + [any_spec()] + [vmem_spec()] * 2,
+        out_specs=[vmem_spec()] * 7,
+        scratch_shapes=[
+            VMEM((rows, chans), F32),
+            VMEM((rows // S, S, chans), F32),
+            VMEM((rows // S, S, chans), F32),
+            pltpu.SemaphoreType.DMA((1,)),
+        ],
+        compiler_params=LIMIT,
+        cost_estimate=cost(0, 5 << 20),
+    )(table, edges_v, edges_t, keep, far, w, bias)
+    return outs[0], outs[1], outs[2:]
+
+
+def rims_two_kernel(tiles, share, table, *refs):
+    parts, w = refs[:ARRIVALS], refs[ARRIVALS]
+    keep_t, send_t, keep_v, send_v, ring, rims_v, rims, c_t, c_v, sems = refs[ARRIVALS + 1 :]
+    z = lax.axis_index("tiles")
+    rows, tail = tiles * 4 * S, share * 4 * S
+    bases = [rows] * (ARRIVALS - 1) + [rows + tail]
+    pairs = [(e.at[pl.ds(0, rows)], ring.at[where]) for e, where in zip(parts, came_from(z))]
+    pairs += [(e.at[pl.ds(base, tail)], rims_v.at[k]) for k, (e, base) in enumerate(zip(parts, bases))]
+    finished(started(pairs, sems))
+    for m in range(tiles * 4):
+        where, loc, code, mirrored = source(table[z * tiles * 4 + m], tiles)
+        e = ring[where, pl.ds(pl.multiple_of((loc * 4 + code) * S, S), S), :]
+        rims[m * S : (m + 1) * S, :] = jnp.where(mirrored, flip16(e), e)
+    rims[rows:, :] = ((rims_v[0] + rims_v[1]) + (rims_v[2] + rims_v[3])) + (rims_v[4] + rims_v[5])
+    every = tiles + share
+    for side in range(4):
+        part = jnp.concatenate([rims[(t * 4 + side) * S : (t * 4 + side + 1) * S, :] for t in range(every)], axis=0)
+        c = rim_sums(part, w, side)
+        for t in range(tiles):
+            c_t[(t * 4 + side) * S : (t * 4 + side + 1) * S, :] = c[t * S : (t + 1) * S]
+        for t in range(share):
+            c_v[(t * 4 + side) * S : (t * 4 + side + 1) * S, :] = c[(tiles + t) * S : (tiles + t + 1) * S]
+    for c, keep, send in ((c_t, keep_t, send_t), (c_v, keep_v, send_v)):
+        half = c.shape[0] // 2
+        a, b = c[0:half, :], c[half:, :]
+        low = lane_half(a.shape)
+        keep[...] = jnp.where(low, a, swap(b))
+        send[...] = jnp.where(low, swap(a), b)
+
+
+def rims_two(table, parts, w, tiles, share):
+    chans = parts[0].shape[1]
+    rows, tail = tiles * 4 * S, share * 4 * S
+    return pl.pallas_call(
+        functools.partial(rims_two_kernel, tiles, share),
+        out_shape=(f32_of(rows // 2, chans),) * 2 + (f32_of(tail // 2, chans),) * 2,
+        in_specs=[smem_spec()] + [any_spec()] * len(parts) + [vmem_spec()],
+        out_specs=[vmem_spec()] * 4,
+        scratch_shapes=[
+            VMEM((SLOTS, rows, chans), F32),
+            VMEM((ARRIVALS, tail, chans), F32),
+            VMEM((rows + tail, chans), F32),
+            VMEM((rows, chans), F32),
+            VMEM((tail, chans), F32),
+            pltpu.SemaphoreType.DMA((2 * len(parts),)),
+        ],
+        compiler_params=LIMIT,
+        cost_estimate=cost(0, 4 << 20),
+    )(table, *parts, w)
+
+
+def finish_kernel(own_a, own_b, far_a, far_b, v_own, v_far, v_mate, v_diag, c_own, c_far, cv_own, cv_far, cv_mate, cv_diag, out_v, out_t):
+    x = lax.axis_index("chan")
+    d = lax.axis_index("dirs")
+    share, half, _ = v_own.shape
+    pick = edge_cells(4 * S)
+    pick = jnp.concatenate([pick, pick], axis=0)
+
+    def spread(c, k):
+        c = below(c[k * 4 * S : (k + 1) * 4 * S, :])
+        return lax.dot_general(c, pick, (((0,), (0,)), ((), ())), preferred_element_type=F32)
+
+    group = own_a.shape[0]
+    for at, a, b, c in ((x, own_a, own_b, c_own), (1 - x, far_a, far_b, c_far)):
+        for t in range(group):
+            v = spread(c, t)
+            out_t[at, t] = a[t] + v[:half]
+            out_t[at, t + group] = b[t] + v[half:]
+    for q, main, c in (
+        (x * 2 + d, v_own, cv_own),
+        ((1 - x) * 2 + d, v_far, cv_far),
+        (x * 2 + 1 - d, v_mate, cv_mate),
+        ((1 - x) * 2 + 1 - d, v_diag, cv_diag),
+    ):
+        for t in range(share // 2):
+            v = spread(c, t)
+            out_v[q * share + t] = main[t] + v[:half]
+            out_v[q * share + t + share // 2] = main[t + share // 2] + v[half:]
+
+
+def finish(tiles, *arrays):
+    half, cells = arrays[0].shape[1:]
+    return pl.pallas_call(
+        finish_kernel,
+        out_shape=(f32_of(tiles, half, cells), f32_of(2, tiles, half, cells)),
+        in_specs=[vmem_spec()] * len(arrays),
+        out_specs=[vmem_spec()] * 2,
+        compiler_params=LIMIT,
+        cost_estimate=cost(0, 6 << 20),
+    )(*arrays)
+
+
+def across(v):
+    return lax.ppermute(v, "chan", [(0, 1), (1, 0)])
+
+
+def mate(v):
+    return lax.ppermute(v, "dirs", [(0, 1), (1, 0)])
+
+
+def along(v, pairs):
+    return lax.ppermute(v, "tiles", pairs)
+
+
+def to_all(home, near, inner, mirror, outer):
+    inner = along(inner, [(1, 2), (2, 1)])
+    near = along(near, [(0, 1), (1, 0), (2, 3), (3, 2)])
+    mirror = along(mirror, [(0, 3), (3, 0)])
+    outer = along(outer, [(0, 2), (3, 1)])
+    passed = along(inner, [(2, 3), (1, 0)])
+    return [home, near, inner, mirror, outer, passed]
+
+
+def split_streams(field, tangents, weight_one, bias_one, weight_two, bias_two, adjacency, side_code, mirror_flag, placement):
+    tiles = field.shape[0]
+    share = tiles // 4
+    edges, t_send, f_send, where = read_inputs(tangents, field)
+    edges = to_all(*(edges,) * 5)
+    f_far = across(f_send)
+    t_far = across(t_send)
+    table = index_table((adjacency * 4 + side_code) * 2 + mirror_flag, placement)
+    w1, w2, b1, b2 = prepare_weights(weight_one, bias_one, weight_two, bias_two)
+    main_v, edges_v = conv_in(where, field, (f_far, mate(f_far)), w1, share)
+    main_t, edges_t = conv_in(where, tangents, (t_far,), w1, share)
+    keep, send = rims_one(table, edges, tiles)
+    far = across(send)
+    c_v, c_t, messages = seam(table, edges_v, edges_t, keep, far, w1, b1, share)
+    edges = to_all(*messages)
+    mains = (where, main_v, main_t, c_v, c_t, w2, b1, b2, share)
+    own_a, oth_a = conv_out(*mains, 0, tiles // 2, False)
+    own_b, oth_b, v_own, v_oth = conv_out(*mains, tiles // 2, tiles, True)
+    far_a, far_b, v_far = across(oth_a), across(oth_b), across(v_oth)
+    v_mate, v_diag = mate(v_own), mate(v_far)
+    c_own, c_send, cv_own, cv_send = rims_two(table, edges, w2, tiles, share)
+    cv_mate = mate(cv_own)
+    cv_far = across(cv_send)
+    c_far = across(c_send)
+    cv_diag = mate(cv_far)
+    arrays = (own_a, own_b, far_a, far_b, v_own, v_far, v_mate, v_diag, c_own, c_far, cv_own, cv_far, cv_mate, cv_diag)
+    return finish(tiles, *arrays)
 
 
 def static_tables():
@@ -146,25 +808,19 @@
 
 
 def solution(mesh):
-    placed = (
-        P(("members", "tiles"), "chan", None),
-        P("dirs", ("members", "tiles"), "chan", None),
-        P(),
-        P(),
-        P(),
-        P(),
-        P(),
-        P(),
-        P(),
-        P(),
-    )
+    shared = ("members", "tiles")
+    placed = (P(shared, "chan", None), P("dirs", shared, "chan", None)) + (P(),) * 8
+
+    def program(field, tangents, *rest):
+        sizes = (mesh.shape["tiles"], mesh.shape["chan"], mesh.shape["dirs"])
+        if sizes == (LINE, 2, 2) and tangents.shape[0] == 2 and field.shape[0] == 8:
+            return split_streams(field, tangents, *rest)
+        return local(field, tangents, *rest)
+
     return jax.shard_map(
-        local,
+        program,
         mesh=mesh,
         in_specs=placed,
-        out_specs=(
-            P(("members", "tiles"), "chan", None),
-            P("dirs", ("members", "tiles"), "chan", None),
-        ),
+        out_specs=(P(shared, "chan", None), P("dirs", shared, "chan", None)),
         check_vma=False,
     )

time: 607 us -> 114 us (0.19); the launches traced: 596 us -> 113 us
  local copies, waits for them, and re-layouts: 293 us -> 4.32 us
  waiting for transfers between devices: 191 us -> 28.8 us
  matrix products: 52.6 us -> 0 us
  starting transfers between devices: 0.16 us -> 49.3 us
  other arithmetic: 45.5 us -> 0.74 us
  Pallas kernels: 0 us -> 29.5 us
  between operations: 14.5 us -> 0.94 us
    all_gather x4 -> x0, waiting for transfers between devices: 191 us -> none  [the longest x2 123 us: layer_sums(): gathered = lax.all_gather(padded, 'chan', axis=2, tiled=True)]
    gather x16 -> x0, local copies, waits for them, and re-layouts: 86.3 us -> none  [the longest x5 68.6 us: pad_fields(): return jnp.take_along_axis(source, index[None, :, None, :], axis=-1)]
    unnamed x68 -> x25, local copies, waits for them, and re-layouts: 89.5 us -> 3.63 us
    dot_general x2 -> x0, matrix products: 52.6 us -> none  [convolve(): jnp.einsum('kc,btcl->btkl', flat_weight, padded, precision=lax.Precision....]
    ppermute x0 -> x23, starting transfers between devices: none -> 49.3 us  [the longest x10 38.8 us: along(): return lax.ppermute(v, 'tiles', pairs)]
    transpose x4 -> x0, local copies, waits for them, and re-layouts: 49.2 us -> none  [the longest x2 44.5 us: convolve(): jnp.einsum('kc,btcl->btkl', flat_weight, padded, precision=lax.Precision....]
    pallas_call x0 -> x11, Pallas kernels: none -> 29.5 us  [the longest x2 11.3 us: conv_in(): pl.pallas_call(functools.partial(conv_in_kernel, count), out_shape=(f32_o...]
    ppermute x0 -> x23, waiting for transfers between devices: none -> 28.8 us  [the longest x10 19.9 us: along(): return lax.ppermute(v, 'tiles', pairs)]
  transfers between devices with their start and end apart: 4 -> 23, of which waited for: 4 -> 7; matrix products, arithmetic and copies ran while one was open for 2% -> 2% of each run, Pallas kernels for 0% -> 22%
where the time goes in v1:
time: 114 us; the launch traced here: 113 us
  starting transfers between devices  49.3 us (43%)
  Pallas kernels  29.5 us (26%)
  waiting for transfers between devices  28.8 us (25%)
  local copies, waits for them, and re-layouts  4.32 us (4%)
    ppermute x10, starting transfers between devices, along(): return lax.ppermute(v, 'tiles', pairs)  38.8 us
    ppermute x10, waiting for transfers between devices, along(): return lax.ppermute(v, 'tiles', pairs)  19.9 us
    pallas_call x2, Pallas kernels, conv_in(): pl.pallas_call(functools.partial(conv_in_kernel, count), out_shape=(f32_o...  11.3 us
    ppermute x8, starting transfers between devices, across(): return lax.ppermute(v, 'chan', [(0, 1), (1, 0)])  9.91 us
    ppermute x8, waiting for transfers between devices, across(): return lax.ppermute(v, 'chan', [(0, 1), (1, 0)])  7.62 us
    pallas_call x2, Pallas kernels, conv_out(): pl.pallas_call(functools.partial(conv_out_kernel, count, values_too), out...  6.9 us
    unnamed x25, local copies, waits for them, and re-layouts  3.63 us
    pallas_call x1, Pallas kernels, rims_one(): pl.pallas_call(functools.partial(rims_one_kernel, tiles), out_shape=(out,...  2.36 us
  transfers between devices with their start and end apart: 23, of which 7 were waited for; matrix products, arithmetic and copies ran while one was open for 2% of the time, Pallas kernels for 22%

profile of v1, /device:TPU:0, one launch (start us, length us, event | category | flops | bytes accessed | tf_op | source)
XLA Modules:
  0.0 113.5 jit_solution(9529385010824931769)
XLA Ops:
  2.9 1.4 %shard_map.113 = (f32[768,128]{1,0:T(8,128)S(1)}, f32[8,64,256]{2,1,0:T(8,128)}, f32[4,64,256]{2,1,0:T(8,128)S(1)}, s32[2]{0:T(128)S(1)}) custom-call(f32[2,8,64,256]{3,2,1,0:T(8,128)S(1)} %copy-done, f32[8,64,256]{2,1,0:T(8,128)S(1)} %copy-done.4), custom_call_target="tpu_custom_call" | custom-call | bytes 3145728 | tf_op jit(solution)/shard_map/pallas_call | solution.py:163
  5.0 3.0 %collective-permute-start = (f32[4,64,256]{2,1,0:T(8,128)S(1)}, f32[4,64,256]{2,1,0:T(8,128)}, u32[]{:S(2)}, u32[]{:S(2)}) collective-permute-start(f32[4,64,256]{2,1,0:T(8,128)S(1)} %get-tuple-element.34), channel_id=1, source_target_pairs={{0,2},{2,0},{1,3},{3,1},{4,6},{6,4},{5,7},{7,5},{8,10},{10,8},{9,1... | collective-permute-start | bytes 786440 | tf_op jit(solution)/shard_map/ppermute | solution.py:623
  8.1 6.2 %collective-permute-start.6 = (f32[768,128]{1,0:T(8,128)S(1)}, f32[768,128]{1,0:T(8,128)S(1)}, u32[]{:S(2)}, u32[]{:S(2)}) collective-permute-start(f32[768,128]{1,0:T(8,128)S(1)} %get-tuple-element.41.refs_0_), channel_id=1, source_target_pairs={{0,8},{12,4},{1,9},{13,5},{2,10},{14,6},{3,11},{15,7},{16,24},{28,... | collective-permute-start | bytes 1179656 | tf_op jit(solution)/shard_map/ppermute | solution.py:631
  14.9 4.4 %collective-permute-start.5 = (f32[768,128]{1,0:T(8,128)S(1)}, f32[768,128]{1,0:T(8,128)S(1)}, u32[]{:S(2)}, u32[]{:S(2)}) collective-permute-start(f32[768,128]{1,0:T(8,128)S(1)} %get-tuple-element.41.refs_0_), channel_id=1, source_target_pairs={{0,12},{12,0},{1,13},{13,1},{2,14},{14,2},{3,15},{15,3},{16,28},{2... | collective-permute-start | bytes 1179656 | tf_op jit(solution)/shard_map/ppermute | solution.py:631
  24.5 1.8 %shard_map.117.table = s32[128]{0:T(128)S(1)} custom-call(s32[32,4]{1,0:T(8,128)S(1)} %multiply_add_fusion.packed, s32[32]{0:T(128)S(1)} %copy-done.8), custom_call_target="tpu_custom_call" | custom-call | bytes 1048576 | tf_op jit(solution)/shard_map/pallas_call | solution.py:199
  27.4 7.8 %collective-permute-done.5.refs_3_ = f32[768,128]{1,0:T(8,128)S(1)} collective-permute-done((f32[768,128]{1,0:T(8,128)S(1)}, f32[768,128]{1,0:T(8,128)S(1)}, u32[]{:S(2)}, u32[]{:S(2)}) %collective-permute-start.5) | collective-permute-done | bytes 393248 | tf_op jit(solution)/shard_map/ppermute | solution.py:631
  35.1 3.8 %collective-permute-done.3.refs_1_ = f32[768,128]{1,0:T(8,128)S(1)} collective-permute-done((f32[768,128]{1,0:T(8,128)S(1)}, f32[768,128]{1,0:T(8,128)S(1)}, u32[]{:S(2)}, u32[]{:S(2)}) %collective-permute-start.3) | collective-permute-done | bytes 393248 | tf_op jit(solution)/shard_map/ppermute | solution.py:631
  39.0 7.5 %collective-permute-done.7.refs_5_ = f32[768,128]{1,0:T(8,128)S(1)} collective-permute-done((f32[768,128]{1,0:T(8,128)S(1)}, f32[768,128]{1,0:T(8,128)S(1)}, u32[]{:S(2)}, u32[]{:S(2)}) %collective-permute-start.7) | collective-permute-done | bytes 393248 | tf_op jit(solution)/shard_map/ppermute | solution.py:631
  46.5 2.4 %shard_map.118 = (f32[512,128]{1,0:T(8,128)S(1)}, f32[512,128]{1,0:T(8,128)S(1)}) custom-call(s32[128]{0:T(128)S(1)} %shard_map.117.table, f32[768,128]{1,0:T(8,128)S(1)} %get-tuple-element.41.refs_0_, f32[768,128]{1,0:T(8,128)S(1)} %collective-permute-done.3.refs_1_, f32[768,128]{1,0:T(8,128)S(1)} %collective-permute-done.4.refs_2_, ...), custom_call_target="tpu_custom_call" | custom-call | bytes 3145728 | tf_op jit(solution)/shard_map/pallas_call | solution.py:421
  48.9 1.6 %collective-permute-start.8 = (f32[512,128]{1,0:T(8,128)S(1)}, f32[512,128]{1,0:T(8,128)S(1)}, u32[]{:S(2)}, u32[]{:S(2)}) collective-permute-start(f32[512,128]{1,0:T(8,128)S(1)} %get-tuple-element.43), channel_id=1, source_target_pairs={{0,2},{2,0},{1,3},{3,1},{4,6},{6,4},{5,7},{7,5},{8,10},{10,8},{9,1... | collective-permute-start | bytes 786440 | tf_op jit(solution)/shard_map/ppermute | solution.py:623
  50.5 5.6 %shard_map.116 = (f32[8,256,128]{2,1,0:T(8,128)S(1)}, f32[512,128]{1,0:T(8,128)S(1)}) custom-call(s32[2]{0:T(128)S(1)} %get-tuple-element.33.where, f32[2,8,64,256]{3,2,1,0:T(8,128)S(1)} %copy-done.1, f32[8,64,256]{2,1,0:T(8,128)} %collective-permute-done.2.refs_1_, bf16[1152,256]{1,0:T(8,128)(2,1)S(1)} %get-tuple-element.35.refs_3_.refs_2_.w), custom_call_target="tpu_custom_call" | custom-call | flops 2415919104 | bytes 4194304 | tf_op jit(solution)/shard_map/pallas_call | solution.py:277
  56.1 5.6 %shard_map.115 = (f32[8,256,128]{2,1,0:T(8,128)S(1)}, f32[512,128]{1,0:T(8,128)S(1)}) custom-call(s32[2]{0:T(128)S(1)} %get-tuple-element.33.where, f32[8,64,256]{2,1,0:T(8,128)S(1)} %copy-done.5, f32[4,64,256]{2,1,0:T(8,128)} %collective-permute-done.refs_1_, f32[4,64,256]{2,1,0:T(8,128)S(1)} %collective-permute-done.1.refs_2_, ...), custom_call_target="tpu_custom_call" | custom-call | flops 2415919104 | bytes 4194304 | tf_op jit(solution)/shard_map/pallas_call | solution.py:277
  61.8 1.8 %shard_map.119 = (f32[512,128]{1,0:T(8,128)S(1)}, f32[512,128]{1,0:T(8,128)S(1)}, f32[640,128]{1,0:T(8,128)S(1)}, f32[640,128]{1,0:T(8,128)S(1)}, f32[768,128]{1...) custom-call(s32[128]{0:T(128)S(1)} %shard_map.117.table, f32[512,128]{1,0:T(8,128)S(1)} %get-tuple-element.39.edges_v, ...), custom_call_target="tpu_custom_call" | custom-call | bytes 5242880 | tf_op jit(solution)/shard_map/pallas_call | solution.py:513
  64.3 2.4 %collective-permute-start.14 = (f32[640,128]{1,0:T(8,128)S(1)}, f32[640,128]{1,0:T(8,128)S(1)}, u32[]{:S(2)}, u32[]{:S(2)}) collective-permute-start(f32[640,128]{1,0:T(8,128)S(1)} %get-tuple-element.56), channel_id=1, source_target_pairs={{0,4},{4,0},{8,12},{12,8},{1,5},{5,1},{9,13},{13,9},{2,6},{6,2},{1... | collective-permute-start | bytes 983048 | tf_op jit(solution)/shard_map/ppermute | solution.py:631
  66.7 3.3 %collective-permute-start.16 = (f32[640,128]{1,0:T(8,128)S(1)}, f32[640,128]{1,0:T(8,128)S(1)}, u32[]{:S(2)}, u32[]{:S(2)}) collective-permute-start(f32[640,128]{1,0:T(8,128)S(1)} %get-tuple-element.58), channel_id=1, source_target_pairs={{0,12},{12,0},{1,13},{13,1},{2,14},{14,2},{3,15},{15,3},{16,28},{2... | collective-permute-start | bytes 983048 | tf_op jit(solution)/shard_map/ppermute | solution.py:631
  71.3 17.7 %collective-permute-start.17 = (f32[640,128]{1,0:T(8,128)S(1)}, f32[640,128]{1,0:T(8,128)S(1)}, u32[]{:S(2)}, u32[]{:S(2)}) collective-permute-start(f32[640,128]{1,0:T(8,128)S(1)} %get-tuple-element.59), channel_id=1, source_target_pairs={{0,8},{12,4},{1,9},{13,5},{2,10},{14,6},{3,11},{15,7},{16,24},{28,... | collective-permute-start | bytes 983048 | tf_op jit(solution)/shard_map/ppermute | solution.py:631
  89.0 4.1 %shard_map.121 = (f32[4,64,256]{2,1,0:T(8,128)S(1)}, f32[4,64,256]{2,1,0:T(8,128)S(1)}, f32[2,64,256]{2,1,0:T(8,128)S(1)}, f32[2,64,256]{2,1,0:T(8,128)S(1)}) custom-call(s32[2]{0:T(128)S(1)} %get-tuple-element.33.where, f32[8,256,128]{2,1,0:T(8,128)S(1)} %get-tuple-element.36.main_v, f32[8,256,128]{2,1,0:T(8,128)S(1)} %get-tuple-element.38.main_t, ...), custom_call_target="tpu_custom_call" | custom-call | flops 1207959552 | bytes 6291456 | tf_op jit(solution)/shard_map/pallas_call | solution.py:347
  93.7 2.8 %shard_map.120 = (f32[4,64,256]{2,1,0:T(8,128)S(1)}, f32[4,64,256]{2,1,0:T(8,128)S(1)}) custom-call(s32[2]{0:T(128)S(1)} %get-tuple-element.33.where, f32[8,256,128]{2,1,0:T(8,128)S(1)} %get-tuple-element.36.main_v, f32[8,256,128]{2,1,0:T(8,128)S(1)} %get-tuple-element.38.main_t, f32[512,128]{1,0:T(8,128)S(1)} %get-tuple-element.45.c_v, ...), custom_call_target="tpu_custom_call" | custom-call | flops 1207959552 | bytes 6291456 | tf_op jit(solution)/shard_map/pallas_call | solution.py:347
  96.5 1.6 %collective-permute-done.11.v_far = f32[2,64,256]{2,1,0:T(8,128)S(1)} collective-permute-done((f32[2,64,256]{2,1,0:T(8,128)S(1)}, f32[2,64,256]{2,1,0:T(8,128)S(1)}, u32[]{:S(2)}, u32[]{:S(2)}) %collective-permute-start.11) | collective-permute-done | bytes 131104 | tf_op jit(solution)/shard_map/ppermute | solution.py:623
  98.6 1.5 %collective-permute-start.10 = (f32[4,64,256]{2,1,0:T(8,128)S(1)}, f32[4,64,256]{2,1,0:T(8,128)S(1)}, u32[]{:S(2)}, u32[]{:S(2)}) collective-permute-start(f32[4,64,256]{2,1,0:T(8,128)S(1)} %get-tuple-element.52), channel_id=1, source_target_pairs={{0,2},{2,0},{1,3},{3,1},{4,6},{6,4},{5,7},{7,5},{8,10},{10,8},{9,1... | collective-permute-start | bytes 786440 | tf_op jit(solution)/shard_map/ppermute | solution.py:623
  100.7 2.0 %shard_map.122 = (f32[256,128]{1,0:T(8,128)S(1)}, f32[256,128]{1,0:T(8,128)S(1)}, f32[64,128]{1,0:T(8,128)S(1)}, f32[64,128]{1,0:T(8,128)S(1)}) custom-call(s32[128]{0:T(128)S(1)} %shard_map.117.table, f32[640,128]{1,0:T(8,128)S(1)} %get-tuple-element.55.refs_0_, f32[640,128]{1,0:T(8,128)S(1)} %collective-permute-done.14.refs_1_, ...), custom_call_target="tpu_custom_call" | custom-call | bytes 4194304 | tf_op jit(solution)/shard_map/pallas_call | solution.py:563
  103.3 1.5 %collective-permute-start.20 = (f32[64,128]{1,0:T(8,128)S(1)}, f32[64,128]{1,0:T(8,128)S(1)}, u32[]{:S(2)}, u32[]{:S(2)}) collective-permute-start(f32[64,128]{1,0:T(8,128)S(1)} %get-tuple-element.63), channel_id=1, source_target_pairs={{0,2},{2,0},{1,3},{3,1},{4,6},{6,4},{5,7},{7,5},{8,10},{10,8},{9,1... | collective-permute-start | bytes 98312 | tf_op jit(solution)/shard_map/ppermute | solution.py:623
  104.8 6.0 %collective-permute-done.20.cv_far = f32[64,128]{1,0:T(8,128)S(1)} collective-permute-done((f32[64,128]{1,0:T(8,128)S(1)}, f32[64,128]{1,0:T(8,128)S(1)}, u32[]{:S(2)}, u32[]{:S(2)}) %collective-permute-start.20) | collective-permute-done | bytes 32800 | tf_op jit(solution)/shard_map/ppermute | solution.py:623
  112.0 1.5 %shard_map.123 = (f32[8,64,256]{2,1,0:T(8,128)}, f32[2,8,64,256]{3,2,1,0:T(8,128)}) custom-call(f32[4,64,256]{2,1,0:T(8,128)S(1)} %get-tuple-element.49.own_a, f32[4,64,256]{2,1,0:T(8,128)S(1)} %get-tuple-element.50.own_b, f32[4,64,256]{2,1,0:T(8,128)S(1)} %collective-permute-done.9.far_a, f32[4,64,256]{2,1,0:T(8,128)S(1)} %collective-permute-done.10.far_b, ...), custom_call_target="tpu_custom_call" | custom-call | bytes 6291456 | tf_op jit(solution)/shard_map/pallas_call | solution.py:612
  (61 shorter events, 15.2 us)
Async XLA Ops:
  2.9 23.4 %copy-start.3 = (f32[9,128,128]{2,1,0:T(8,128)S(1)}, f32[9,128,128]{2,1,0:T(8,128)}, u32[]{:S(2)}) copy-start(f32[9,128,128]{2,1,0:T(8,128)} %w2.1) | copy-start | bytes 1769476
  4.4 15.9 %collective-permute-start.4 = (f32[768,128]{1,0:T(8,128)S(1)}, f32[768,128]{1,0:T(8,128)S(1)}, u32[]{:S(2)}, u32[]{:S(2)}) collective-permute-start(f32[768,128]{1,0:T(8,128)S(1)} %get-tuple-element.41.refs_0_), channel_id=1, source_target_pairs={{4,8},{8,4},{5,9},{9,5},{6,10},{10,6},{7,11},{11,7},{20,24},{24,20... | collective-permute-start | bytes 1179656 | tf_op jit(solution)/shard_map/ppermute | solution.py:631
  5.0 14.2 %collective-permute-start = (f32[4,64,256]{2,1,0:T(8,128)S(1)}, f32[4,64,256]{2,1,0:T(8,128)}, u32[]{:S(2)}, u32[]{:S(2)}) collective-permute-start(f32[4,64,256]{2,1,0:T(8,128)S(1)} %get-tuple-element.34), channel_id=1, source_target_pairs={{0,2},{2,0},{1,3},{3,1},{4,6},{6,4},{5,7},{7,5},{8,10},{10,8},{9,1... | collective-permute-start | bytes 786440 | tf_op jit(solution)/shard_map/ppermute | solution.py:623
  8.1 15.6 %collective-permute-start.6 = (f32[768,128]{1,0:T(8,128)S(1)}, f32[768,128]{1,0:T(8,128)S(1)}, u32[]{:S(2)}, u32[]{:S(2)}) collective-permute-start(f32[768,128]{1,0:T(8,128)S(1)} %get-tuple-element.41.refs_0_), channel_id=1, source_target_pairs={{0,8},{12,4},{1,9},{13,5},{2,10},{14,6},{3,11},{15,7},{16,24},{28,... | collective-permute-start | bytes 1179656 | tf_op jit(solution)/shard_map/ppermute | solution.py:631
  14.3 36.2 %collective-permute-start.2 = (f32[8,64,256]{2,1,0:T(8,128)}, f32[8,64,256]{2,1,0:T(8,128)}, u32[]{:S(2)}, u32[]{:S(2)}) collective-permute-start(f32[8,64,256]{2,1,0:T(8,128)} %get-tuple-element.37), channel_id=1, source_target_pairs={{0,2},{2,0},{1,3},{3,1},{4,6},{6,4},{5,7},{7,5},{8,10},{10,8},{9,1... | collective-permute-start | bytes 1572872 | tf_op jit(solution)/shard_map/ppermute | solution.py:623
  14.9 20.3 %collective-permute-start.5 = (f32[768,128]{1,0:T(8,128)S(1)}, f32[768,128]{1,0:T(8,128)S(1)}, u32[]{:S(2)}, u32[]{:S(2)}) collective-permute-start(f32[768,128]{1,0:T(8,128)S(1)} %get-tuple-element.41.refs_0_), channel_id=1, source_target_pairs={{0,12},{12,0},{1,13},{13,1},{2,14},{14,2},{3,15},{15,3},{16,28},{2... | collective-permute-start | bytes 1179656 | tf_op jit(solution)/shard_map/ppermute | solution.py:631
  19.3 19.7 %collective-permute-start.3 = (f32[768,128]{1,0:T(8,128)S(1)}, f32[768,128]{1,0:T(8,128)S(1)}, u32[]{:S(2)}, u32[]{:S(2)}) collective-permute-start(f32[768,128]{1,0:T(8,128)S(1)} %get-tuple-element.41.refs_0_), channel_id=1, source_target_pairs={{0,4},{4,0},{8,12},{12,8},{1,5},{5,1},{9,13},{13,9},{2,6},{6,2},{1... | collective-permute-start | bytes 1179656 | tf_op jit(solution)/shard_map/ppermute | solution.py:631
  20.3 26.3 %collective-permute-start.7 = (f32[768,128]{1,0:T(8,128)S(1)}, f32[768,128]{1,0:T(8,128)S(1)}, u32[]{:S(2)}, u32[]{:S(2)}) collective-permute-start(f32[768,128]{1,0:T(8,128)S(1)} %collective-permute-done.4.refs_2_), channel_id=1, source_target_pairs={{8,12},{4,0},{9,13},{5,1},{10,14},{6,2},{11,15},{7,3},{24,28},{20,... | collective-permute-start | bytes 1179656 | tf_op jit(solution)/shard_map/ppermute | solution.py:631
  23.7 32.4 %collective-permute-start.1 = (f32[4,64,256]{2,1,0:T(8,128)}, f32[4,64,256]{2,1,0:T(8,128)S(1)}, u32[]{:S(2)}, u32[]{:S(2)}) collective-permute-start(f32[4,64,256]{2,1,0:T(8,128)} %collective-permute-done.refs_1_), channel_id=1, source_target_pairs={{0,1},{1,0},{2,3},{3,2},{4,5},{5,4},{6,7},{7,6},{8,9},{9,8},{10,11... | collective-permute-start | bytes 786440 | tf_op jit(solution)/shard_map/ppermute | solution.py:627
  48.9 12.9 %collective-permute-start.8 = (f32[512,128]{1,0:T(8,128)S(1)}, f32[512,128]{1,0:T(8,128)S(1)}, u32[]{:S(2)}, u32[]{:S(2)}) collective-permute-start(f32[512,128]{1,0:T(8,128)S(1)} %get-tuple-element.43), channel_id=1, source_target_pairs={{0,2},{2,0},{1,3},{3,1},{4,6},{6,4},{5,7},{7,5},{8,10},{10,8},{9,1... | collective-permute-start | bytes 786440 | tf_op jit(solution)/shard_map/ppermute | solution.py:623
  63.6 6.4 %collective-permute-start.15 = (f32[768,128]{1,0:T(8,128)S(1)}, f32[768,128]{1,0:T(8,128)S(1)}, u32[]{:S(2)}, u32[]{:S(2)}) collective-permute-start(f32[768,128]{1,0:T(8,128)S(1)} %get-tuple-element.57), channel_id=1, source_target_pairs={{4,8},{8,4},{5,9},{9,5},{6,10},{10,6},{7,11},{11,7},{20,24},{24,20... | collective-permute-start | bytes 1179656 | tf_op jit(solution)/shard_map/ppermute | solution.py:631
  64.3 34.3 %collective-permute-start.14 = (f32[640,128]{1,0:T(8,128)S(1)}, f32[640,128]{1,0:T(8,128)S(1)}, u32[]{:S(2)}, u32[]{:S(2)}) collective-permute-start(f32[640,128]{1,0:T(8,128)S(1)} %get-tuple-element.56), channel_id=1, source_target_pairs={{0,4},{4,0},{8,12},{12,8},{1,5},{5,1},{9,13},{13,9},{2,6},{6,2},{1... | collective-permute-start | bytes 983048 | tf_op jit(solution)/shard_map/ppermute | solution.py:631
  66.7 33.4 %collective-permute-start.16 = (f32[640,128]{1,0:T(8,128)S(1)}, f32[640,128]{1,0:T(8,128)S(1)}, u32[]{:S(2)}, u32[]{:S(2)}) collective-permute-start(f32[640,128]{1,0:T(8,128)S(1)} %get-tuple-element.58), channel_id=1, source_target_pairs={{0,12},{12,0},{1,13},{13,1},{2,14},{14,2},{3,15},{15,3},{16,28},{2... | collective-permute-start | bytes 983048 | tf_op jit(solution)/shard_map/ppermute | solution.py:631
  70.0 30.7 %collective-permute-start.18 = (f32[768,128]{1,0:T(8,128)S(1)}, f32[768,128]{1,0:T(8,128)S(1)}, u32[]{:S(2)}, u32[]{:S(2)}) collective-permute-start(f32[768,128]{1,0:T(8,128)S(1)} %collective-permute-done.15.refs_2_), channel_id=1, source_target_pairs={{8,12},{4,0},{9,13},{5,1},{10,14},{6,2},{11,15},{7,3},{24,28},{20,... | collective-permute-start | bytes 1179656 | tf_op jit(solution)/shard_map/ppermute | solution.py:631
  71.3 28.8 %collective-permute-start.17 = (f32[640,128]{1,0:T(8,128)S(1)}, f32[640,128]{1,0:T(8,128)S(1)}, u32[]{:S(2)}, u32[]{:S(2)}) collective-permute-start(f32[640,128]{1,0:T(8,128)S(1)} %get-tuple-element.59), channel_id=1, source_target_pairs={{0,8},{12,4},{1,9},{13,5},{2,10},{14,6},{3,11},{15,7},{16,24},{28,... | collective-permute-start | bytes 983048 | tf_op jit(solution)/shard_map/ppermute | solution.py:631
  93.1 5.0 %collective-permute-start.11 = (f32[2,64,256]{2,1,0:T(8,128)S(1)}, f32[2,64,256]{2,1,0:T(8,128)S(1)}, u32[]{:S(2)}, u32[]{:S(2)}) collective-permute-start(f32[2,64,256]{2,1,0:T(8,128)S(1)} %get-tuple-element.54), channel_id=1, source_target_pairs={{0,2},{2,0},{1,3},{3,1},{4,6},{6,4},{5,7},{7,5},{8,10},{10,8},{9,1... | collective-permute-start | bytes 393224 | tf_op jit(solution)/shard_map/ppermute | solution.py:623
  98.1 12.7 %collective-permute-start.9 = (f32[4,64,256]{2,1,0:T(8,128)S(1)}, f32[4,64,256]{2,1,0:T(8,128)S(1)}, u32[]{:S(2)}, u32[]{:S(2)}) collective-permute-start(f32[4,64,256]{2,1,0:T(8,128)S(1)} %get-tuple-element.51), channel_id=1, source_target_pairs={{0,2},{2,0},{1,3},{3,1},{4,6},{6,4},{5,7},{7,5},{8,10},{10,8},{9,1... | collective-permute-start | bytes 786440 | tf_op jit(solution)/shard_map/ppermute | solution.py:623
  98.6 12.2 %collective-permute-start.10 = (f32[4,64,256]{2,1,0:T(8,128)S(1)}, f32[4,64,256]{2,1,0:T(8,128)S(1)}, u32[]{:S(2)}, u32[]{:S(2)}) collective-permute-start(f32[4,64,256]{2,1,0:T(8,128)S(1)} %get-tuple-element.52), channel_id=1, source_target_pairs={{0,2},{2,0},{1,3},{3,1},{4,6},{6,4},{5,7},{7,5},{8,10},{10,8},{9,1... | collective-permute-start | bytes 786440 | tf_op jit(solution)/shard_map/ppermute | solution.py:623
  100.1 3.2 %collective-permute-start.12 = (f32[2,64,256]{2,1,0:T(8,128)S(1)}, f32[2,64,256]{2,1,0:T(8,128)S(1)}, u32[]{:S(2)}, u32[]{:S(2)}) collective-permute-start(f32[2,64,256]{2,1,0:T(8,128)S(1)} %get-tuple-element.53.v_own), channel_id=1, source_target_pairs={{0,1},{1,0},{2,3},{3,2},{4,5},{5,4},{6,7},{7,6},{8,9},{9,8},{10,11... | collective-permute-start | bytes 393224 | tf_op jit(solution)/shard_map/ppermute | solution.py:627
  100.1 4.6 %collective-permute-start.13 = (f32[2,64,256]{2,1,0:T(8,128)S(1)}, f32[2,64,256]{2,1,0:T(8,128)S(1)}, u32[]{:S(2)}, u32[]{:S(2)}) collective-permute-start(f32[2,64,256]{2,1,0:T(8,128)S(1)} %collective-permute-done.11.v_far), channel_id=1, source_target_pairs={{0,1},{1,0},{2,3},{3,2},{4,5},{5,4},{6,7},{7,6},{8,9},{9,8},{10,11... | collective-permute-start | bytes 393224 | tf_op jit(solution)/shard_map/ppermute | solution.py:627
  102.7 9.3 %collective-permute-start.19 = (f32[256,128]{1,0:T(8,128)S(1)}, f32[256,128]{1,0:T(8,128)S(1)}, u32[]{:S(2)}, u32[]{:S(2)}) collective-permute-start(f32[256,128]{1,0:T(8,128)S(1)} %get-tuple-element.61), channel_id=1, source_target_pairs={{0,2},{2,0},{1,3},{3,1},{4,6},{6,4},{5,7},{7,5},{8,10},{10,8},{9,1... | collective-permute-start | bytes 393224 | tf_op jit(solution)/shard_map/ppermute | solution.py:623
  103.3 7.5 %collective-permute-start.20 = (f32[64,128]{1,0:T(8,128)S(1)}, f32[64,128]{1,0:T(8,128)S(1)}, u32[]{:S(2)}, u32[]{:S(2)}) collective-permute-start(f32[64,128]{1,0:T(8,128)S(1)} %get-tuple-element.63), channel_id=1, source_target_pairs={{0,2},{2,0},{1,3},{3,1},{4,6},{6,4},{5,7},{7,5},{8,10},{10,8},{9,1... | collective-permute-start | bytes 98312 | tf_op jit(solution)/shard_map/ppermute | solution.py:623
  104.8 6.0 %collective-permute-start.21 = (f32[64,128]{1,0:T(8,128)S(1)}, f32[64,128]{1,0:T(8,128)S(1)}, u32[]{:S(2)}, u32[]{:S(2)}) collective-permute-start(f32[64,128]{1,0:T(8,128)S(1)} %get-tuple-element.62.cv_own), channel_id=1, source_target_pairs={{0,1},{1,0},{2,3},{3,2},{4,5},{5,4},{6,7},{7,6},{8,9},{9,8},{10,11... | collective-permute-start | bytes 98312 | tf_op jit(solution)/shard_map/ppermute | solution.py:627
  110.8 1.2 %collective-permute-start.22 = (f32[64,128]{1,0:T(8,128)S(1)}, f32[64,128]{1,0:T(8,128)S(1)}, u32[]{:S(2)}, u32[]{:S(2)}) collective-permute-start(f32[64,128]{1,0:T(8,128)S(1)} %collective-permute-done.20.cv_far), channel_id=1, source_target_pairs={{0,1},{1,0},{2,3},{3,2},{4,5},{5,4},{6,7},{7,6},{8,9},{9,8},{10,11... | collective-permute-start | bytes 98312 | tf_op jit(solution)/shard_map/ppermute | solution.py:627
  (11 other events, 92.4 us)

commit v2 on v1

--- a/solution.py
+++ b/solution.py
@@ -101,6 +101,10 @@
     return pl.BlockSpec(memory_space=pl.ANY)
 
 
+def hbm_spec():
+    return pl.BlockSpec(memory_space=pltpu.HBM)
+
+
 def started(pairs, sems):
     copies = [pltpu.make_async_copy(a, b, sems.at[k]) for k, (a, b) in enumerate(pairs)]
     for c in copies:
@@ -113,7 +117,14 @@
         c.wait()
 
 
-def weights_kernel(w1, w2, b1, b2, o1, o2, c1, c2):
+def prepare_kernel(adj, side_code, mirror, place, w1, w2, b1, b2, table, o1, o2, c1, c2, slot_of):
+    total = place.shape[0]
+    for p in range(total):
+        slot_of[place[p]] = p
+    for p in range(total):
+        t = place[p]
+        for s in range(4):
+            table[p * 4 + s] = (slot_of[adj[s, t]] * 4 + side_code[s, t]) * 2 + mirror[s, t]
     x = lax.axis_index("chan")
     chans = w1.shape[1]
     half = chans // 2
@@ -128,34 +139,50 @@
             o[pl.ds(pl.multiple_of(tap * chans + (1 - x) * half, half), half), :] = v[half:]
 
 
-def prepare_weights(w1, b1, w2, b2):
+def prepare(adj, side_code, mirror, place, w1, b1, w2, b2):
     taps, chans, _ = w1.shape
+    total = place.shape[0]
     wide = jax.ShapeDtypeStruct((taps * chans, 2 * chans), BF16)
     return pl.pallas_call(
-        weights_kernel,
-        out_shape=(wide, wide, f32_of(1, chans), f32_of(1, chans)),
-        in_specs=[vmem_spec()] * 4,
-        out_specs=[vmem_spec()] * 4,
+        prepare_kernel,
+        out_shape=(jax.ShapeDtypeStruct((total * 4,), jnp.int32), wide, wide, f32_of(1, chans), f32_of(1, chans)),
+        in_specs=[smem_spec()] * 4 + [vmem_spec()] * 4,
+        out_specs=[smem_spec()] + [vmem_spec()] * 4,
+        scratch_shapes=[SMEM((total,), jnp.int32)],
         compiler_params=LIMIT,
         cost_estimate=cost(0, 4 << 20),
-    )(w1, w2, b1.reshape(1, chans), b2.reshape(1, chans))
-
-
-def inputs_kernel(t, f, edges, send_t, send_f, where, sems):
+    )(adj.T, side_code.T, mirror.T, place, w1, w2, b1.reshape(1, chans), b2.reshape(1, chans))
+
+
+CHUNK = 8
+
+
+def inputs_kernel(t, f, first, second, send_t, send_f, where, away, home, field, sems):
     x = lax.axis_index("chan")
     d = lax.axis_index("dirs")
     where[0] = x
     where[1] = d
     tiles = f.shape[0]
     group = tiles // 2
-    copies = started([(f.at[pl.ds(d * group, group)], send_f), (t.at[1 - x], send_t)], sems)
+    cut = [pl.ds(k * CHUNK, CHUNK) for k in range(tiles // CHUNK)]
+    pairs = [(r, k) for k in cut for r in ((t.at[1 - x], away), (f, field))] + [((t.at[x], home), k) for k in cut]
+    copies = started([(a.at[k], b.at[k]) for (a, b), k in pairs], sems)
     pick = edge_cells(4 * S)
-    pairs = [(t, (x, k), (1 - x, k)) for k in range(tiles)] + [(f, (k,), (k + group,)) for k in range(group)]
-    for k, (r, a, b) in enumerate(pairs):
-        e = dot_rows(pick, below(jnp.concatenate([r[a], r[b]], axis=0)))
+
+    def edges_of(out, k, a, b):
+        e = dot_rows(pick, below(jnp.concatenate([a, b], axis=0)))
         half = e.shape[1] // 2
-        edges[k * 4 * S : (k + 1) * 4 * S, :] = e[:, :half] + e[:, half:]
-    finished(copies)
+        out[k * 4 * S : (k + 1) * 4 * S, :] = e[:, :half] + e[:, half:]
+
+    for k in range(tiles):
+        if k % CHUNK == 0:
+            finished(copies[2 * (k // CHUNK) : 2 * (k // CHUNK) + 2])
+        edges_of(first, k, away[k], field[k])
+    sent = started([(field.at[pl.ds(d * group, group)], send_f), (away, send_t)], sems.at[pl.ds(len(pairs), 2)])
+    finished(copies[2 * len(cut) :])
+    for k in range(group):
+        edges_of(second, k, home[k], home[k + group])
+    finished(sent)
 
 
 def read_inputs(t, f):
@@ -163,48 +190,18 @@
     return pl.pallas_call(
         inputs_kernel,
         out_shape=(
-            f32_of((tiles + tiles // 2) * 4 * S, 2 * half),
+            f32_of(tiles * 4 * S, 2 * half),
+            f32_of(tiles // 2 * 4 * S, 2 * half),
             f32_of(tiles, half, cells),
             f32_of(tiles // 2, half, cells),
             jax.ShapeDtypeStruct((2,), jnp.int32),
         ),
-        in_specs=[vmem_spec()] * 2,
-        out_specs=[vmem_spec(), any_spec(), any_spec(), smem_spec()],
-        scratch_shapes=[pltpu.SemaphoreType.DMA((2,))],
-        compiler_params=LIMIT,
+        in_specs=[hbm_spec()] * 2,
+        out_specs=[vmem_spec(), vmem_spec(), any_spec(), any_spec(), smem_spec()],
+        scratch_shapes=[VMEM((tiles, half, cells), F32)] * 3 + [pltpu.SemaphoreType.DMA((3 * tiles // CHUNK + 2,))],
+        compiler_params=pltpu.CompilerParams(vmem_limit_bytes=60 << 20),
         cost_estimate=cost(0, 3 << 20),
     )(t, f)
-
-
-def table_kernel(packed, place, table, slot_of):
-    def put(p, _):
-        slot_of[place[p]] = p
-        return 0
-
-    total = place.shape[0]
-    lax.fori_loop(0, total, put, 0, unroll=8)
-
-    def look_up(p, _):
-        t = place[p]
-        for s in range(4):
-            v = packed[t, s]
-            table[p * 4 + s] = slot_of[v >> 3] * 8 + (v & 7)
-        return 0
-
-    lax.fori_loop(0, total, look_up, 0, unroll=4)
-
-
-def index_table(packed, place):
-    total = place.shape[0]
-    return pl.pallas_call(
-        table_kernel,
-        out_shape=jax.ShapeDtypeStruct((total * 4,), jnp.int32),
-        in_specs=[smem_spec()] * 2,
-        out_specs=smem_spec(),
-        scratch_shapes=[SMEM((total,), jnp.int32)],
-        compiler_params=LIMIT,
-        cost_estimate=cost(0, 1 << 20),
-    )(packed, place)
 
 
 def planes_of(count, chans):
@@ -374,18 +371,20 @@
 SLOTS = LINE + 2
 
 
+def is_end(z):
+    return jnp.logical_or(z == 0, z == LINE - 1)
+
+
 def came_from(z):
-    end = jnp.logical_or(z == 0, z == LINE - 1)
+    end = is_end(z)
     mirrored, two_on = LINE - 1 - z, (z + 2) % LINE
-    inside = lambda where, other: jnp.where(end, other, where)
-    at_end = lambda where, other: jnp.where(end, where, other)
     return [
         z,
         z ^ 1,
-        inside(mirrored, LINE),
-        at_end(mirrored, LINE),
-        inside(two_on, LINE + 1),
-        at_end(two_on, LINE + 1),
+        jnp.where(end, LINE, mirrored),
+        jnp.where(end, LINE + 1, two_on),
+        jnp.where(end, two_on, LINE),
+        jnp.where(end, mirrored, LINE + 1),
     ]
 
 
@@ -395,34 +394,32 @@
     return where, slot - where * tiles, (v >> 1) & 3, (v & 1) == 1
 
 
+def gather_rims(tiles, table, z, ring, out, packed):
+    group = tiles // 2
+    for m in range(tiles * 4):
+        where, loc, code, mirrored = source(table[z * tiles * 4 + m], tiles)
+        upper = loc // group if packed else 0
+        row = pl.multiple_of(((loc - upper * group) * 4 + code) * S, S)
+        v = ring[where, pl.ds(row, S), :]
+        if packed:
+            v = jnp.where(upper == 1, swap(v), v)
+        out[m * S : (m + 1) * S, :] = jnp.where(mirrored, flip16(v), v)
+
+
 def rims_one_kernel(tiles, table, *refs):
-    parts, (keep, send, ring, sems) = refs[:ARRIVALS], refs[ARRIVALS:]
+    parts, (out, ring, sems) = refs[:ARRIVALS], refs[ARRIVALS:]
     z = lax.axis_index("tiles")
     finished(started([(e, ring.at[w]) for e, w in zip(parts, came_from(z))], sems))
-    base = tiles * 4 * S
-    low = lane_half((S, keep.shape[1]))
-    for m in range(tiles * 4):
-        where, loc, code, mirrored = source(table[z * tiles * 4 + m], tiles)
-        upper = loc // (tiles // 2)
-        t_row = pl.multiple_of((loc * 4 + code) * S, S)
-        v_row = pl.multiple_of(base + ((loc - upper * (tiles // 2)) * 4 + code) * S, S)
-        t = ring[where, pl.ds(t_row, S), :]
-        v = ring[where, pl.ds(v_row, S), :]
-        v = jnp.where(upper == 1, v, swap(v))
-        a = jnp.where(low, t, v)
-        b = jnp.where(low, swap(t), v)
-        keep[m * S : (m + 1) * S, :] = jnp.where(mirrored, flip16(a), a)
-        send[m * S : (m + 1) * S, :] = jnp.where(mirrored, flip16(b), b)
+    gather_rims(tiles, table, z, ring, out, False)
 
 
 def rims_one(table, parts, tiles):
     rows, chans = parts[0].shape
-    out = f32_of(tiles * 4 * S, chans)
     return pl.pallas_call(
         functools.partial(rims_one_kernel, tiles),
-        out_shape=(out, out),
+        out_shape=f32_of(tiles * 4 * S, chans),
         in_specs=[smem_spec()] + [any_spec()] * len(parts),
-        out_specs=[vmem_spec()] * 2,
+        out_specs=vmem_spec(),
         scratch_shapes=[VMEM((SLOTS, rows, chans), F32), pltpu.SemaphoreType.DMA((len(parts),))],
         compiler_params=LIMIT,
         cost_estimate=cost(0, 3 << 20),
@@ -455,23 +452,24 @@
     )
 
 
-def seam_kernel(share, table, edges_v, edges_t, keep, far, w, bias, c_v, c_t, home, near, inner, mirror, outer, got, plain, mirrored, sem):
-    arrival = started([(far, got)], sem)
+def seam_kernel(share, table, *refs):
+    parts, (edges_v, edges_t, sent, far, w, bias, c_v, c_t, home, near, inner, outer, mirror, plain, mirrored, ring, keep, sems) = refs[:ARRIVALS], refs[ARRIVALS:]
     z = lax.axis_index("tiles")
     q = lax.axis_index("chan") * 2 + lax.axis_index("dirs")
     rows = edges_v.shape[0]
     tiles = rows // (4 * S)
+    finished(started([(e, ring.at[k]) for e, k in zip(parts, came_from(z))], sems))
+    gather_rims(tiles, table, z, ring, keep, True)
     run = tiles * S
 
     def side_of(v, side):
         return jnp.concatenate([v[(t * 4 + side) * S : (t * 4 + side + 1) * S, :] for t in range(tiles)], axis=0)
 
-    finished(arrival)
     low = lane_half((run, keep.shape[1]))
     sums = []
     for side in range(4):
-        k, g = side_of(keep, side), side_of(got, side)
-        c = rim_sums(jnp.concatenate([jnp.where(low, swap(k), g), jnp.where(low, k, swap(g))], axis=0), w, side)
+        k, v, g = (side_of(r, side) for r in (keep, sent, far))
+        c = rim_sums(jnp.concatenate([jnp.where(low, swap(v), g), jnp.where(low, k, swap(g))], axis=0), w, side)
         sums.append((c[:run], c[run:]))
     for out, k in ((c_v, 0), (c_t, 1)):
         for side in range(4):
@@ -485,17 +483,16 @@
         for t in range(tiles):
             at = t * 4 + side
             e = tangent[t * S : (t + 1) * S]
-            for msg in (home, near, inner, mirror, outer):
+            for msg in (home, near, inner, outer, mirror):
                 msg[at * S : (at + 1) * S, :] = e
             v = hidden[t * S : (t + 1) * S]
             plain[at] = v
             mirrored[at] = flip16(v)
-    across_two = (z + 2) % LINE
     for zz, places in (
         (z, ((home, rows),)),
         (z ^ 1, ((near, rows),)),
         (LINE - 1 - z, ((inner, rows), (mirror, rows))),
-        (across_two, ((outer, rows), (inner, rows + share * 4 * S))),
+        ((z + 2) % LINE, ((outer, rows), (inner, rows + share * 4 * S))),
     ):
         for m in range(share * 4):
             where, loc, code, flip = source(table[(zz * tiles + q * share) * 4 + m], tiles)
@@ -506,24 +503,25 @@
                 msg[base + m * S : base + (m + 1) * S, :] = v
 
 
-def seam(table, edges_v, edges_t, keep, far, w, bias, share):
+def seam(table, parts, edges_v, edges_t, sent, far, w, bias, share):
     rows, chans = edges_v.shape
     tail = share * 4 * S
     single, double = f32_of(rows + tail, chans), f32_of(rows + 2 * tail, chans)
     outs = pl.pallas_call(
         functools.partial(seam_kernel, share),
         out_shape=(f32_of(rows, chans),) * 2 + (single, single, double, single, single),
-        in_specs=[smem_spec()] + [vmem_spec()] * 3 + [any_spec()] + [vmem_spec()] * 2,
+        in_specs=[smem_spec()] + [any_spec()] * len(parts) + [vmem_spec()] * 6,
         out_specs=[vmem_spec()] * 7,
         scratch_shapes=[
-            VMEM((rows, chans), F32),
             VMEM((rows // S, S, chans), F32),
             VMEM((rows // S, S, chans), F32),
-            pltpu.SemaphoreType.DMA((1,)),
+            VMEM((SLOTS,) + parts[0].shape, F32),
+            VMEM((rows, chans), F32),
+            pltpu.SemaphoreType.DMA((len(parts),)),
         ],
         compiler_params=LIMIT,
         cost_estimate=cost(0, 5 << 20),
-    )(table, edges_v, edges_t, keep, far, w, bias)
+    )(table, *parts, edges_v, edges_t, sent, far, w, bias)
     return outs[0], outs[1], outs[2:]
 
 
@@ -532,7 +530,7 @@
     keep_t, send_t, keep_v, send_v, ring, rims_v, rims, c_t, c_v, sems = refs[ARRIVALS + 1 :]
     z = lax.axis_index("tiles")
     rows, tail = tiles * 4 * S, share * 4 * S
-    bases = [rows] * (ARRIVALS - 1) + [rows + tail]
+    bases = [rows] * 4 + [rows + tail, rows]
     pairs = [(e.at[pl.ds(0, rows)], ring.at[where]) for e, where in zip(parts, came_from(z))]
     pairs += [(e.at[pl.ds(base, tail)], rims_v.at[k]) for k, (e, base) in enumerate(zip(parts, bases))]
     finished(started(pairs, sems))
@@ -631,29 +629,35 @@
     return lax.ppermute(v, "tiles", pairs)
 
 
-def to_all(home, near, inner, mirror, outer):
+def to_all(home, near, inner, outer, mirror=None):
+    outwards = [(2, 3), (1, 0)]
     inner = along(inner, [(1, 2), (2, 1)])
     near = along(near, [(0, 1), (1, 0), (2, 3), (3, 2)])
-    mirror = along(mirror, [(0, 3), (3, 0)])
     outer = along(outer, [(0, 2), (3, 1)])
-    passed = along(inner, [(2, 3), (1, 0)])
-    return [home, near, inner, mirror, outer, passed]
+    passed = along(inner, outwards)
+    if mirror is None:
+        mirror = along(outer, outwards)
+    else:
+        mirror = along(mirror, [(0, 3), (3, 0)])
+    return [home, near, inner, outer, passed, mirror]
 
 
 def split_streams(field, tangents, weight_one, bias_one, weight_two, bias_two, adjacency, side_code, mirror_flag, placement):
     tiles = field.shape[0]
     share = tiles // 4
-    edges, t_send, f_send, where = read_inputs(tangents, field)
-    edges = to_all(*(edges,) * 5)
+    first, second, t_send, f_send, where = read_inputs(tangents, field)
+    first = to_all(*(first,) * 4)
+    second = to_all(*(second,) * 4)
     f_far = across(f_send)
     t_far = across(t_send)
-    table = index_table((adjacency * 4 + side_code) * 2 + mirror_flag, placement)
-    w1, w2, b1, b2 = prepare_weights(weight_one, bias_one, weight_two, bias_two)
-    main_v, edges_v = conv_in(where, field, (f_far, mate(f_far)), w1, share)
-    main_t, edges_t = conv_in(where, tangents, (t_far,), w1, share)
-    keep, send = rims_one(table, edges, tiles)
+    table, w1, w2, b1, b2 = prepare(
+        adjacency, side_code, mirror_flag, placement, weight_one, bias_one, weight_two, bias_two
+    )
+    main_v, edges_v = conv_in(where, field, (f_far, mate(f_far)), w1, 2 * share)
+    main_t, edges_t = conv_in(where, tangents, (t_far,), w1, 2 * share)
+    send = rims_one(table, first, tiles)
     far = across(send)
-    c_v, c_t, messages = seam(table, edges_v, edges_t, keep, far, w1, b1, share)
+    c_v, c_t, messages = seam(table, second, edges_v, edges_t, send, far, w1, b1, share)
     edges = to_all(*messages)
     mains = (where, main_v, main_t, c_v, c_t, w2, b1, b2, share)
     own_a, oth_a = conv_out(*mains, 0, tiles // 2, False)

time: 114 us -> 115 us (level)
  the two profiles are of different devices: /device:TPU:0 before, /device:TPU:17 now
where the time goes in v2:
time: 115 us
  starting transfers between devices  55.8 us (49%)
  waiting for transfers between devices  29.2 us (25%)
  Pallas kernels  27.7 us (24%)
  local copies, waits for them, and re-layouts  1.32 us (1%)
    ppermute x15, starting transfers between devices, along(): return lax.ppermute(v, 'tiles', pairs)  26.2 us
    ppermute x15, waiting for transfers between devices, along(): return lax.ppermute(v, 'tiles', pairs)  23.6 us
    ppermute x5, starting transfers between devices, mate(): return lax.ppermute(v, 'dirs', [(0, 1), (1, 0)])  22.7 us
    pallas_call x2, Pallas kernels, conv_in(): pl.pallas_call(functools.partial(conv_in_kernel, count), out_shape=(f32_o...  8.2 us
    ppermute x8, starting transfers between devices, across(): return lax.ppermute(v, 'chan', [(0, 1), (1, 0)])  6.95 us
    pallas_call x2, Pallas kernels, conv_out(): pl.pallas_call(functools.partial(conv_out_kernel, count, values_too), out...  6.91 us
    ppermute x8, waiting for transfers between devices, across(): return lax.ppermute(v, 'chan', [(0, 1), (1, 0)])  4.78 us
    pallas_call x1, Pallas kernels, seam(): pl.pallas_call(functools.partial(seam_kernel, share), out_shape=(f32_of(r...  3.17 us
  transfers between devices with their start and end apart: 28, of which 8 were waited for; matrix products, arithmetic and copies ran while one was open for 0% of the time, Pallas kernels for 17%

profile of v2, /device:TPU:17, one launch (start us, length us, event | category | flops | bytes accessed | tf_op | source)
XLA Modules:
  0.0 115.1 jit_solution(12854618299943089376)
XLA Ops:
  0.7 3.0 %shard_map.113 = (f32[512,128]{1,0:T(8,128)}, f32[256,128]{1,0:T(8,128)}, f32[8,64,256]{2,1,0:T(8,128)}, f32[4,64,256]{2,1,0:T(8,128)}, s32[2]{0:T(128)}) custom-call(f32[2,8,64,256]{3,2,1,0:T(8,128)} %refs_0_.3, f32[8,64,256]{2,1,0:T(8,128)} %refs_0_.2), custom_call_target="tpu_custom_call" | custom-call | bytes 3145728 | tf_op jit(solution)/shard_map/pallas_call | solution.py:190
  4.9 2.1 %collective-permute-start.9 = (f32[512,128]{1,0:T(8,128)}, f32[512,128]{1,0:T(8,128)S(1)}, u32[]{:S(2)}, u32[]{:S(2)}) collective-permute-start(f32[512,128]{1,0:T(8,128)} %get-tuple-element.43.refs_0_), channel_id=1, source_target_pairs={{4,8},{8,4},{5,9},{9,5},{6,10},{10,6},{7,11},{11,7},{20,24},{24,20... | collective-permute-start | bytes 786440 | tf_op jit(solution)/shard_map/ppermute | solution.py:629
  9.6 3.2 %collective-permute-start.4 = (f32[256,128]{1,0:T(8,128)}, f32[256,128]{1,0:T(8,128)S(1)}, u32[]{:S(2)}, u32[]{:S(2)}) collective-permute-start(f32[256,128]{1,0:T(8,128)} %get-tuple-element.40.refs_0_), channel_id=1, source_target_pairs={{4,8},{8,4},{5,9},{9,5},{6,10},{10,6},{7,11},{11,7},{20,24},{24,20... | collective-permute-start | bytes 393224 | tf_op jit(solution)/shard_map/ppermute | solution.py:629
  12.8 4.0 %collective-permute-done.5.refs_3_ = f32[256,128]{1,0:T(8,128)S(1)} collective-permute-done((f32[256,128]{1,0:T(8,128)}, f32[256,128]{1,0:T(8,128)S(1)}, u32[]{:S(2)}, u32[]{:S(2)}) %collective-permute-start.5) | collective-permute-done | bytes 131104 | tf_op jit(solution)/shard_map/ppermute | solution.py:629
  17.9 8.2 %collective-permute-done.4.refs_2_ = f32[256,128]{1,0:T(8,128)S(1)} collective-permute-done((f32[256,128]{1,0:T(8,128)}, f32[256,128]{1,0:T(8,128)S(1)}, u32[]{:S(2)}, u32[]{:S(2)}) %collective-permute-start.4) | collective-permute-done | bytes 131104 | tf_op jit(solution)/shard_map/ppermute | solution.py:629
  26.1 3.4 %collective-permute-start.12 = (f32[512,128]{1,0:T(8,128)S(1)}, f32[512,128]{1,0:T(8,128)S(1)}, u32[]{:S(2)}, u32[]{:S(2)}) collective-permute-start(f32[512,128]{1,0:T(8,128)S(1)} %collective-permute-done.10.refs_3_), channel_id=1, source_target_pairs={{8,12},{4,0},{9,13},{5,1},{10,14},{6,2},{11,15},{7,3},{24,28},{20,... | collective-permute-start | bytes 786440 | tf_op jit(solution)/shard_map/ppermute | solution.py:629
  29.5 1.3 %collective-permute-start.11 = (f32[512,128]{1,0:T(8,128)S(1)}, f32[512,128]{1,0:T(8,128)S(1)}, u32[]{:S(2)}, u32[]{:S(2)}) collective-permute-start(f32[512,128]{1,0:T(8,128)S(1)} %collective-permute-done.9.refs_2_), channel_id=1, source_target_pairs={{8,12},{4,0},{9,13},{5,1},{10,14},{6,2},{11,15},{7,3},{24,28},{20,... | collective-permute-start | bytes 786440 | tf_op jit(solution)/shard_map/ppermute | solution.py:629
  32.7 2.0 %shard_map.114 = (s32[128]{0:T(128)S(1)}, bf16[1152,256]{1,0:T(8,128)(2,1)S(1)}, bf16[1152,256]{1,0:T(8,128)(2,1)S(1)}, f32[1,128]{1,0:T(1,128)S(1)}, f32[1,128]{1,0:T(1,128)S(1)}) custom-call(s32[4,32]{1,0:T(4,128)S(1)} %bitcast.5, s32[4,32]{1,0:T(4,128)S(1)} %bitcast.6, s32[4,32]{1,0:T(4,128)S(1)} %bitcast.7, s32[32]{0:T(128)S(1)} %copy-done.9, ...), custom_call_target="tpu_custom_call" | custom-call | bytes 4194304 | tf_op jit(solution)/shard_map/pallas_call | solution.py:146
  34.8 2.6 %collective-permute-done.12.refs_5_ = f32[512,128]{1,0:T(8,128)S(1)} collective-permute-done((f32[512,128]{1,0:T(8,128)S(1)}, f32[512,128]{1,0:T(8,128)S(1)}, u32[]{:S(2)}, u32[]{:S(2)}) %collective-permute-start.12) | collective-permute-done | bytes 262176 | tf_op jit(solution)/shard_map/ppermute | solution.py:629
  37.4 4.1 %collective-permute-start.7 = (f32[256,128]{1,0:T(8,128)S(1)}, f32[256,128]{1,0:T(8,128)S(1)}, u32[]{:S(2)}, u32[]{:S(2)}) collective-permute-start(f32[256,128]{1,0:T(8,128)S(1)} %collective-permute-done.5.refs_3_), channel_id=1, source_target_pairs={{8,12},{4,0},{9,13},{5,1},{10,14},{6,2},{11,15},{7,3},{24,28},{20,... | collective-permute-start | bytes 393224 | tf_op jit(solution)/shard_map/ppermute | solution.py:629
  41.5 1.5 %collective-permute-done.11.refs_4_ = f32[512,128]{1,0:T(8,128)S(1)} collective-permute-done((f32[512,128]{1,0:T(8,128)S(1)}, f32[512,128]{1,0:T(8,128)S(1)}, u32[]{:S(2)}, u32[]{:S(2)}) %collective-permute-start.11) | collective-permute-done | bytes 262176 | tf_op jit(solution)/shard_map/ppermute | solution.py:629
  43.0 4.1 %collective-permute-start.6 = (f32[256,128]{1,0:T(8,128)S(1)}, f32[256,128]{1,0:T(8,128)S(1)}, u32[]{:S(2)}, u32[]{:S(2)}) collective-permute-start(f32[256,128]{1,0:T(8,128)S(1)} %collective-permute-done.4.refs_2_), channel_id=1, source_target_pairs={{8,12},{4,0},{9,13},{5,1},{10,14},{6,2},{11,15},{7,3},{24,28},{20,... | collective-permute-start | bytes 393224 | tf_op jit(solution)/shard_map/ppermute | solution.py:629
  50.0 4.1 %shard_map.116 = (f32[8,256,128]{2,1,0:T(8,128)S(1)}, f32[512,128]{1,0:T(8,128)S(1)}) custom-call(s32[2]{0:T(128)S(1)} %copy-done.12, f32[2,8,64,256]{3,2,1,0:T(8,128)S(1)} %copy-done, f32[8,64,256]{2,1,0:T(8,128)S(1)} %collective-permute-done.2.refs_1_, bf16[1152,256]{1,0:T(8,128)(2,1)S(1)} %get-tuple-element.35.refs_3_.refs_2_.refs_10_), custom_call_target="tpu_custom_call" | custom-call | flops 2415919104 | bytes 4194304 | tf_op jit(solution)/shard_map/pallas_call | solution.py:274
  54.2 4.1 %shard_map.115 = (f32[8,256,128]{2,1,0:T(8,128)S(1)}, f32[512,128]{1,0:T(8,128)S(1)}) custom-call(s32[2]{0:T(128)S(1)} %copy-done.12, f32[8,64,256]{2,1,0:T(8,128)S(1)} %copy-done.3, f32[4,64,256]{2,1,0:T(8,128)S(1)} %collective-permute-done.refs_1_, f32[4,64,256]{2,1,0:T(8,128)S(1)} %collective-permute-done.1.refs_2_, ...), custom_call_target="tpu_custom_call" | custom-call | flops 2415919104 | bytes 4194304 | tf_op jit(solution)/shard_map/pallas_call | solution.py:274
  58.3 3.2 %shard_map.118 = (f32[512,128]{1,0:T(8,128)S(1)}, f32[512,128]{1,0:T(8,128)S(1)}, f32[640,128]{1,0:T(8,128)S(1)}, f32[640,128]{1,0:T(8,128)S(1)}, f32[768,128]{1...) custom-call(s32[128]{0:T(128)S(1)} %get-tuple-element.39.table, f32[256,128]{1,0:T(8,128)S(1)} %copy-done.5, ...), custom_call_target="tpu_custom_call" | custom-call | bytes 5242880 | tf_op jit(solution)/shard_map/pallas_call | solution.py:510
  61.5 2.1 %collective-permute-start.20 = (f32[768,128]{1,0:T(8,128)S(1)}, f32[768,128]{1,0:T(8,128)S(1)}, u32[]{:S(2)}, u32[]{:S(2)}) collective-permute-start(f32[768,128]{1,0:T(8,128)S(1)} %get-tuple-element.57), channel_id=1, source_target_pairs={{4,8},{8,4},{5,9},{9,5},{6,10},{10,6},{7,11},{11,7},{20,24},{24,20... | collective-permute-start | bytes 1179656 | tf_op jit(solution)/shard_map/ppermute | solution.py:629
  65.0 7.2 %collective-permute-done.20.refs_2_ = f32[768,128]{1,0:T(8,128)S(1)} collective-permute-done((f32[768,128]{1,0:T(8,128)S(1)}, f32[768,128]{1,0:T(8,128)S(1)}, u32[]{:S(2)}, u32[]{:S(2)}) %collective-permute-start.20) | collective-permute-done | bytes 393248 | tf_op jit(solution)/shard_map/ppermute | solution.py:629
  74.2 4.1 %shard_map.120 = (f32[4,64,256]{2,1,0:T(8,128)S(1)}, f32[4,64,256]{2,1,0:T(8,128)S(1)}, f32[2,64,256]{2,1,0:T(8,128)S(1)}, f32[2,64,256]{2,1,0:T(8,128)S(1)}) custom-call(s32[2]{0:T(128)S(1)} %copy-done.12, f32[8,256,128]{2,1,0:T(8,128)S(1)} %get-tuple-element.36.main_v, f32[8,256,128]{2,1,0:T(8,128)S(1)} %get-tuple-element.38.main_t, ...), custom_call_target="tpu_custom_call" | custom-call | flops 1207959552 | bytes 6291456 | tf_op jit(solution)/shard_map/pallas_call | solution.py:344
  78.6 2.8 %shard_map.119 = (f32[4,64,256]{2,1,0:T(8,128)S(1)}, f32[4,64,256]{2,1,0:T(8,128)S(1)}) custom-call(s32[2]{0:T(128)S(1)} %copy-done.12, f32[8,256,128]{2,1,0:T(8,128)S(1)} %get-tuple-element.36.main_v, f32[8,256,128]{2,1,0:T(8,128)S(1)} %get-tuple-element.38.main_t, f32[512,128]{1,0:T(8,128)S(1)} %get-tuple-element.45.c_v, ...), custom_call_target="tpu_custom_call" | custom-call | flops 1207959552 | bytes 6291456 | tf_op jit(solution)/shard_map/pallas_call | solution.py:344
  83.9 18.2 %collective-permute-start.17 = (f32[2,64,256]{2,1,0:T(8,128)S(1)}, f32[2,64,256]{2,1,0:T(8,128)S(1)}, u32[]{:S(2)}, u32[]{:S(2)}) collective-permute-start(f32[2,64,256]{2,1,0:T(8,128)S(1)} %get-tuple-element.53.v_own), channel_id=1, source_target_pairs={{0,1},{1,0},{2,3},{3,2},{4,5},{5,4},{6,7},{7,6},{8,9},{9,8},{10,11... | collective-permute-start | bytes 393224 | tf_op jit(solution)/shard_map/ppermute | solution.py:625
  102.2 2.0 %shard_map.121 = (f32[256,128]{1,0:T(8,128)S(1)}, f32[256,128]{1,0:T(8,128)S(1)}, f32[64,128]{1,0:T(8,128)S(1)}, f32[64,128]{1,0:T(8,128)S(1)}) custom-call(s32[128]{0:T(128)S(1)} %get-tuple-element.39.table, f32[640,128]{1,0:T(8,128)S(1)} %get-tuple-element.55.refs_0_, f32[640,128]{1,0:T(8,128)S(1)} %collective-permute-done.19.refs_1_, ...), custom_call_target="tpu_custom_call" | custom-call | bytes 4194304 | tf_op jit(solution)/shard_map/pallas_call | solution.py:561
  106.8 3.7 %collective-permute-done.25.cv_far = f32[64,128]{1,0:T(8,128)S(1)} collective-permute-done((f32[64,128]{1,0:T(8,128)S(1)}, f32[64,128]{1,0:T(8,128)S(1)}, u32[]{:S(2)}, u32[]{:S(2)}) %collective-permute-start.25) | collective-permute-done | bytes 32800 | tf_op jit(solution)/shard_map/ppermute | solution.py:621
  110.5 2.3 %collective-permute-start.27 = (f32[64,128]{1,0:T(8,128)S(1)}, f32[64,128]{1,0:T(8,128)S(1)}, u32[]{:S(2)}, u32[]{:S(2)}) collective-permute-start(f32[64,128]{1,0:T(8,128)S(1)} %collective-permute-done.25.cv_far), channel_id=1, source_target_pairs={{0,1},{1,0},{2,3},{3,2},{4,5},{5,4},{6,7},{7,6},{8,9},{9,8},{10,11... | collective-permute-start | bytes 98312 | tf_op jit(solution)/shard_map/ppermute | solution.py:625
  113.6 1.5 %shard_map.122 = (f32[8,64,256]{2,1,0:T(8,128)}, f32[2,8,64,256]{3,2,1,0:T(8,128)}) custom-call(f32[4,64,256]{2,1,0:T(8,128)S(1)} %get-tuple-element.49.own_a, f32[4,64,256]{2,1,0:T(8,128)S(1)} %get-tuple-element.50.own_b, f32[4,64,256]{2,1,0:T(8,128)S(1)} %collective-permute-done.14.far_a, f32[4,64,256]{2,1,0:T(8,128)S(1)} %collective-permute-done.15.far_b, ...), custom_call_target="tpu_custom_call" | custom-call | bytes 6291456 | tf_op jit(solution)/shard_map/pallas_call | solution.py:610
  (68 shorter events, 19.4 us)
Async XLA Ops:
  3.6 22.5 %collective-permute-start.10 = (f32[512,128]{1,0:T(8,128)}, f32[512,128]{1,0:T(8,128)S(1)}, u32[]{:S(2)}, u32[]{:S(2)}) collective-permute-start(f32[512,128]{1,0:T(8,128)} %get-tuple-element.43.refs_0_), channel_id=1, source_target_pairs={{0,8},{12,4},{1,9},{13,5},{2,10},{14,6},{3,11},{15,7},{16,24},{28,... | collective-permute-start | bytes 786440 | tf_op jit(solution)/shard_map/ppermute | solution.py:629
  4.9 24.6 %collective-permute-start.9 = (f32[512,128]{1,0:T(8,128)}, f32[512,128]{1,0:T(8,128)S(1)}, u32[]{:S(2)}, u32[]{:S(2)}) collective-permute-start(f32[512,128]{1,0:T(8,128)} %get-tuple-element.43.refs_0_), channel_id=1, source_target_pairs={{4,8},{8,4},{5,9},{9,5},{6,10},{10,6},{7,11},{11,7},{20,24},{24,20... | collective-permute-start | bytes 786440 | tf_op jit(solution)/shard_map/ppermute | solution.py:629
  7.0 41.1 %collective-permute-start.2 = (f32[8,64,256]{2,1,0:T(8,128)}, f32[8,64,256]{2,1,0:T(8,128)S(1)}, u32[]{:S(2)}, u32[]{:S(2)}) collective-permute-start(f32[8,64,256]{2,1,0:T(8,128)} %get-tuple-element.37), channel_id=1, source_target_pairs={{0,2},{2,0},{1,3},{3,1},{4,6},{6,4},{5,7},{7,5},{8,10},{10,8},{9,1... | collective-permute-start | bytes 1572872 | tf_op jit(solution)/shard_map/ppermute | solution.py:621
  8.3 8.5 %collective-permute-start.5 = (f32[256,128]{1,0:T(8,128)}, f32[256,128]{1,0:T(8,128)S(1)}, u32[]{:S(2)}, u32[]{:S(2)}) collective-permute-start(f32[256,128]{1,0:T(8,128)} %get-tuple-element.40.refs_0_), channel_id=1, source_target_pairs={{0,8},{12,4},{1,9},{13,5},{2,10},{14,6},{3,11},{15,7},{16,24},{28,... | collective-permute-start | bytes 393224 | tf_op jit(solution)/shard_map/ppermute | solution.py:629
  9.6 16.5 %collective-permute-start.4 = (f32[256,128]{1,0:T(8,128)}, f32[256,128]{1,0:T(8,128)S(1)}, u32[]{:S(2)}, u32[]{:S(2)}) collective-permute-start(f32[256,128]{1,0:T(8,128)} %get-tuple-element.40.refs_0_), channel_id=1, source_target_pairs={{4,8},{8,4},{5,9},{9,5},{6,10},{10,6},{7,11},{11,7},{20,24},{24,20... | collective-permute-start | bytes 393224 | tf_op jit(solution)/shard_map/ppermute | solution.py:629
  16.8 14.0 %collective-permute-start = (f32[4,64,256]{2,1,0:T(8,128)}, f32[4,64,256]{2,1,0:T(8,128)S(1)}, u32[]{:S(2)}, u32[]{:S(2)}) collective-permute-start(f32[4,64,256]{2,1,0:T(8,128)} %get-tuple-element.34), channel_id=1, source_target_pairs={{0,2},{2,0},{1,3},{3,1},{4,6},{6,4},{5,7},{7,5},{8,10},{10,8},{9,1... | collective-permute-start | bytes 786440 | tf_op jit(solution)/shard_map/ppermute | solution.py:621
  26.1 8.6 %collective-permute-start.8 = (f32[512,128]{1,0:T(8,128)}, f32[512,128]{1,0:T(8,128)S(1)}, u32[]{:S(2)}, u32[]{:S(2)}) collective-permute-start(f32[512,128]{1,0:T(8,128)} %get-tuple-element.43.refs_0_), channel_id=1, source_target_pairs={{0,4},{4,0},{8,12},{12,8},{1,5},{5,1},{9,13},{13,9},{2,6},{6,2},{1... | collective-permute-start | bytes 786440 | tf_op jit(solution)/shard_map/ppermute | solution.py:629
  26.1 11.3 %collective-permute-start.12 = (f32[512,128]{1,0:T(8,128)S(1)}, f32[512,128]{1,0:T(8,128)S(1)}, u32[]{:S(2)}, u32[]{:S(2)}) collective-permute-start(f32[512,128]{1,0:T(8,128)S(1)} %collective-permute-done.10.refs_3_), channel_id=1, source_target_pairs={{8,12},{4,0},{9,13},{5,1},{10,14},{6,2},{11,15},{7,3},{24,28},{20,... | collective-permute-start | bytes 786440 | tf_op jit(solution)/shard_map/ppermute | solution.py:629
  29.5 13.5 %collective-permute-start.11 = (f32[512,128]{1,0:T(8,128)S(1)}, f32[512,128]{1,0:T(8,128)S(1)}, u32[]{:S(2)}, u32[]{:S(2)}) collective-permute-start(f32[512,128]{1,0:T(8,128)S(1)} %collective-permute-done.9.refs_2_), channel_id=1, source_target_pairs={{8,12},{4,0},{9,13},{5,1},{10,14},{6,2},{11,15},{7,3},{24,28},{20,... | collective-permute-start | bytes 786440 | tf_op jit(solution)/shard_map/ppermute | solution.py:629
  30.8 23.3 %collective-permute-start.1 = (f32[4,64,256]{2,1,0:T(8,128)S(1)}, f32[4,64,256]{2,1,0:T(8,128)S(1)}, u32[]{:S(2)}, u32[]{:S(2)}) collective-permute-start(f32[4,64,256]{2,1,0:T(8,128)S(1)} %collective-permute-done.refs_1_), channel_id=1, source_target_pairs={{0,1},{1,0},{2,3},{3,2},{4,5},{5,4},{6,7},{7,6},{8,9},{9,8},{10,11... | collective-permute-start | bytes 786440 | tf_op jit(solution)/shard_map/ppermute | solution.py:625
  34.7 23.6 %collective-permute-start.3 = (f32[256,128]{1,0:T(8,128)S(1)}, f32[256,128]{1,0:T(8,128)S(1)}, u32[]{:S(2)}, u32[]{:S(2)}) collective-permute-start(f32[256,128]{1,0:T(8,128)S(1)} %copy-done.5), channel_id=1, source_target_pairs={{0,4},{4,0},{8,12},{12,8},{1,5},{5,1},{9,13},{13,9},{2,6},{6,2},{1... | collective-permute-start | bytes 393224 | tf_op jit(solution)/shard_map/ppermute | solution.py:629
  37.4 20.9 %collective-permute-start.7 = (f32[256,128]{1,0:T(8,128)S(1)}, f32[256,128]{1,0:T(8,128)S(1)}, u32[]{:S(2)}, u32[]{:S(2)}) collective-permute-start(f32[256,128]{1,0:T(8,128)S(1)} %collective-permute-done.5.refs_3_), channel_id=1, source_target_pairs={{8,12},{4,0},{9,13},{5,1},{10,14},{6,2},{11,15},{7,3},{24,28},{20,... | collective-permute-start | bytes 393224 | tf_op jit(solution)/shard_map/ppermute | solution.py:629
  43.0 15.3 %collective-permute-start.6 = (f32[256,128]{1,0:T(8,128)S(1)}, f32[256,128]{1,0:T(8,128)S(1)}, u32[]{:S(2)}, u32[]{:S(2)}) collective-permute-start(f32[256,128]{1,0:T(8,128)S(1)} %collective-permute-done.4.refs_2_), channel_id=1, source_target_pairs={{8,12},{4,0},{9,13},{5,1},{10,14},{6,2},{11,15},{7,3},{24,28},{20,... | collective-permute-start | bytes 393224 | tf_op jit(solution)/shard_map/ppermute | solution.py:629
  48.1 10.2 %collective-permute-start.13 = (f32[512,128]{1,0:T(8,128)S(1)}, f32[512,128]{1,0:T(8,128)S(1)}, u32[]{:S(2)}, u32[]{:S(2)}) collective-permute-start(f32[512,128]{1,0:T(8,128)S(1)} %shard_map.117.refs_8_), channel_id=1, source_target_pairs={{0,2},{2,0},{1,3},{3,1},{4,6},{6,4},{5,7},{7,5},{8,10},{10,8},{9,1... | collective-permute-start | bytes 786440 | tf_op jit(solution)/shard_map/ppermute | solution.py:621
  61.5 10.7 %collective-permute-start.20 = (f32[768,128]{1,0:T(8,128)S(1)}, f32[768,128]{1,0:T(8,128)S(1)}, u32[]{:S(2)}, u32[]{:S(2)}) collective-permute-start(f32[768,128]{1,0:T(8,128)S(1)} %get-tuple-element.57), channel_id=1, source_target_pairs={{4,8},{8,4},{5,9},{9,5},{6,10},{10,6},{7,11},{11,7},{20,24},{24,20... | collective-permute-start | bytes 1179656 | tf_op jit(solution)/shard_map/ppermute | solution.py:629
  63.6 19.1 %collective-permute-start.19 = (f32[640,128]{1,0:T(8,128)S(1)}, f32[640,128]{1,0:T(8,128)S(1)}, u32[]{:S(2)}, u32[]{:S(2)}) collective-permute-start(f32[640,128]{1,0:T(8,128)S(1)} %get-tuple-element.56), channel_id=1, source_target_pairs={{0,4},{4,0},{8,12},{12,8},{1,5},{5,1},{9,13},{13,9},{2,6},{6,2},{1... | collective-permute-start | bytes 983048 | tf_op jit(solution)/shard_map/ppermute | solution.py:629
  63.7 20.3 %collective-permute-start.21 = (f32[640,128]{1,0:T(8,128)S(1)}, f32[640,128]{1,0:T(8,128)S(1)}, u32[]{:S(2)}, u32[]{:S(2)}) collective-permute-start(f32[640,128]{1,0:T(8,128)S(1)} %get-tuple-element.58), channel_id=1, source_target_pairs={{0,8},{12,4},{1,9},{13,5},{2,10},{14,6},{3,11},{15,7},{16,24},{28,... | collective-permute-start | bytes 983048 | tf_op jit(solution)/shard_map/ppermute | solution.py:629
  72.2 30.0 %collective-permute-start.22 = (f32[768,128]{1,0:T(8,128)S(1)}, f32[768,128]{1,0:T(8,128)S(1)}, u32[]{:S(2)}, u32[]{:S(2)}) collective-permute-start(f32[768,128]{1,0:T(8,128)S(1)} %collective-permute-done.20.refs_2_), channel_id=1, source_target_pairs={{8,12},{4,0},{9,13},{5,1},{10,14},{6,2},{11,15},{7,3},{24,28},{20,... | collective-permute-start | bytes 1179656 | tf_op jit(solution)/shard_map/ppermute | solution.py:629
  73.5 28.6 %collective-permute-start.23 = (f32[640,128]{1,0:T(8,128)S(1)}, f32[640,128]{1,0:T(8,128)S(1)}, u32[]{:S(2)}, u32[]{:S(2)}) collective-permute-start(f32[640,128]{1,0:T(8,128)S(1)} %get-tuple-element.59), channel_id=1, source_target_pairs={{0,12},{12,0},{1,13},{13,1},{2,14},{14,2},{3,15},{15,3},{16,28},{2... | collective-permute-start | bytes 983048 | tf_op jit(solution)/shard_map/ppermute | solution.py:629
  82.4 30.3 %collective-permute-start.14 = (f32[4,64,256]{2,1,0:T(8,128)S(1)}, f32[4,64,256]{2,1,0:T(8,128)S(1)}, u32[]{:S(2)}, u32[]{:S(2)}) collective-permute-start(f32[4,64,256]{2,1,0:T(8,128)S(1)} %get-tuple-element.51), channel_id=1, source_target_pairs={{0,2},{2,0},{1,3},{3,1},{4,6},{6,4},{5,7},{7,5},{8,10},{10,8},{9,1... | collective-permute-start | bytes 786440 | tf_op jit(solution)/shard_map/ppermute | solution.py:621
  82.7 30.1 %collective-permute-start.15 = (f32[4,64,256]{2,1,0:T(8,128)S(1)}, f32[4,64,256]{2,1,0:T(8,128)S(1)}, u32[]{:S(2)}, u32[]{:S(2)}) collective-permute-start(f32[4,64,256]{2,1,0:T(8,128)S(1)} %get-tuple-element.52), channel_id=1, source_target_pairs={{0,2},{2,0},{1,3},{3,1},{4,6},{6,4},{5,7},{7,5},{8,10},{10,8},{9,1... | collective-permute-start | bytes 786440 | tf_op jit(solution)/shard_map/ppermute | solution.py:621
  83.9 20.6 %collective-permute-start.17 = (f32[2,64,256]{2,1,0:T(8,128)S(1)}, f32[2,64,256]{2,1,0:T(8,128)S(1)}, u32[]{:S(2)}, u32[]{:S(2)}) collective-permute-start(f32[2,64,256]{2,1,0:T(8,128)S(1)} %get-tuple-element.53.v_own), channel_id=1, source_target_pairs={{0,1},{1,0},{2,3},{3,2},{4,5},{5,4},{6,7},{7,6},{8,9},{9,8},{10,11... | collective-permute-start | bytes 393224 | tf_op jit(solution)/shard_map/ppermute | solution.py:625
  104.2 9.4 %collective-permute-start.24 = (f32[256,128]{1,0:T(8,128)S(1)}, f32[256,128]{1,0:T(8,128)S(1)}, u32[]{:S(2)}, u32[]{:S(2)}) collective-permute-start(f32[256,128]{1,0:T(8,128)S(1)} %get-tuple-element.61), channel_id=1, source_target_pairs={{0,2},{2,0},{1,3},{3,1},{4,6},{6,4},{5,7},{7,5},{8,10},{10,8},{9,1... | collective-permute-start | bytes 393224 | tf_op jit(solution)/shard_map/ppermute | solution.py:621
  105.8 7.0 %collective-permute-start.26 = (f32[64,128]{1,0:T(8,128)S(1)}, f32[64,128]{1,0:T(8,128)S(1)}, u32[]{:S(2)}, u32[]{:S(2)}) collective-permute-start(f32[64,128]{1,0:T(8,128)S(1)} %get-tuple-element.62.cv_own), channel_id=1, source_target_pairs={{0,1},{1,0},{2,3},{3,2},{4,5},{5,4},{6,7},{7,6},{8,9},{9,8},{10,11... | collective-permute-start | bytes 98312 | tf_op jit(solution)/shard_map/ppermute | solution.py:625
  (17 other events, 150.4 us)

commit v3 on v2

--- a/solution.py
+++ b/solution.py
@@ -410,7 +410,7 @@
     parts, (out, ring, sems) = refs[:ARRIVALS], refs[ARRIVALS:]
     z = lax.axis_index("tiles")
     finished(started([(e, ring.at[w]) for e, w in zip(parts, came_from(z))], sems))
-    gather_rims(tiles, table, z, ring, out, False)
+    gather_rims(tiles, table, z, ring, out, ring.shape[1] < out.shape[0])
 
 
 def rims_one(table, parts, tiles):
@@ -452,14 +452,11 @@
     )
 
 
-def seam_kernel(share, table, *refs):
-    parts, (edges_v, edges_t, sent, far, w, bias, c_v, c_t, home, near, inner, outer, mirror, plain, mirrored, ring, keep, sems) = refs[:ARRIVALS], refs[ARRIVALS:]
+def seam_kernel(share, table, edges_v, edges_t, keep, sent, far, w, bias, c_v, c_t, home, near, inner, outer, mirror, plain, mirrored):
     z = lax.axis_index("tiles")
     q = lax.axis_index("chan") * 2 + lax.axis_index("dirs")
     rows = edges_v.shape[0]
     tiles = rows // (4 * S)
-    finished(started([(e, ring.at[k]) for e, k in zip(parts, came_from(z))], sems))
-    gather_rims(tiles, table, z, ring, keep, True)
     run = tiles * S
 
     def side_of(v, side):
@@ -503,25 +500,22 @@
                 msg[base + m * S : base + (m + 1) * S, :] = v
 
 
-def seam(table, parts, edges_v, edges_t, sent, far, w, bias, share):
+def seam(table, edges_v, edges_t, keep, sent, far, w, bias, share):
     rows, chans = edges_v.shape
     tail = share * 4 * S
     single, double = f32_of(rows + tail, chans), f32_of(rows + 2 * tail, chans)
     outs = pl.pallas_call(
         functools.partial(seam_kernel, share),
         out_shape=(f32_of(rows, chans),) * 2 + (single, single, double, single, single),
-        in_specs=[smem_spec()] + [any_spec()] * len(parts) + [vmem_spec()] * 6,
+        in_specs=[smem_spec()] + [vmem_spec()] * 7,
         out_specs=[vmem_spec()] * 7,
         scratch_shapes=[
             VMEM((rows // S, S, chans), F32),
             VMEM((rows // S, S, chans), F32),
-            VMEM((SLOTS,) + parts[0].shape, F32),
-            VMEM((rows, chans), F32),
-            pltpu.SemaphoreType.DMA((len(parts),)),
         ],
         compiler_params=LIMIT,
         cost_estimate=cost(0, 5 << 20),
-    )(table, *parts, edges_v, edges_t, sent, far, w, bias)
+    )(table, edges_v, edges_t, keep, sent, far, w, bias)
     return outs[0], outs[1], outs[2:]
 
 
@@ -625,6 +619,10 @@
     return lax.ppermute(v, "dirs", [(0, 1), (1, 0)])
 
 
+def diagonal(v):
+    return lax.ppermute(v, ("chan", "dirs"), [(0, 3), (1, 2), (2, 1), (3, 0)])
+
+
 def along(v, pairs):
     return lax.ppermute(v, "tiles", pairs)
 
@@ -656,19 +654,20 @@
     main_v, edges_v = conv_in(where, field, (f_far, mate(f_far)), w1, 2 * share)
     main_t, edges_t = conv_in(where, tangents, (t_far,), w1, 2 * share)
     send = rims_one(table, first, tiles)
+    keep = rims_one(table, second, tiles)
     far = across(send)
-    c_v, c_t, messages = seam(table, second, edges_v, edges_t, send, far, w1, b1, share)
+    c_v, c_t, messages = seam(table, edges_v, edges_t, keep, send, far, w1, b1, share)
     edges = to_all(*messages)
     mains = (where, main_v, main_t, c_v, c_t, w2, b1, b2, share)
     own_a, oth_a = conv_out(*mains, 0, tiles // 2, False)
     own_b, oth_b, v_own, v_oth = conv_out(*mains, tiles // 2, tiles, True)
     far_a, far_b, v_far = across(oth_a), across(oth_b), across(v_oth)
-    v_mate, v_diag = mate(v_own), mate(v_far)
+    v_mate, v_diag = mate(v_own), diagonal(v_oth)
     c_own, c_send, cv_own, cv_send = rims_two(table, edges, w2, tiles, share)
     cv_mate = mate(cv_own)
     cv_far = across(cv_send)
     c_far = across(c_send)
-    cv_diag = mate(cv_far)
+    cv_diag = diagonal(cv_send)
     arrays = (own_a, own_b, far_a, far_b, v_own, v_far, v_mate, v_diag, c_own, c_far, cv_own, cv_far, cv_mate, cv_diag)
     return finish(tiles, *arrays)
 

time: 115 us -> 109 us (0.948)
  waiting for transfers between devices: 29.2 us -> 23.7 us
  starting transfers between devices: 55.8 us -> 54.5 us
    ppermute x15, waiting for transfers between devices: 23.6 us -> 14.2 us  [along(): return lax.ppermute(v, 'tiles', pairs)]
    ppermute x0 -> x2, waiting for transfers between devices: none -> 6.53 us  [diagonal(): return lax.ppermute(v, ('chan', 'dirs'), [(0, 3), (1, 2), (2, 1), (3, 0)])]
    ppermute x15, starting transfers between devices: 26.2 us -> 22.7 us  [along(): return lax.ppermute(v, 'tiles', pairs)]
    ppermute x0 -> x2, starting transfers between devices: none -> 3.49 us  [diagonal(): return lax.ppermute(v, ('chan', 'dirs'), [(0, 3), (1, 2), (2, 1), (3, 0)])]
    pallas_call x1 -> x2, Pallas kernels: 0.99 us -> 3.14 us  [rims_one(): pl.pallas_call(functools.partial(rims_one_kernel, tiles), out_shape=f32_o...]
    ppermute x5 -> x3, starting transfers between devices: 22.7 us -> 20.8 us  [mate(): return lax.ppermute(v, 'dirs', [(0, 1), (1, 0)])]
    ppermute x8, waiting for transfers between devices: 4.78 us -> 3.02 us  [across(): return lax.ppermute(v, 'chan', [(0, 1), (1, 0)])]
    pallas_call x1, Pallas kernels: 3.17 us -> 1.8 us  [seam(): pl.pallas_call(functools.partial(seam_kernel, share), out_shape=(f32_of(r...]
  transfers between devices with their start and end apart: 28 -> 28, of which waited for: 8 -> 9; matrix products, arithmetic and copies ran while one was open for 0% -> 0% of each run, Pallas kernels for 17% -> 20%
where the time goes in v3:
time: 109 us
  starting transfers between devices  54.5 us (50%)
  Pallas kernels  28.4 us (26%)
  waiting for transfers between devices  23.7 us (22%)
  local copies, waits for them, and re-layouts  1.32 us (1%)
    ppermute x15, starting transfers between devices, along(): return lax.ppermute(v, 'tiles', pairs)  22.7 us
    ppermute x3, starting transfers between devices, mate(): return lax.ppermute(v, 'dirs', [(0, 1), (1, 0)])  20.8 us
    ppermute x15, waiting for transfers between devices, along(): return lax.ppermute(v, 'tiles', pairs)  14.2 us
    pallas_call x2, Pallas kernels, conv_in(): pl.pallas_call(functools.partial(conv_in_kernel, count), out_shape=(f32_o...  8.17 us
    ppermute x8, starting transfers between devices, across(): return lax.ppermute(v, 'chan', [(0, 1), (1, 0)])  7.48 us
    pallas_call x2, Pallas kernels, conv_out(): pl.pallas_call(functools.partial(conv_out_kernel, count, values_too), out...  6.9 us
    ppermute x2, waiting for transfers between devices, diagonal(): return lax.ppermute(v, ('chan', 'dirs'), [(0, 3), (1, 2), (2, 1), (3, 0)])  6.53 us
    ppermute x2, starting transfers between devices, diagonal(): return lax.ppermute(v, ('chan', 'dirs'), [(0, 3), (1, 2), (2, 1), (3, 0)])  3.49 us
  transfers between devices with their start and end apart: 28, of which 9 were waited for; matrix products, arithmetic and copies ran while one was open for 0% of the time, Pallas kernels for 20%

profile of v3, /device:TPU:17, one launch (start us, length us, event | category | flops | bytes accessed | tf_op | source)
XLA Modules:
  0.0 109.0 jit_solution(11121220221303734552)
XLA Ops:
  0.7 3.0 %shard_map.113 = (f32[512,128]{1,0:T(8,128)}, f32[256,128]{1,0:T(8,128)}, f32[8,64,256]{2,1,0:T(8,128)}, f32[4,64,256]{2,1,0:T(8,128)}, s32[2]{0:T(128)}) custom-call(f32[2,8,64,256]{3,2,1,0:T(8,128)} %refs_0_.3, f32[8,64,256]{2,1,0:T(8,128)} %refs_0_.2), custom_call_target="tpu_custom_call" | custom-call | bytes 3145728 | tf_op jit(solution)/shard_map/pallas_call | solution.py:190
  4.9 2.1 %collective-permute-start.4 = (f32[256,128]{1,0:T(8,128)}, f32[256,128]{1,0:T(8,128)S(1)}, u32[]{:S(2)}, u32[]{:S(2)}) collective-permute-start(f32[256,128]{1,0:T(8,128)} %get-tuple-element.42.refs_0_), channel_id=1, source_target_pairs={{4,8},{8,4},{5,9},{9,5},{6,10},{10,6},{7,11},{11,7},{20,24},{24,20... | collective-permute-start | bytes 393224 | tf_op jit(solution)/shard_map/ppermute | solution.py:627
  8.9 3.2 %collective-permute-start.9 = (f32[512,128]{1,0:T(8,128)}, f32[512,128]{1,0:T(8,128)S(1)}, u32[]{:S(2)}, u32[]{:S(2)}) collective-permute-start(f32[512,128]{1,0:T(8,128)} %get-tuple-element.43.refs_0_), channel_id=1, source_target_pairs={{4,8},{8,4},{5,9},{9,5},{6,10},{10,6},{7,11},{11,7},{20,24},{24,20... | collective-permute-start | bytes 786440 | tf_op jit(solution)/shard_map/ppermute | solution.py:627
  13.4 2.5 %collective-permute-done.4.refs_2_ = f32[256,128]{1,0:T(8,128)S(1)} collective-permute-done((f32[256,128]{1,0:T(8,128)}, f32[256,128]{1,0:T(8,128)S(1)}, u32[]{:S(2)}, u32[]{:S(2)}) %collective-permute-start.4) | collective-permute-done | bytes 131104 | tf_op jit(solution)/shard_map/ppermute | solution.py:627
  22.3 2.2 %collective-permute-start.8 = (f32[512,128]{1,0:T(8,128)}, f32[512,128]{1,0:T(8,128)S(1)}, u32[]{:S(2)}, u32[]{:S(2)}) collective-permute-start(f32[512,128]{1,0:T(8,128)} %get-tuple-element.43.refs_0_), channel_id=1, source_target_pairs={{0,4},{4,0},{8,12},{12,8},{1,5},{5,1},{9,13},{13,9},{2,6},{6,2},{1... | collective-permute-start | bytes 786440 | tf_op jit(solution)/shard_map/ppermute | solution.py:627
  24.5 1.9 %collective-permute-start.12 = (f32[512,128]{1,0:T(8,128)S(1)}, f32[512,128]{1,0:T(8,128)S(1)}, u32[]{:S(2)}, u32[]{:S(2)}) collective-permute-start(f32[512,128]{1,0:T(8,128)S(1)} %collective-permute-done.10.refs_3_), channel_id=1, source_target_pairs={{8,12},{4,0},{9,13},{5,1},{10,14},{6,2},{11,15},{7,3},{24,28},{20,... | collective-permute-start | bytes 786440 | tf_op jit(solution)/shard_map/ppermute | solution.py:627
  27.7 2.3 %collective-permute-done.refs_1_ = f32[4,64,256]{2,1,0:T(8,128)S(1)} collective-permute-done((f32[4,64,256]{2,1,0:T(8,128)}, f32[4,64,256]{2,1,0:T(8,128)S(1)}, u32[]{:S(2)}, u32[]{:S(2)}) %collective-permute-start) | collective-permute-done | bytes 262176 | tf_op jit(solution)/shard_map/ppermute | solution.py:615
  30.0 2.4 %collective-permute-start.1 = (f32[4,64,256]{2,1,0:T(8,128)S(1)}, f32[4,64,256]{2,1,0:T(8,128)S(1)}, u32[]{:S(2)}, u32[]{:S(2)}) collective-permute-start(f32[4,64,256]{2,1,0:T(8,128)S(1)} %collective-permute-done.refs_1_), channel_id=1, source_target_pairs={{0,1},{1,0},{2,3},{3,2},{4,5},{5,4},{6,7},{7,6},{8,9},{9,8},{10,11... | collective-permute-start | bytes 786440 | tf_op jit(solution)/shard_map/ppermute | solution.py:619
  33.1 2.0 %shard_map.114 = (s32[128]{0:T(128)S(1)}, bf16[1152,256]{1,0:T(8,128)(2,1)S(1)}, bf16[1152,256]{1,0:T(8,128)(2,1)S(1)}, f32[1,128]{1,0:T(1,128)S(1)}, f32[1,128]{1,0:T(1,128)S(1)}) custom-call(s32[4,32]{1,0:T(4,128)S(1)} %bitcast.5, s32[4,32]{1,0:T(4,128)S(1)} %bitcast.6, s32[4,32]{1,0:T(4,128)S(1)} %bitcast.7, s32[32]{0:T(128)S(1)} %copy-done.9, ...), custom_call_target="tpu_custom_call" | custom-call | bytes 4194304 | tf_op jit(solution)/shard_map/pallas_call | solution.py:146
  35.1 2.1 %shard_map.117.keep = f32[512,128]{1,0:T(8,128)S(1)} custom-call(s32[128]{0:T(128)S(1)} %get-tuple-element.39.table, f32[256,128]{1,0:T(8,128)S(1)} %copy-done.5, f32[256,128]{1,0:T(8,128)S(1)} %collective-permute-done.3.refs_1_, f32[256,128]{1,0:T(8,128)S(1)} %collective-permute-done.4.refs_2_, f32[256,128]{1,0:T(8,128)S(1)} %collective-permute-done.5.refs_3_, ...), custom_call_target="tpu_custom_call" | custom-call | bytes 3145728 | tf_op jit(solution)/shard_map/pallas_call | solution.py:418
  37.3 2.9 %collective-permute-done.11.refs_4_ = f32[512,128]{1,0:T(8,128)S(1)} collective-permute-done((f32[512,128]{1,0:T(8,128)S(1)}, f32[512,128]{1,0:T(8,128)S(1)}, u32[]{:S(2)}, u32[]{:S(2)}) %collective-permute-start.11) | collective-permute-done | bytes 262176 | tf_op jit(solution)/shard_map/ppermute | solution.py:627
  43.4 4.1 %shard_map.116 = (f32[8,256,128]{2,1,0:T(8,128)S(1)}, f32[512,128]{1,0:T(8,128)S(1)}) custom-call(s32[2]{0:T(128)S(1)} %copy-done.12, f32[2,8,64,256]{3,2,1,0:T(8,128)S(1)} %copy-done, f32[8,64,256]{2,1,0:T(8,128)S(1)} %collective-permute-done.2.refs_1_, bf16[1152,256]{1,0:T(8,128)(2,1)S(1)} %get-tuple-element.35.refs_3_.refs_2_.w), custom_call_target="tpu_custom_call" | custom-call | flops 2415919104 | bytes 4194304 | tf_op jit(solution)/shard_map/pallas_call | solution.py:274
  47.5 4.1 %shard_map.115 = (f32[8,256,128]{2,1,0:T(8,128)S(1)}, f32[512,128]{1,0:T(8,128)S(1)}) custom-call(s32[2]{0:T(128)S(1)} %copy-done.12, f32[8,64,256]{2,1,0:T(8,128)S(1)} %copy-done.3, f32[4,64,256]{2,1,0:T(8,128)S(1)} %collective-permute-done.refs_1_, f32[4,64,256]{2,1,0:T(8,128)S(1)} %collective-permute-done.1.refs_2_, ...), custom_call_target="tpu_custom_call" | custom-call | flops 2415919104 | bytes 4194304 | tf_op jit(solution)/shard_map/pallas_call | solution.py:274
  51.6 1.8 %shard_map.119 = (f32[512,128]{1,0:T(8,128)S(1)}, f32[512,128]{1,0:T(8,128)S(1)}, f32[640,128]{1,0:T(8,128)S(1)}, f32[640,128]{1,0:T(8,128)S(1)}, f32[768,128]{1...) custom-call(s32[128]{0:T(128)S(1)} %get-tuple-element.39.table, ...), custom_call_target="tpu_custom_call" | custom-call | bytes 5242880 | tf_op jit(solution)/shard_map/pallas_call | solution.py:507
  53.4 1.9 %collective-permute-start.20 = (f32[768,128]{1,0:T(8,128)S(1)}, f32[768,128]{1,0:T(8,128)S(1)}, u32[]{:S(2)}, u32[]{:S(2)}) collective-permute-start(f32[768,128]{1,0:T(8,128)S(1)} %get-tuple-element.57), channel_id=1, source_target_pairs={{4,8},{8,4},{5,9},{9,5},{6,10},{10,6},{7,11},{11,7},{20,24},{24,20... | collective-permute-start | bytes 1179656 | tf_op jit(solution)/shard_map/ppermute | solution.py:627
  57.6 6.3 %collective-permute-done.20.refs_2_ = f32[768,128]{1,0:T(8,128)S(1)} collective-permute-done((f32[768,128]{1,0:T(8,128)S(1)}, f32[768,128]{1,0:T(8,128)S(1)}, u32[]{:S(2)}, u32[]{:S(2)}) %collective-permute-start.20) | collective-permute-done | bytes 393248 | tf_op jit(solution)/shard_map/ppermute | solution.py:627
  65.9 2.8 %shard_map.120 = (f32[4,64,256]{2,1,0:T(8,128)S(1)}, f32[4,64,256]{2,1,0:T(8,128)S(1)}) custom-call(s32[2]{0:T(128)S(1)} %copy-done.12, f32[8,256,128]{2,1,0:T(8,128)S(1)} %get-tuple-element.36.main_v, f32[8,256,128]{2,1,0:T(8,128)S(1)} %get-tuple-element.38.main_t, f32[512,128]{1,0:T(8,128)S(1)} %get-tuple-element.45.c_v, ...), custom_call_target="tpu_custom_call" | custom-call | flops 1207959552 | bytes 6291456 | tf_op jit(solution)/shard_map/pallas_call | solution.py:344
  68.9 4.1 %shard_map.121 = (f32[4,64,256]{2,1,0:T(8,128)S(1)}, f32[4,64,256]{2,1,0:T(8,128)S(1)}, f32[2,64,256]{2,1,0:T(8,128)S(1)}, f32[2,64,256]{2,1,0:T(8,128)S(1)}) custom-call(s32[2]{0:T(128)S(1)} %copy-done.12, f32[8,256,128]{2,1,0:T(8,128)S(1)} %get-tuple-element.36.main_v, f32[8,256,128]{2,1,0:T(8,128)S(1)} %get-tuple-element.38.main_t, ...), custom_call_target="tpu_custom_call" | custom-call | flops 1207959552 | bytes 6291456 | tf_op jit(solution)/shard_map/pallas_call | solution.py:344
  73.0 1.5 %collective-permute-start.15 = (f32[4,64,256]{2,1,0:T(8,128)S(1)}, f32[4,64,256]{2,1,0:T(8,128)S(1)}, u32[]{:S(2)}, u32[]{:S(2)}) collective-permute-start(f32[4,64,256]{2,1,0:T(8,128)S(1)} %get-tuple-element.52), channel_id=1, source_target_pairs={{0,2},{2,0},{1,3},{3,1},{4,6},{6,4},{5,7},{7,5},{8,10},{10,8},{9,1... | collective-permute-start | bytes 786440 | tf_op jit(solution)/shard_map/ppermute | solution.py:615
  74.5 17.5 %collective-permute-start.17 = (f32[2,64,256]{2,1,0:T(8,128)S(1)}, f32[2,64,256]{2,1,0:T(8,128)S(1)}, u32[]{:S(2)}, u32[]{:S(2)}) collective-permute-start(f32[2,64,256]{2,1,0:T(8,128)S(1)} %get-tuple-element.53.v_own), channel_id=1, source_target_pairs={{0,1},{1,0},{2,3},{3,2},{4,5},{5,4},{6,7},{7,6},{8,9},{9,8},{10,11... | collective-permute-start | bytes 393224 | tf_op jit(solution)/shard_map/ppermute | solution.py:619
  93.4 2.0 %shard_map.122 = (f32[256,128]{1,0:T(8,128)S(1)}, f32[256,128]{1,0:T(8,128)S(1)}, f32[64,128]{1,0:T(8,128)S(1)}, f32[64,128]{1,0:T(8,128)S(1)}) custom-call(s32[128]{0:T(128)S(1)} %get-tuple-element.39.table, f32[640,128]{1,0:T(8,128)S(1)} %get-tuple-element.55.refs_0_, f32[640,128]{1,0:T(8,128)S(1)} %collective-permute-done.19.refs_1_, ...), custom_call_target="tpu_custom_call" | custom-call | bytes 4194304 | tf_op jit(solution)/shard_map/pallas_call | solution.py:555
  95.6 4.7 %collective-permute-done.18.v_diag = f32[2,64,256]{2,1,0:T(8,128)S(1)} collective-permute-done((f32[2,64,256]{2,1,0:T(8,128)S(1)}, f32[2,64,256]{2,1,0:T(8,128)S(1)}, u32[]{:S(2)}, u32[]{:S(2)}) %collective-permute-start.18) | collective-permute-done | bytes 131104 | tf_op jit(solution)/shard_map/ppermute | solution.py:623
  101.3 3.5 %collective-permute-start.27 = (f32[64,128]{1,0:T(8,128)S(1)}, f32[64,128]{1,0:T(8,128)S(1)}, u32[]{:S(2)}, u32[]{:S(2)}) collective-permute-start(f32[64,128]{1,0:T(8,128)S(1)} %get-tuple-element.63), channel_id=1, source_target_pairs={{0,3},{1,2},{2,1},{3,0},{4,7},{5,6},{6,5},{7,4},{8,11},{9,10},{10,... | collective-permute-start | bytes 98312 | tf_op jit(solution)/shard_map/ppermute | solution.py:623
  105.0 1.8 %collective-permute-done.27.cv_diag = f32[64,128]{1,0:T(8,128)S(1)} collective-permute-done((f32[64,128]{1,0:T(8,128)S(1)}, f32[64,128]{1,0:T(8,128)S(1)}, u32[]{:S(2)}, u32[]{:S(2)}) %collective-permute-start.27) | collective-permute-done | bytes 32800 | tf_op jit(solution)/shard_map/ppermute | solution.py:623
  (69 shorter events, 25.4 us)
Async XLA Ops:
  3.6 8.5 %collective-permute-start.5 = (f32[256,128]{1,0:T(8,128)}, f32[256,128]{1,0:T(8,128)S(1)}, u32[]{:S(2)}, u32[]{:S(2)}) collective-permute-start(f32[256,128]{1,0:T(8,128)} %get-tuple-element.42.refs_0_), channel_id=1, source_target_pairs={{0,8},{12,4},{1,9},{13,5},{2,10},{14,6},{3,11},{15,7},{16,24},{28,... | collective-permute-start | bytes 393224 | tf_op jit(solution)/shard_map/ppermute | solution.py:627
  4.9 11.0 %collective-permute-start.4 = (f32[256,128]{1,0:T(8,128)}, f32[256,128]{1,0:T(8,128)S(1)}, u32[]{:S(2)}, u32[]{:S(2)}) collective-permute-start(f32[256,128]{1,0:T(8,128)} %get-tuple-element.42.refs_0_), channel_id=1, source_target_pairs={{4,8},{8,4},{5,9},{9,5},{6,10},{10,6},{7,11},{11,7},{20,24},{24,20... | collective-permute-start | bytes 393224 | tf_op jit(solution)/shard_map/ppermute | solution.py:627
  7.0 10.2 %collective-permute-start.3 = (f32[256,128]{1,0:T(8,128)}, f32[256,128]{1,0:T(8,128)S(1)}, u32[]{:S(2)}, u32[]{:S(2)}) collective-permute-start(f32[256,128]{1,0:T(8,128)} %get-tuple-element.42.refs_0_), channel_id=1, source_target_pairs={{0,4},{4,0},{8,12},{12,8},{1,5},{5,1},{9,13},{13,9},{2,6},{6,2},{1... | collective-permute-start | bytes 393224 | tf_op jit(solution)/shard_map/ppermute | solution.py:627
  7.7 16.9 %collective-permute-start.10 = (f32[512,128]{1,0:T(8,128)}, f32[512,128]{1,0:T(8,128)S(1)}, u32[]{:S(2)}, u32[]{:S(2)}) collective-permute-start(f32[512,128]{1,0:T(8,128)} %get-tuple-element.43.refs_0_), channel_id=1, source_target_pairs={{0,8},{12,4},{1,9},{13,5},{2,10},{14,6},{3,11},{15,7},{16,24},{28,... | collective-permute-start | bytes 786440 | tf_op jit(solution)/shard_map/ppermute | solution.py:627
  8.9 17.5 %collective-permute-start.9 = (f32[512,128]{1,0:T(8,128)}, f32[512,128]{1,0:T(8,128)S(1)}, u32[]{:S(2)}, u32[]{:S(2)}) collective-permute-start(f32[512,128]{1,0:T(8,128)} %get-tuple-element.43.refs_0_), channel_id=1, source_target_pairs={{4,8},{8,4},{5,9},{9,5},{6,10},{10,6},{7,11},{11,7},{20,24},{24,20... | collective-permute-start | bytes 786440 | tf_op jit(solution)/shard_map/ppermute | solution.py:627
  12.2 30.6 %collective-permute-start.2 = (f32[8,64,256]{2,1,0:T(8,128)}, f32[8,64,256]{2,1,0:T(8,128)S(1)}, u32[]{:S(2)}, u32[]{:S(2)}) collective-permute-start(f32[8,64,256]{2,1,0:T(8,128)} %get-tuple-element.37), channel_id=1, source_target_pairs={{0,2},{2,0},{1,3},{3,1},{4,6},{6,4},{5,7},{7,5},{8,10},{10,8},{9,1... | collective-permute-start | bytes 1572872 | tf_op jit(solution)/shard_map/ppermute | solution.py:615
  19.5 10.5 %collective-permute-start = (f32[4,64,256]{2,1,0:T(8,128)}, f32[4,64,256]{2,1,0:T(8,128)S(1)}, u32[]{:S(2)}, u32[]{:S(2)}) collective-permute-start(f32[4,64,256]{2,1,0:T(8,128)} %get-tuple-element.34), channel_id=1, source_target_pairs={{0,2},{2,0},{1,3},{3,1},{4,6},{6,4},{5,7},{7,5},{8,10},{10,8},{9,1... | collective-permute-start | bytes 786440 | tf_op jit(solution)/shard_map/ppermute | solution.py:615
  22.3 15.0 %collective-permute-start.8 = (f32[512,128]{1,0:T(8,128)}, f32[512,128]{1,0:T(8,128)S(1)}, u32[]{:S(2)}, u32[]{:S(2)}) collective-permute-start(f32[512,128]{1,0:T(8,128)} %get-tuple-element.43.refs_0_), channel_id=1, source_target_pairs={{0,4},{4,0},{8,12},{12,8},{1,5},{5,1},{9,13},{13,9},{2,6},{6,2},{1... | collective-permute-start | bytes 786440 | tf_op jit(solution)/shard_map/ppermute | solution.py:627
  24.5 12.8 %collective-permute-start.12 = (f32[512,128]{1,0:T(8,128)S(1)}, f32[512,128]{1,0:T(8,128)S(1)}, u32[]{:S(2)}, u32[]{:S(2)}) collective-permute-start(f32[512,128]{1,0:T(8,128)S(1)} %collective-permute-done.10.refs_3_), channel_id=1, source_target_pairs={{8,12},{4,0},{9,13},{5,1},{10,14},{6,2},{11,15},{7,3},{24,28},{20,... | collective-permute-start | bytes 786440 | tf_op jit(solution)/shard_map/ppermute | solution.py:627
  26.4 13.8 %collective-permute-start.11 = (f32[512,128]{1,0:T(8,128)S(1)}, f32[512,128]{1,0:T(8,128)S(1)}, u32[]{:S(2)}, u32[]{:S(2)}) collective-permute-start(f32[512,128]{1,0:T(8,128)S(1)} %collective-permute-done.9.refs_2_), channel_id=1, source_target_pairs={{8,12},{4,0},{9,13},{5,1},{10,14},{6,2},{11,15},{7,3},{24,28},{20,... | collective-permute-start | bytes 786440 | tf_op jit(solution)/shard_map/ppermute | solution.py:627
  30.0 17.4 %collective-permute-start.1 = (f32[4,64,256]{2,1,0:T(8,128)S(1)}, f32[4,64,256]{2,1,0:T(8,128)S(1)}, u32[]{:S(2)}, u32[]{:S(2)}) collective-permute-start(f32[4,64,256]{2,1,0:T(8,128)S(1)} %collective-permute-done.refs_1_), channel_id=1, source_target_pairs={{0,1},{1,0},{2,3},{3,2},{4,5},{5,4},{6,7},{7,6},{8,9},{9,8},{10,11... | collective-permute-start | bytes 786440 | tf_op jit(solution)/shard_map/ppermute | solution.py:619
  41.2 10.3 %collective-permute-start.13 = (f32[512,128]{1,0:T(8,128)S(1)}, f32[512,128]{1,0:T(8,128)S(1)}, u32[]{:S(2)}, u32[]{:S(2)}) collective-permute-start(f32[512,128]{1,0:T(8,128)S(1)} %shard_map.118.sent), channel_id=1, source_target_pairs={{0,2},{2,0},{1,3},{3,1},{4,6},{6,4},{5,7},{7,5},{8,10},{10,8},{9,1... | collective-permute-start | bytes 786440 | tf_op jit(solution)/shard_map/ppermute | solution.py:615
  53.4 10.6 %collective-permute-start.20 = (f32[768,128]{1,0:T(8,128)S(1)}, f32[768,128]{1,0:T(8,128)S(1)}, u32[]{:S(2)}, u32[]{:S(2)}) collective-permute-start(f32[768,128]{1,0:T(8,128)S(1)} %get-tuple-element.57), channel_id=1, source_target_pairs={{4,8},{8,4},{5,9},{9,5},{6,10},{10,6},{7,11},{11,7},{20,24},{24,20... | collective-permute-start | bytes 1179656 | tf_op jit(solution)/shard_map/ppermute | solution.py:627
  55.3 17.6 %collective-permute-start.19 = (f32[640,128]{1,0:T(8,128)S(1)}, f32[640,128]{1,0:T(8,128)S(1)}, u32[]{:S(2)}, u32[]{:S(2)}) collective-permute-start(f32[640,128]{1,0:T(8,128)S(1)} %get-tuple-element.56), channel_id=1, source_target_pairs={{0,4},{4,0},{8,12},{12,8},{1,5},{5,1},{9,13},{13,9},{2,6},{6,2},{1... | collective-permute-start | bytes 983048 | tf_op jit(solution)/shard_map/ppermute | solution.py:627
  56.3 18.1 %collective-permute-start.21 = (f32[640,128]{1,0:T(8,128)S(1)}, f32[640,128]{1,0:T(8,128)S(1)}, u32[]{:S(2)}, u32[]{:S(2)}) collective-permute-start(f32[640,128]{1,0:T(8,128)S(1)} %get-tuple-element.58), channel_id=1, source_target_pairs={{0,8},{12,4},{1,9},{13,5},{2,10},{14,6},{3,11},{15,7},{16,24},{28,... | collective-permute-start | bytes 983048 | tf_op jit(solution)/shard_map/ppermute | solution.py:627
  63.9 28.0 %collective-permute-start.22 = (f32[768,128]{1,0:T(8,128)S(1)}, f32[768,128]{1,0:T(8,128)S(1)}, u32[]{:S(2)}, u32[]{:S(2)}) collective-permute-start(f32[768,128]{1,0:T(8,128)S(1)} %collective-permute-done.20.refs_2_), channel_id=1, source_target_pairs={{8,12},{4,0},{9,13},{5,1},{10,14},{6,2},{11,15},{7,3},{24,28},{20,... | collective-permute-start | bytes 1179656 | tf_op jit(solution)/shard_map/ppermute | solution.py:627
  65.3 26.7 %collective-permute-start.23 = (f32[640,128]{1,0:T(8,128)S(1)}, f32[640,128]{1,0:T(8,128)S(1)}, u32[]{:S(2)}, u32[]{:S(2)}) collective-permute-start(f32[640,128]{1,0:T(8,128)S(1)} %get-tuple-element.59), channel_id=1, source_target_pairs={{0,12},{12,0},{1,13},{13,1},{2,14},{14,2},{3,15},{15,3},{16,28},{2... | collective-permute-start | bytes 983048 | tf_op jit(solution)/shard_map/ppermute | solution.py:627
  68.8 36.0 %collective-permute-start.14 = (f32[4,64,256]{2,1,0:T(8,128)S(1)}, f32[4,64,256]{2,1,0:T(8,128)S(1)}, u32[]{:S(2)}, u32[]{:S(2)}) collective-permute-start(f32[4,64,256]{2,1,0:T(8,128)S(1)} %get-tuple-element.51), channel_id=1, source_target_pairs={{0,2},{2,0},{1,3},{3,1},{4,6},{6,4},{5,7},{7,5},{8,10},{10,8},{9,1... | collective-permute-start | bytes 786440 | tf_op jit(solution)/shard_map/ppermute | solution.py:615
  73.0 32.0 %collective-permute-start.15 = (f32[4,64,256]{2,1,0:T(8,128)S(1)}, f32[4,64,256]{2,1,0:T(8,128)S(1)}, u32[]{:S(2)}, u32[]{:S(2)}) collective-permute-start(f32[4,64,256]{2,1,0:T(8,128)S(1)} %get-tuple-element.52), channel_id=1, source_target_pairs={{0,2},{2,0},{1,3},{3,1},{4,6},{6,4},{5,7},{7,5},{8,10},{10,8},{9,1... | collective-permute-start | bytes 786440 | tf_op jit(solution)/shard_map/ppermute | solution.py:615
  74.5 20.9 %collective-permute-start.17 = (f32[2,64,256]{2,1,0:T(8,128)S(1)}, f32[2,64,256]{2,1,0:T(8,128)S(1)}, u32[]{:S(2)}, u32[]{:S(2)}) collective-permute-start(f32[2,64,256]{2,1,0:T(8,128)S(1)} %get-tuple-element.53.v_own), channel_id=1, source_target_pairs={{0,1},{1,0},{2,3},{3,2},{4,5},{5,4},{6,7},{7,6},{8,9},{9,8},{10,11... | collective-permute-start | bytes 393224 | tf_op jit(solution)/shard_map/ppermute | solution.py:619
  91.9 8.3 %collective-permute-start.18 = (f32[2,64,256]{2,1,0:T(8,128)S(1)}, f32[2,64,256]{2,1,0:T(8,128)S(1)}, u32[]{:S(2)}, u32[]{:S(2)}) collective-permute-start(f32[2,64,256]{2,1,0:T(8,128)S(1)} %get-tuple-element.54), channel_id=1, source_target_pairs={{0,3},{1,2},{2,1},{3,0},{4,7},{5,6},{6,5},{7,4},{8,11},{9,10},{10,... | collective-permute-start | bytes 393224 | tf_op jit(solution)/shard_map/ppermute | solution.py:623
  91.9 9.3 %collective-permute-start.16 = (f32[2,64,256]{2,1,0:T(8,128)S(1)}, f32[2,64,256]{2,1,0:T(8,128)S(1)}, u32[]{:S(2)}, u32[]{:S(2)}) collective-permute-start(f32[2,64,256]{2,1,0:T(8,128)S(1)} %get-tuple-element.54), channel_id=1, source_target_pairs={{0,2},{2,0},{1,3},{3,1},{4,6},{6,4},{5,7},{7,5},{8,10},{10,8},{9,1... | collective-permute-start | bytes 393224 | tf_op jit(solution)/shard_map/ppermute | solution.py:615
  95.4 12.1 %collective-permute-start.24 = (f32[256,128]{1,0:T(8,128)S(1)}, f32[256,128]{1,0:T(8,128)S(1)}, u32[]{:S(2)}, u32[]{:S(2)}) collective-permute-start(f32[256,128]{1,0:T(8,128)S(1)} %get-tuple-element.61), channel_id=1, source_target_pairs={{0,2},{2,0},{1,3},{3,1},{4,6},{6,4},{5,7},{7,5},{8,10},{10,8},{9,1... | collective-permute-start | bytes 393224 | tf_op jit(solution)/shard_map/ppermute | solution.py:615
  101.3 5.5 %collective-permute-start.27 = (f32[64,128]{1,0:T(8,128)S(1)}, f32[64,128]{1,0:T(8,128)S(1)}, u32[]{:S(2)}, u32[]{:S(2)}) collective-permute-start(f32[64,128]{1,0:T(8,128)S(1)} %get-tuple-element.63), channel_id=1, source_target_pairs={{0,3},{1,2},{2,1},{3,0},{4,7},{5,6},{6,5},{7,4},{8,11},{9,10},{10,... | collective-permute-start | bytes 98312 | tf_op jit(solution)/shard_map/ppermute | solution.py:623
  (17 other events, 132.3 us)

commit v4 on v3

--- a/solution.py
+++ b/solution.py
@@ -377,7 +377,7 @@
 
 def came_from(z):
     end = is_end(z)
-    mirrored, two_on = LINE - 1 - z, (z + 2) % LINE
+    mirrored, two_on = LINE - 1 - z, (z + 2) & (LINE - 1)
     return [
         z,
         z ^ 1,
@@ -388,19 +388,21 @@
     ]
 
 
+def split_index(v, n):
+    return v >> (n.bit_length() - 1), v & (n - 1)
+
+
 def source(v, tiles):
-    slot = v >> 3
-    where = slot // tiles
-    return where, slot - where * tiles, (v >> 1) & 3, (v & 1) == 1
+    where, edge = split_index(v >> 1, 4 * tiles)
+    return where, edge, (v & 1) == 1
 
 
 def gather_rims(tiles, table, z, ring, out, packed):
-    group = tiles // 2
     for m in range(tiles * 4):
-        where, loc, code, mirrored = source(table[z * tiles * 4 + m], tiles)
-        upper = loc // group if packed else 0
-        row = pl.multiple_of(((loc - upper * group) * 4 + code) * S, S)
-        v = ring[where, pl.ds(row, S), :]
+        where, edge, mirrored = source(table[z * tiles * 4 + m], tiles)
+        if packed:
+            upper, edge = split_index(edge, tiles * 2)
+        v = ring[where, pl.ds(pl.multiple_of(edge * S, S), S), :]
         if packed:
             v = jnp.where(upper == 1, swap(v), v)
         out[m * S : (m + 1) * S, :] = jnp.where(mirrored, flip16(v), v)
@@ -489,11 +491,10 @@
         (z, ((home, rows),)),
         (z ^ 1, ((near, rows),)),
         (LINE - 1 - z, ((inner, rows), (mirror, rows))),
-        ((z + 2) % LINE, ((outer, rows), (inner, rows + share * 4 * S))),
+        ((z + 2) & (LINE - 1), ((outer, rows), (inner, rows + share * 4 * S))),
     ):
         for m in range(share * 4):
-            where, loc, code, flip = source(table[(zz * tiles + q * share) * 4 + m], tiles)
-            at = loc * 4 + code
+            where, at, flip = source(table[(zz * tiles + q * share) * 4 + m], tiles)
             v = jnp.where(flip, mirrored[at], plain[at])
             v = jnp.where(where == z, v, 0.0)
             for msg, base in places:
@@ -528,10 +529,7 @@
     pairs = [(e.at[pl.ds(0, rows)], ring.at[where]) for e, where in zip(parts, came_from(z))]
     pairs += [(e.at[pl.ds(base, tail)], rims_v.at[k]) for k, (e, base) in enumerate(zip(parts, bases))]
     finished(started(pairs, sems))
-    for m in range(tiles * 4):
-        where, loc, code, mirrored = source(table[z * tiles * 4 + m], tiles)
-        e = ring[where, pl.ds(pl.multiple_of((loc * 4 + code) * S, S), S), :]
-        rims[m * S : (m + 1) * S, :] = jnp.where(mirrored, flip16(e), e)
+    gather_rims(tiles, table, z, ring, rims, False)
     rims[rows:, :] = ((rims_v[0] + rims_v[1]) + (rims_v[2] + rims_v[3])) + (rims_v[4] + rims_v[5])
     every = tiles + share
     for side in range(4):

time: 109 us -> 109 us (level)
  no operation moved by 1% of the time
where the time goes in v4:
time: 109 us
  starting transfers between devices  54.5 us (50%)
  Pallas kernels  27.7 us (25%)
  waiting for transfers between devices  24.2 us (22%)
  local copies, waits for them, and re-layouts  1.32 us (1%)
    ppermute x15, starting transfers between devices, along(): return lax.ppermute(v, 'tiles', pairs)  22.7 us
    ppermute x3, starting transfers between devices, mate(): return lax.ppermute(v, 'dirs', [(0, 1), (1, 0)])  20.8 us
    ppermute x15, waiting for transfers between devices, along(): return lax.ppermute(v, 'tiles', pairs)  14.5 us
    pallas_call x2, Pallas kernels, conv_in(): pl.pallas_call(functools.partial(conv_in_kernel, count), out_shape=(f32_o...  8.17 us
    ppermute x8, starting transfers between devices, across(): return lax.ppermute(v, 'chan', [(0, 1), (1, 0)])  7.49 us
    pallas_call x2, Pallas kernels, conv_out(): pl.pallas_call(functools.partial(conv_out_kernel, count, values_too), out...  6.9 us
    ppermute x2, waiting for transfers between devices, diagonal(): return lax.ppermute(v, ('chan', 'dirs'), [(0, 3), (1, 2), (2, 1), (3, 0)])  6.65 us
    ppermute x2, starting transfers between devices, diagonal(): return lax.ppermute(v, ('chan', 'dirs'), [(0, 3), (1, 2), (2, 1), (3, 0)])  3.49 us
  transfers between devices with their start and end apart: 28, of which 9 were waited for; matrix products, arithmetic and copies ran while one was open for 0% of the time, Pallas kernels for 20%

profile of v4, /device:TPU:17, one launch (start us, length us, event | category | flops | bytes accessed | tf_op | source)
XLA Modules:
  0.0 108.7 jit_solution(5654943898683156690)
XLA Ops:
  0.7 3.0 %shard_map.113 = (f32[512,128]{1,0:T(8,128)}, f32[256,128]{1,0:T(8,128)}, f32[8,64,256]{2,1,0:T(8,128)}, f32[4,64,256]{2,1,0:T(8,128)}, s32[2]{0:T(128)}) custom-call(f32[2,8,64,256]{3,2,1,0:T(8,128)} %refs_0_.3, f32[8,64,256]{2,1,0:T(8,128)} %refs_0_.2), custom_call_target="tpu_custom_call" | custom-call | bytes 3145728 | tf_op jit(solution)/shard_map/pallas_call | solution.py:190
  4.9 2.1 %collective-permute-start.4 = (f32[256,128]{1,0:T(8,128)}, f32[256,128]{1,0:T(8,128)S(1)}, u32[]{:S(2)}, u32[]{:S(2)}) collective-permute-start(f32[256,128]{1,0:T(8,128)} %get-tuple-element.42.refs_0_), channel_id=1, source_target_pairs={{4,8},{8,4},{5,9},{9,5},{6,10},{10,6},{7,11},{11,7},{20,24},{24,20... | collective-permute-start | bytes 393224 | tf_op jit(solution)/shard_map/ppermute | solution.py:625
  8.9 3.2 %collective-permute-start.9 = (f32[512,128]{1,0:T(8,128)}, f32[512,128]{1,0:T(8,128)S(1)}, u32[]{:S(2)}, u32[]{:S(2)}) collective-permute-start(f32[512,128]{1,0:T(8,128)} %get-tuple-element.43.refs_0_), channel_id=1, source_target_pairs={{4,8},{8,4},{5,9},{9,5},{6,10},{10,6},{7,11},{11,7},{20,24},{24,20... | collective-permute-start | bytes 786440 | tf_op jit(solution)/shard_map/ppermute | solution.py:625
  13.4 2.5 %collective-permute-done.4.refs_2_ = f32[256,128]{1,0:T(8,128)S(1)} collective-permute-done((f32[256,128]{1,0:T(8,128)}, f32[256,128]{1,0:T(8,128)S(1)}, u32[]{:S(2)}, u32[]{:S(2)}) %collective-permute-start.4) | collective-permute-done | bytes 131104 | tf_op jit(solution)/shard_map/ppermute | solution.py:625
  22.3 2.2 %collective-permute-start.8 = (f32[512,128]{1,0:T(8,128)}, f32[512,128]{1,0:T(8,128)S(1)}, u32[]{:S(2)}, u32[]{:S(2)}) collective-permute-start(f32[512,128]{1,0:T(8,128)} %get-tuple-element.43.refs_0_), channel_id=1, source_target_pairs={{0,4},{4,0},{8,12},{12,8},{1,5},{5,1},{9,13},{13,9},{2,6},{6,2},{1... | collective-permute-start | bytes 786440 | tf_op jit(solution)/shard_map/ppermute | solution.py:625
  24.5 1.9 %collective-permute-start.12 = (f32[512,128]{1,0:T(8,128)S(1)}, f32[512,128]{1,0:T(8,128)S(1)}, u32[]{:S(2)}, u32[]{:S(2)}) collective-permute-start(f32[512,128]{1,0:T(8,128)S(1)} %collective-permute-done.10.refs_3_), channel_id=1, source_target_pairs={{8,12},{4,0},{9,13},{5,1},{10,14},{6,2},{11,15},{7,3},{24,28},{20,... | collective-permute-start | bytes 786440 | tf_op jit(solution)/shard_map/ppermute | solution.py:625
  27.7 2.3 %collective-permute-done.refs_1_ = f32[4,64,256]{2,1,0:T(8,128)S(1)} collective-permute-done((f32[4,64,256]{2,1,0:T(8,128)}, f32[4,64,256]{2,1,0:T(8,128)S(1)}, u32[]{:S(2)}, u32[]{:S(2)}) %collective-permute-start) | collective-permute-done | bytes 262176 | tf_op jit(solution)/shard_map/ppermute | solution.py:613
  30.0 2.4 %collective-permute-start.1 = (f32[4,64,256]{2,1,0:T(8,128)S(1)}, f32[4,64,256]{2,1,0:T(8,128)S(1)}, u32[]{:S(2)}, u32[]{:S(2)}) collective-permute-start(f32[4,64,256]{2,1,0:T(8,128)S(1)} %collective-permute-done.refs_1_), channel_id=1, source_target_pairs={{0,1},{1,0},{2,3},{3,2},{4,5},{5,4},{6,7},{7,6},{8,9},{9,8},{10,11... | collective-permute-start | bytes 786440 | tf_op jit(solution)/shard_map/ppermute | solution.py:617
  33.1 2.0 %shard_map.114 = (s32[128]{0:T(128)S(1)}, bf16[1152,256]{1,0:T(8,128)(2,1)S(1)}, bf16[1152,256]{1,0:T(8,128)(2,1)S(1)}, f32[1,128]{1,0:T(1,128)S(1)}, f32[1,128]{1,0:T(1,128)S(1)}) custom-call(s32[4,32]{1,0:T(4,128)S(1)} %bitcast.5, s32[4,32]{1,0:T(4,128)S(1)} %bitcast.6, s32[4,32]{1,0:T(4,128)S(1)} %bitcast.7, s32[32]{0:T(128)S(1)} %copy-done.9, ...), custom_call_target="tpu_custom_call" | custom-call | bytes 4194304 | tf_op jit(solution)/shard_map/pallas_call | solution.py:146
  35.1 1.8 %shard_map.117.keep = f32[512,128]{1,0:T(8,128)S(1)} custom-call(s32[128]{0:T(128)S(1)} %get-tuple-element.39.table, f32[256,128]{1,0:T(8,128)S(1)} %copy-done.5, f32[256,128]{1,0:T(8,128)S(1)} %collective-permute-done.3.refs_1_, f32[256,128]{1,0:T(8,128)S(1)} %collective-permute-done.4.refs_2_, f32[256,128]{1,0:T(8,128)S(1)} %collective-permute-done.5.refs_3_, ...), custom_call_target="tpu_custom_call" | custom-call | bytes 3145728 | tf_op jit(solution)/shard_map/pallas_call | solution.py:420
  37.0 3.2 %collective-permute-done.11.refs_4_ = f32[512,128]{1,0:T(8,128)S(1)} collective-permute-done((f32[512,128]{1,0:T(8,128)S(1)}, f32[512,128]{1,0:T(8,128)S(1)}, u32[]{:S(2)}, u32[]{:S(2)}) %collective-permute-start.11) | collective-permute-done | bytes 262176 | tf_op jit(solution)/shard_map/ppermute | solution.py:625
  43.2 4.1 %shard_map.116 = (f32[8,256,128]{2,1,0:T(8,128)S(1)}, f32[512,128]{1,0:T(8,128)S(1)}) custom-call(s32[2]{0:T(128)S(1)} %copy-done.12, f32[2,8,64,256]{3,2,1,0:T(8,128)S(1)} %copy-done, f32[8,64,256]{2,1,0:T(8,128)S(1)} %collective-permute-done.2.refs_1_, bf16[1152,256]{1,0:T(8,128)(2,1)S(1)} %get-tuple-element.35.refs_3_.refs_2_.w), custom_call_target="tpu_custom_call" | custom-call | flops 2415919104 | bytes 4194304 | tf_op jit(solution)/shard_map/pallas_call | solution.py:274
  47.3 4.1 %shard_map.115 = (f32[8,256,128]{2,1,0:T(8,128)S(1)}, f32[512,128]{1,0:T(8,128)S(1)}) custom-call(s32[2]{0:T(128)S(1)} %copy-done.12, f32[8,64,256]{2,1,0:T(8,128)S(1)} %copy-done.3, f32[4,64,256]{2,1,0:T(8,128)S(1)} %collective-permute-done.refs_1_, f32[4,64,256]{2,1,0:T(8,128)S(1)} %collective-permute-done.1.refs_2_, ...), custom_call_target="tpu_custom_call" | custom-call | flops 2415919104 | bytes 4194304 | tf_op jit(solution)/shard_map/pallas_call | solution.py:274
  51.4 1.7 %shard_map.119 = (f32[512,128]{1,0:T(8,128)S(1)}, f32[512,128]{1,0:T(8,128)S(1)}, f32[640,128]{1,0:T(8,128)S(1)}, f32[640,128]{1,0:T(8,128)S(1)}, f32[768,128]{1...) custom-call(s32[128]{0:T(128)S(1)} %get-tuple-element.39.table, ...), custom_call_target="tpu_custom_call" | custom-call | bytes 5242880 | tf_op jit(solution)/shard_map/pallas_call | solution.py:508
  53.1 1.9 %collective-permute-start.20 = (f32[768,128]{1,0:T(8,128)S(1)}, f32[768,128]{1,0:T(8,128)S(1)}, u32[]{:S(2)}, u32[]{:S(2)}) collective-permute-start(f32[768,128]{1,0:T(8,128)S(1)} %get-tuple-element.57), channel_id=1, source_target_pairs={{4,8},{8,4},{5,9},{9,5},{6,10},{10,6},{7,11},{11,7},{20,24},{24,20... | collective-permute-start | bytes 1179656 | tf_op jit(solution)/shard_map/ppermute | solution.py:625
  57.4 6.3 %collective-permute-done.20.refs_2_ = f32[768,128]{1,0:T(8,128)S(1)} collective-permute-done((f32[768,128]{1,0:T(8,128)S(1)}, f32[768,128]{1,0:T(8,128)S(1)}, u32[]{:S(2)}, u32[]{:S(2)}) %collective-permute-start.20) | collective-permute-done | bytes 393248 | tf_op jit(solution)/shard_map/ppermute | solution.py:625
  65.7 2.8 %shard_map.120 = (f32[4,64,256]{2,1,0:T(8,128)S(1)}, f32[4,64,256]{2,1,0:T(8,128)S(1)}) custom-call(s32[2]{0:T(128)S(1)} %copy-done.12, f32[8,256,128]{2,1,0:T(8,128)S(1)} %get-tuple-element.36.main_v, f32[8,256,128]{2,1,0:T(8,128)S(1)} %get-tuple-element.38.main_t, f32[512,128]{1,0:T(8,128)S(1)} %get-tuple-element.45.c_v, ...), custom_call_target="tpu_custom_call" | custom-call | flops 1207959552 | bytes 6291456 | tf_op jit(solution)/shard_map/pallas_call | solution.py:344
  68.6 4.1 %shard_map.121 = (f32[4,64,256]{2,1,0:T(8,128)S(1)}, f32[4,64,256]{2,1,0:T(8,128)S(1)}, f32[2,64,256]{2,1,0:T(8,128)S(1)}, f32[2,64,256]{2,1,0:T(8,128)S(1)}) custom-call(s32[2]{0:T(128)S(1)} %copy-done.12, f32[8,256,128]{2,1,0:T(8,128)S(1)} %get-tuple-element.36.main_v, f32[8,256,128]{2,1,0:T(8,128)S(1)} %get-tuple-element.38.main_t, ...), custom_call_target="tpu_custom_call" | custom-call | flops 1207959552 | bytes 6291456 | tf_op jit(solution)/shard_map/pallas_call | solution.py:344
  72.7 1.5 %collective-permute-start.15 = (f32[4,64,256]{2,1,0:T(8,128)S(1)}, f32[4,64,256]{2,1,0:T(8,128)S(1)}, u32[]{:S(2)}, u32[]{:S(2)}) collective-permute-start(f32[4,64,256]{2,1,0:T(8,128)S(1)} %get-tuple-element.52), channel_id=1, source_target_pairs={{0,2},{2,0},{1,3},{3,1},{4,6},{6,4},{5,7},{7,5},{8,10},{10,8},{9,1... | collective-permute-start | bytes 786440 | tf_op jit(solution)/shard_map/ppermute | solution.py:613
  74.2 17.5 %collective-permute-start.17 = (f32[2,64,256]{2,1,0:T(8,128)S(1)}, f32[2,64,256]{2,1,0:T(8,128)S(1)}, u32[]{:S(2)}, u32[]{:S(2)}) collective-permute-start(f32[2,64,256]{2,1,0:T(8,128)S(1)} %get-tuple-element.53.v_own), channel_id=1, source_target_pairs={{0,1},{1,0},{2,3},{3,2},{4,5},{5,4},{6,7},{7,6},{8,9},{9,8},{10,11... | collective-permute-start | bytes 393224 | tf_op jit(solution)/shard_map/ppermute | solution.py:617
  93.1 1.9 %shard_map.122 = (f32[256,128]{1,0:T(8,128)S(1)}, f32[256,128]{1,0:T(8,128)S(1)}, f32[64,128]{1,0:T(8,128)S(1)}, f32[64,128]{1,0:T(8,128)S(1)}) custom-call(s32[128]{0:T(128)S(1)} %get-tuple-element.39.table, f32[640,128]{1,0:T(8,128)S(1)} %get-tuple-element.55.refs_0_, f32[640,128]{1,0:T(8,128)S(1)} %collective-permute-done.19.refs_1_, ...), custom_call_target="tpu_custom_call" | custom-call | bytes 4194304 | tf_op jit(solution)/shard_map/pallas_call | solution.py:553
  95.2 4.8 %collective-permute-done.18.v_diag = f32[2,64,256]{2,1,0:T(8,128)S(1)} collective-permute-done((f32[2,64,256]{2,1,0:T(8,128)S(1)}, f32[2,64,256]{2,1,0:T(8,128)S(1)}, u32[]{:S(2)}, u32[]{:S(2)}) %collective-permute-start.18) | collective-permute-done | bytes 131104 | tf_op jit(solution)/shard_map/ppermute | solution.py:621
  101.0 3.5 %collective-permute-start.27 = (f32[64,128]{1,0:T(8,128)S(1)}, f32[64,128]{1,0:T(8,128)S(1)}, u32[]{:S(2)}, u32[]{:S(2)}) collective-permute-start(f32[64,128]{1,0:T(8,128)S(1)} %get-tuple-element.63), channel_id=1, source_target_pairs={{0,3},{1,2},{2,1},{3,0},{4,7},{5,6},{6,5},{7,4},{8,11},{9,10},{10,... | collective-permute-start | bytes 98312 | tf_op jit(solution)/shard_map/ppermute | solution.py:621
  104.7 1.8 %collective-permute-done.27.cv_diag = f32[64,128]{1,0:T(8,128)S(1)} collective-permute-done((f32[64,128]{1,0:T(8,128)S(1)}, f32[64,128]{1,0:T(8,128)S(1)}, u32[]{:S(2)}, u32[]{:S(2)}) %collective-permute-start.27) | collective-permute-done | bytes 32800 | tf_op jit(solution)/shard_map/ppermute | solution.py:621
  (69 shorter events, 25.2 us)
Async XLA Ops:
  3.6 8.5 %collective-permute-start.5 = (f32[256,128]{1,0:T(8,128)}, f32[256,128]{1,0:T(8,128)S(1)}, u32[]{:S(2)}, u32[]{:S(2)}) collective-permute-start(f32[256,128]{1,0:T(8,128)} %get-tuple-element.42.refs_0_), channel_id=1, source_target_pairs={{0,8},{12,4},{1,9},{13,5},{2,10},{14,6},{3,11},{15,7},{16,24},{28,... | collective-permute-start | bytes 393224 | tf_op jit(solution)/shard_map/ppermute | solution.py:625
  4.9 11.0 %collective-permute-start.4 = (f32[256,128]{1,0:T(8,128)}, f32[256,128]{1,0:T(8,128)S(1)}, u32[]{:S(2)}, u32[]{:S(2)}) collective-permute-start(f32[256,128]{1,0:T(8,128)} %get-tuple-element.42.refs_0_), channel_id=1, source_target_pairs={{4,8},{8,4},{5,9},{9,5},{6,10},{10,6},{7,11},{11,7},{20,24},{24,20... | collective-permute-start | bytes 393224 | tf_op jit(solution)/shard_map/ppermute | solution.py:625
  7.0 10.2 %collective-permute-start.3 = (f32[256,128]{1,0:T(8,128)}, f32[256,128]{1,0:T(8,128)S(1)}, u32[]{:S(2)}, u32[]{:S(2)}) collective-permute-start(f32[256,128]{1,0:T(8,128)} %get-tuple-element.42.refs_0_), channel_id=1, source_target_pairs={{0,4},{4,0},{8,12},{12,8},{1,5},{5,1},{9,13},{13,9},{2,6},{6,2},{1... | collective-permute-start | bytes 393224 | tf_op jit(solution)/shard_map/ppermute | solution.py:625
  7.7 16.9 %collective-permute-start.10 = (f32[512,128]{1,0:T(8,128)}, f32[512,128]{1,0:T(8,128)S(1)}, u32[]{:S(2)}, u32[]{:S(2)}) collective-permute-start(f32[512,128]{1,0:T(8,128)} %get-tuple-element.43.refs_0_), channel_id=1, source_target_pairs={{0,8},{12,4},{1,9},{13,5},{2,10},{14,6},{3,11},{15,7},{16,24},{28,... | collective-permute-start | bytes 786440 | tf_op jit(solution)/shard_map/ppermute | solution.py:625
  8.9 17.5 %collective-permute-start.9 = (f32[512,128]{1,0:T(8,128)}, f32[512,128]{1,0:T(8,128)S(1)}, u32[]{:S(2)}, u32[]{:S(2)}) collective-permute-start(f32[512,128]{1,0:T(8,128)} %get-tuple-element.43.refs_0_), channel_id=1, source_target_pairs={{4,8},{8,4},{5,9},{9,5},{6,10},{10,6},{7,11},{11,7},{20,24},{24,20... | collective-permute-start | bytes 786440 | tf_op jit(solution)/shard_map/ppermute | solution.py:625
  12.2 30.4 %collective-permute-start.2 = (f32[8,64,256]{2,1,0:T(8,128)}, f32[8,64,256]{2,1,0:T(8,128)S(1)}, u32[]{:S(2)}, u32[]{:S(2)}) collective-permute-start(f32[8,64,256]{2,1,0:T(8,128)} %get-tuple-element.37), channel_id=1, source_target_pairs={{0,2},{2,0},{1,3},{3,1},{4,6},{6,4},{5,7},{7,5},{8,10},{10,8},{9,1... | collective-permute-start | bytes 1572872 | tf_op jit(solution)/shard_map/ppermute | solution.py:613
  19.5 10.5 %collective-permute-start = (f32[4,64,256]{2,1,0:T(8,128)}, f32[4,64,256]{2,1,0:T(8,128)S(1)}, u32[]{:S(2)}, u32[]{:S(2)}) collective-permute-start(f32[4,64,256]{2,1,0:T(8,128)} %get-tuple-element.34), channel_id=1, source_target_pairs={{0,2},{2,0},{1,3},{3,1},{4,6},{6,4},{5,7},{7,5},{8,10},{10,8},{9,1... | collective-permute-start | bytes 786440 | tf_op jit(solution)/shard_map/ppermute | solution.py:613
  22.3 14.7 %collective-permute-start.8 = (f32[512,128]{1,0:T(8,128)}, f32[512,128]{1,0:T(8,128)S(1)}, u32[]{:S(2)}, u32[]{:S(2)}) collective-permute-start(f32[512,128]{1,0:T(8,128)} %get-tuple-element.43.refs_0_), channel_id=1, source_target_pairs={{0,4},{4,0},{8,12},{12,8},{1,5},{5,1},{9,13},{13,9},{2,6},{6,2},{1... | collective-permute-start | bytes 786440 | tf_op jit(solution)/shard_map/ppermute | solution.py:625
  24.5 12.5 %collective-permute-start.12 = (f32[512,128]{1,0:T(8,128)S(1)}, f32[512,128]{1,0:T(8,128)S(1)}, u32[]{:S(2)}, u32[]{:S(2)}) collective-permute-start(f32[512,128]{1,0:T(8,128)S(1)} %collective-permute-done.10.refs_3_), channel_id=1, source_target_pairs={{8,12},{4,0},{9,13},{5,1},{10,14},{6,2},{11,15},{7,3},{24,28},{20,... | collective-permute-start | bytes 786440 | tf_op jit(solution)/shard_map/ppermute | solution.py:625
  26.4 13.8 %collective-permute-start.11 = (f32[512,128]{1,0:T(8,128)S(1)}, f32[512,128]{1,0:T(8,128)S(1)}, u32[]{:S(2)}, u32[]{:S(2)}) collective-permute-start(f32[512,128]{1,0:T(8,128)S(1)} %collective-permute-done.9.refs_2_), channel_id=1, source_target_pairs={{8,12},{4,0},{9,13},{5,1},{10,14},{6,2},{11,15},{7,3},{24,28},{20,... | collective-permute-start | bytes 786440 | tf_op jit(solution)/shard_map/ppermute | solution.py:625
  30.0 17.3 %collective-permute-start.1 = (f32[4,64,256]{2,1,0:T(8,128)S(1)}, f32[4,64,256]{2,1,0:T(8,128)S(1)}, u32[]{:S(2)}, u32[]{:S(2)}) collective-permute-start(f32[4,64,256]{2,1,0:T(8,128)S(1)} %collective-permute-done.refs_1_), channel_id=1, source_target_pairs={{0,1},{1,0},{2,3},{3,2},{4,5},{5,4},{6,7},{7,6},{8,9},{9,8},{10,11... | collective-permute-start | bytes 786440 | tf_op jit(solution)/shard_map/ppermute | solution.py:617
  41.1 10.3 %collective-permute-start.13 = (f32[512,128]{1,0:T(8,128)S(1)}, f32[512,128]{1,0:T(8,128)S(1)}, u32[]{:S(2)}, u32[]{:S(2)}) collective-permute-start(f32[512,128]{1,0:T(8,128)S(1)} %shard_map.118.sent), channel_id=1, source_target_pairs={{0,2},{2,0},{1,3},{3,1},{4,6},{6,4},{5,7},{7,5},{8,10},{10,8},{9,1... | collective-permute-start | bytes 786440 | tf_op jit(solution)/shard_map/ppermute | solution.py:613
  53.1 10.6 %collective-permute-start.20 = (f32[768,128]{1,0:T(8,128)S(1)}, f32[768,128]{1,0:T(8,128)S(1)}, u32[]{:S(2)}, u32[]{:S(2)}) collective-permute-start(f32[768,128]{1,0:T(8,128)S(1)} %get-tuple-element.57), channel_id=1, source_target_pairs={{4,8},{8,4},{5,9},{9,5},{6,10},{10,6},{7,11},{11,7},{20,24},{24,20... | collective-permute-start | bytes 1179656 | tf_op jit(solution)/shard_map/ppermute | solution.py:625
  55.0 17.6 %collective-permute-start.19 = (f32[640,128]{1,0:T(8,128)S(1)}, f32[640,128]{1,0:T(8,128)S(1)}, u32[]{:S(2)}, u32[]{:S(2)}) collective-permute-start(f32[640,128]{1,0:T(8,128)S(1)} %get-tuple-element.56), channel_id=1, source_target_pairs={{0,4},{4,0},{8,12},{12,8},{1,5},{5,1},{9,13},{13,9},{2,6},{6,2},{1... | collective-permute-start | bytes 983048 | tf_op jit(solution)/shard_map/ppermute | solution.py:625
  56.1 18.1 %collective-permute-start.21 = (f32[640,128]{1,0:T(8,128)S(1)}, f32[640,128]{1,0:T(8,128)S(1)}, u32[]{:S(2)}, u32[]{:S(2)}) collective-permute-start(f32[640,128]{1,0:T(8,128)S(1)} %get-tuple-element.58), channel_id=1, source_target_pairs={{0,8},{12,4},{1,9},{13,5},{2,10},{14,6},{3,11},{15,7},{16,24},{28,... | collective-permute-start | bytes 983048 | tf_op jit(solution)/shard_map/ppermute | solution.py:625
  63.7 28.0 %collective-permute-start.22 = (f32[768,128]{1,0:T(8,128)S(1)}, f32[768,128]{1,0:T(8,128)S(1)}, u32[]{:S(2)}, u32[]{:S(2)}) collective-permute-start(f32[768,128]{1,0:T(8,128)S(1)} %collective-permute-done.20.refs_2_), channel_id=1, source_target_pairs={{8,12},{4,0},{9,13},{5,1},{10,14},{6,2},{11,15},{7,3},{24,28},{20,... | collective-permute-start | bytes 1179656 | tf_op jit(solution)/shard_map/ppermute | solution.py:625
  65.0 26.7 %collective-permute-start.23 = (f32[640,128]{1,0:T(8,128)S(1)}, f32[640,128]{1,0:T(8,128)S(1)}, u32[]{:S(2)}, u32[]{:S(2)}) collective-permute-start(f32[640,128]{1,0:T(8,128)S(1)} %get-tuple-element.59), channel_id=1, source_target_pairs={{0,12},{12,0},{1,13},{13,1},{2,14},{14,2},{3,15},{15,3},{16,28},{2... | collective-permute-start | bytes 983048 | tf_op jit(solution)/shard_map/ppermute | solution.py:625
  68.5 36.0 %collective-permute-start.14 = (f32[4,64,256]{2,1,0:T(8,128)S(1)}, f32[4,64,256]{2,1,0:T(8,128)S(1)}, u32[]{:S(2)}, u32[]{:S(2)}) collective-permute-start(f32[4,64,256]{2,1,0:T(8,128)S(1)} %get-tuple-element.51), channel_id=1, source_target_pairs={{0,2},{2,0},{1,3},{3,1},{4,6},{6,4},{5,7},{7,5},{8,10},{10,8},{9,1... | collective-permute-start | bytes 786440 | tf_op jit(solution)/shard_map/ppermute | solution.py:613
  72.7 32.0 %collective-permute-start.15 = (f32[4,64,256]{2,1,0:T(8,128)S(1)}, f32[4,64,256]{2,1,0:T(8,128)S(1)}, u32[]{:S(2)}, u32[]{:S(2)}) collective-permute-start(f32[4,64,256]{2,1,0:T(8,128)S(1)} %get-tuple-element.52), channel_id=1, source_target_pairs={{0,2},{2,0},{1,3},{3,1},{4,6},{6,4},{5,7},{7,5},{8,10},{10,8},{9,1... | collective-permute-start | bytes 786440 | tf_op jit(solution)/shard_map/ppermute | solution.py:613
  74.2 20.8 %collective-permute-start.17 = (f32[2,64,256]{2,1,0:T(8,128)S(1)}, f32[2,64,256]{2,1,0:T(8,128)S(1)}, u32[]{:S(2)}, u32[]{:S(2)}) collective-permute-start(f32[2,64,256]{2,1,0:T(8,128)S(1)} %get-tuple-element.53.v_own), channel_id=1, source_target_pairs={{0,1},{1,0},{2,3},{3,2},{4,5},{5,4},{6,7},{7,6},{8,9},{9,8},{10,11... | collective-permute-start | bytes 393224 | tf_op jit(solution)/shard_map/ppermute | solution.py:617
  91.7 8.4 %collective-permute-start.18 = (f32[2,64,256]{2,1,0:T(8,128)S(1)}, f32[2,64,256]{2,1,0:T(8,128)S(1)}, u32[]{:S(2)}, u32[]{:S(2)}) collective-permute-start(f32[2,64,256]{2,1,0:T(8,128)S(1)} %get-tuple-element.54), channel_id=1, source_target_pairs={{0,3},{1,2},{2,1},{3,0},{4,7},{5,6},{6,5},{7,4},{8,11},{9,10},{10,... | collective-permute-start | bytes 393224 | tf_op jit(solution)/shard_map/ppermute | solution.py:621
  91.7 9.3 %collective-permute-start.16 = (f32[2,64,256]{2,1,0:T(8,128)S(1)}, f32[2,64,256]{2,1,0:T(8,128)S(1)}, u32[]{:S(2)}, u32[]{:S(2)}) collective-permute-start(f32[2,64,256]{2,1,0:T(8,128)S(1)} %get-tuple-element.54), channel_id=1, source_target_pairs={{0,2},{2,0},{1,3},{3,1},{4,6},{6,4},{5,7},{7,5},{8,10},{10,8},{9,1... | collective-permute-start | bytes 393224 | tf_op jit(solution)/shard_map/ppermute | solution.py:613
  95.0 12.2 %collective-permute-start.24 = (f32[256,128]{1,0:T(8,128)S(1)}, f32[256,128]{1,0:T(8,128)S(1)}, u32[]{:S(2)}, u32[]{:S(2)}) collective-permute-start(f32[256,128]{1,0:T(8,128)S(1)} %get-tuple-element.61), channel_id=1, source_target_pairs={{0,2},{2,0},{1,3},{3,1},{4,6},{6,4},{5,7},{7,5},{8,10},{10,8},{9,1... | collective-permute-start | bytes 393224 | tf_op jit(solution)/shard_map/ppermute | solution.py:613
  101.0 5.5 %collective-permute-start.27 = (f32[64,128]{1,0:T(8,128)S(1)}, f32[64,128]{1,0:T(8,128)S(1)}, u32[]{:S(2)}, u32[]{:S(2)}) collective-permute-start(f32[64,128]{1,0:T(8,128)S(1)} %get-tuple-element.63), channel_id=1, source_target_pairs={{0,3},{1,2},{2,1},{3,0},{4,7},{5,6},{6,5},{7,4},{8,11},{9,10},{10,... | collective-permute-start | bytes 98312 | tf_op jit(solution)/shard_map/ppermute | solution.py:621
  (17 other events, 132.4 us)
